TPU v7x, 256 devices: a whole 4x4x8 slice. The times are simulated.
256 devices in a mesh: tile: 64 (over z, x, y_hi), chan: 4 (over y_lo, core).
Axes of the slice: x: 4, y: 4 (y_hi: 2, y_lo: 2; y = y_hi * 2 + y_lo), z: 8, core: 2. Of those that a mesh axis runs over, the one named last changes fastest.
Arguments:
- features: bfloat16 [512, 64, 4096], P('tile', 'chan'), may hold values from -6 to 6
- conv_weight: bfloat16 [64, 576], P('chan'), may hold values from -0.25 to 0.25
- conv_bias: float32 [64], P('chan'), may hold values from -3 to 3
- down_weight: bfloat16 [64, 256], P(None, 'chan'), may hold values from -0.375 to 0.375
- cotangent: bfloat16 [128, 64, 4096], P('tile', 'chan'), may hold values from -0.0078125 to 0.0078125
- edge_links: int32 [512, 4], P('tile'), may hold values from 0 to 511, as said below
- edge_turns: int32 [512, 4], P('tile'), may hold values from 0 to 3
- corner_links: int32 [512, 4], P('tile'), may hold values from -1 to 511, as said below
- corner_turns: int32 [512, 4], P('tile'), may hold values from 0 to 3
- child_slot: int32 [512], P('tile'), may hold values from 0 to 511, as said below
Outputs:
- coarse: bfloat16 [128, 64, 4096], P('tile', 'chan')
- grad_conv: float32 [64, 576], P('chan')
- grad_bias: float32 [64], P('chan')
- grad_down: float32 [64, 256], P(None, 'chan')
Inputs may be any that keep to these rules, and one draw needn't show every extreme that they name: `edge_links`: edge k: 0 north, 1 west, 2 south, 3 east. `corner_links`: corner k: 0 north-west, 1 south-west, 2 south-east, 3 north-east; -1 where no tile touches that corner. `child_slot`: a permutation of 0 to 511; coarse tile k lies on index k // 2 of tile; of the 8 fine tiles of one index of tile, at most 1 have their coarse tiles on any one index of tile, and that many do for some pair.
All inputs are finite; a program needn't handle non-finite values.
Results may differ from a plain program's by a relative error of at most 0.0055.
Values may be sent and summed in bfloat16 or wider, within the bound.
No kernel may reach another device: no remote copies, remote signals or barrier semaphores. Data moves between devices by JAX's collectives and lax.ppermute only.
A program may use at most 64 MiB of HBM per device.

v0:
```python
import jax
import jax.numpy as jnp
from jax import lax
from jax.sharding import PartitionSpec as P

C = 64
S = 64


def edge_parts(tile_grid):
    side_len = tile_grid.shape[-1]
    edge_row = side_len - 1
    rim_strips = jnp.stack(
        [
            tile_grid[:, :, 0, ::-1],
            tile_grid[:, :, :, 0],
            tile_grid[:, :, edge_row, :],
            tile_grid[:, :, ::-1, edge_row],
        ],
        axis=1,
    )
    corners = jnp.stack(
        [
            tile_grid[:, :, 0, 0],
            tile_grid[:, :, edge_row, 0],
            tile_grid[:, :, edge_row, edge_row],
            tile_grid[:, :, 0, edge_row],
        ],
        axis=1,
    )
    return (rim_strips, corners)


def pick_halos(
    piece_rims,
    piece_corners,
    start,
    edge_links,
    edge_turns,
    corner_links,
    corner_turns,
    strips,
    corner_vals,
):
    piece_len = piece_rims.shape[0]
    side_index = jnp.arange(4, dtype=jnp.int32)[None, :]
    chosen = (side_index + 2 + edge_turns) % 4
    relative = edge_links - start
    inside = (relative >= 0) & (relative < piece_len)
    picked = piece_rims[jnp.clip(relative, 0, piece_len - 1), chosen]
    strips = jnp.where(inside[:, :, None, None], picked, strips)
    corner_pick = (side_index + 2 + corner_turns) % 4
    corner_rel = corner_links - start
    corner_in = (corner_links >= 0) & (corner_rel >= 0) & (corner_rel < piece_len)
    corner_got = piece_corners[jnp.clip(corner_rel, 0, piece_len - 1), corner_pick]
    corner_vals = jnp.where(corner_in[:, :, None], corner_got, corner_vals)
    return (strips, corner_vals)


def assemble(tile_grid, strips, corner_vals):
    north_row = strips[:, 0]
    west_col = strips[:, 1, :, ::-1]
    south_row = strips[:, 2, :, ::-1]
    east_col = strips[:, 3]
    upper_row = jnp.concatenate(
        [corner_vals[:, 0, :, None], north_row, corner_vals[:, 3, :, None]], axis=-1
    )
    bottom = jnp.concatenate(
        [corner_vals[:, 1, :, None], south_row, corner_vals[:, 2, :, None]], axis=-1
    )
    middle = jnp.concatenate([west_col[:, :, :, None], tile_grid, east_col[:, :, :, None]], axis=-1)
    return jnp.concatenate([upper_row[:, :, None, :], middle, bottom[:, :, None, :]], axis=2)


def to_patches(tile_field):
    tile_count, channel_count, side_len = (
        tile_field.shape[0],
        tile_field.shape[1],
        tile_field.shape[2],
    )
    half_side = side_len // 2
    blocks = tile_field.reshape(tile_count, channel_count, half_side, 2, half_side, 2).transpose(
        0, 1, 3, 5, 2, 4
    )
    return blocks.reshape(tile_count, channel_count * 4, half_side * half_side)


def from_patches(patches, channel_count, side_len):
    tile_count = patches.shape[0]
    half_side = side_len // 2
    blocks = patches.reshape(tile_count, channel_count, 2, 2, half_side, half_side).transpose(
        0, 1, 4, 2, 5, 3
    )
    return blocks.reshape(tile_count, channel_count, side_len, side_len)


def join_quarters(by_slot, side_len):
    half_side = side_len // 2
    slot_count, channel_count = (by_slot.shape[0], by_slot.shape[1])
    blocks = by_slot.reshape(slot_count // 4, 2, 2, channel_count, half_side, half_side).transpose(
        0, 3, 1, 4, 2, 5
    )
    return blocks.reshape(slot_count // 4, channel_count, side_len * side_len)


def split_coarse(coarse_field, side_len):
    half_side = side_len // 2
    tile_count, channel_count = (coarse_field.shape[0], coarse_field.shape[1])
    blocks = coarse_field.reshape(tile_count, channel_count, 2, half_side, 2, half_side).transpose(
        0, 2, 4, 1, 3, 5
    )
    return blocks.reshape(tile_count * 4, channel_count, half_side * half_side)


def silu_slope(pre_act):
    squashed = jax.nn.sigmoid(pre_act)
    return squashed * (1.0 + pre_act * (1.0 - squashed))


def on_device(
    features,
    conv_weight,
    conv_bias,
    down_weight,
    cotangent,
    edge_links,
    edge_turns,
    corner_links,
    corner_turns,
    child_slot,
):
    tile_count = features.shape[0]
    local_chans = features.shape[1]
    tile_grid = features.reshape(tile_count, local_chans, S, S)
    rim_strips, corners = edge_parts(tile_grid)
    empty_strips = jnp.zeros((tile_count, 4, local_chans, S), jnp.bfloat16)
    empty_corners = jnp.zeros((tile_count, 4, local_chans), jnp.bfloat16)
    every_rim, every_corner = (
        lax.all_gather(rim_strips, "tile", axis=0, tiled=True),
        lax.all_gather(corners, "tile", axis=0, tiled=True),
    )
    strips, corner_vals = pick_halos(
        every_rim,
        every_corner,
        0,
        edge_links,
        edge_turns,
        corner_links,
        corner_turns,
        empty_strips,
        empty_corners,
    )
    padded = assemble(tile_grid, strips, corner_vals)
    flat_pad = padded.reshape(tile_count, local_chans, (S + 2) * (S + 2))
    regrouped = lax.all_to_all(flat_pad, "chan", split_axis=0, concat_axis=1, tiled=True)
    group_tiles = regrouped.shape[0]
    whole_pad = regrouped.reshape(group_tiles, C, S + 2, S + 2)
    conv_all, bias_all, down_all = (
        lax.all_gather(conv_weight.astype(jnp.float32), "chan", axis=0, tiled=True),
        lax.all_gather(conv_bias, "chan", axis=0, tiled=True),
        lax.all_gather(down_weight.astype(jnp.float32), "chan", axis=1, tiled=True),
    )
    conv_all = conv_all.astype(jnp.bfloat16)
    down_all = down_all.astype(jnp.bfloat16)
    filters = conv_all.reshape(C, C, 3, 3)
    pre_act = lax.conv_general_dilated(
        whole_pad,
        filters,
        (1, 1),
        "VALID",
        dimension_numbers=("NCHW", "OIHW", "NCHW"),
        preferred_element_type=jnp.float32,
    )
    pre_act = pre_act + bias_all[None, :, None, None]
    hidden = jax.nn.silu(pre_act).astype(jnp.bfloat16)
    patches = to_patches(hidden)
    quarter_whole = jnp.einsum(
        "ok,tkq->toq", down_all, patches, preferred_element_type=jnp.float32
    ).astype(jnp.bfloat16)
    quarter = lax.all_to_all(quarter_whole, "chan", split_axis=1, concat_axis=0, tiled=True)
    peer_count = lax.axis_size("tile")
    capacity = max(1, tile_count // peer_count)
    owner_index = child_slot // tile_count
    local_slot = child_slot % tile_count
    positions = jnp.arange(tile_count, dtype=jnp.int32)
    same_owner = owner_index[:, None] == owner_index[None, :]
    earlier = positions[None, :] < positions[:, None]
    rank_within = jnp.sum(jnp.where(same_owner & earlier, 1, 0), axis=1).astype(jnp.int32)
    target = owner_index * capacity + rank_within
    rows_out = jnp.arange(peer_count * capacity, dtype=jnp.int32)
    send_mask = rows_out[:, None] == target[None, :]
    send_onehot = send_mask.astype(jnp.bfloat16)
    outgoing = jnp.einsum(
        "rt,toq->roq", send_onehot, quarter, preferred_element_type=jnp.float32
    ).astype(jnp.bfloat16)
    labels = jnp.sum(jnp.where(send_mask, local_slot[None, :] + 1, 0), axis=1)
    arrived, arrived_labels = (
        lax.all_to_all(outgoing, "tile", split_axis=0, concat_axis=0, tiled=True),
        lax.all_to_all(labels, "tile", split_axis=0, concat_axis=0, tiled=True),
    )
    place_mask = (arrived_labels - 1)[None, :] == positions[:, None]
    place_onehot = place_mask.astype(jnp.bfloat16)
    by_slot = jnp.einsum(
        "mr,roq->moq", place_onehot, arrived, preferred_element_type=jnp.float32
    ).astype(jnp.bfloat16)
    coarse = join_quarters(by_slot, S)
    cot_slots = split_coarse(cotangent, S)
    returning = jnp.einsum(
        "mr,moq->roq", place_onehot, cot_slots, preferred_element_type=jnp.float32
    ).astype(jnp.bfloat16)
    returned = lax.all_to_all(returning, "tile", split_axis=0, concat_axis=0, tiled=True)
    cot_tile = jnp.einsum(
        "rt,roq->toq", send_onehot, returned, preferred_element_type=jnp.float32
    ).astype(jnp.bfloat16)
    cot_group = lax.all_to_all(cot_tile, "chan", split_axis=0, concat_axis=1, tiled=True)
    grad_down = jnp.einsum("toq,tkq->ok", cot_group, patches, preferred_element_type=jnp.float32)
    grad_patches = jnp.einsum(
        "ok,toq->tkq", down_all, cot_group, preferred_element_type=jnp.float32
    )
    grad_hidden = from_patches(grad_patches, C, S)
    grad_pre = (grad_hidden * silu_slope(pre_act)).astype(jnp.bfloat16)
    grad_bias = jnp.sum(grad_pre, axis=(0, 2, 3), dtype=jnp.float32)
    products = []
    for row_shift in range(3):
        for col_shift in range(3):
            window = whole_pad[:, :, row_shift : row_shift + S, col_shift : col_shift + S]
            products.append(
                jnp.einsum("toyx,tiyx->oi", grad_pre, window, preferred_element_type=jnp.float32)
            )
    grad_conv = jnp.stack(products, axis=-1).reshape(C, C * 9)
    grad_conv, grad_bias, grad_down = lax.psum((grad_conv, grad_bias, grad_down), ("tile", "chan"))
    first_row = lax.axis_index("chan") * local_chans
    grad_conv = lax.dynamic_slice_in_dim(grad_conv, first_row, local_chans, 0)
    grad_bias = lax.dynamic_slice_in_dim(grad_bias, first_row, local_chans, 0)
    grad_down = lax.dynamic_slice_in_dim(grad_down, first_row * 4, local_chans * 4, 1)
    return (coarse, grad_conv, grad_bias, grad_down)


def solution(mesh):
    in_specs = (
        P("tile", "chan", None),
        P("chan", None),
        P("chan"),
        P(None, "chan"),
        P("tile", "chan", None),
        P("tile", None),
        P("tile", None),
        P("tile", None),
        P("tile", None),
        P("tile"),
    )
    out_specs = (P("tile", "chan", None), P("chan", None), P("chan"), P(None, "chan"))
    return jax.shard_map(
        on_device, mesh=mesh, in_specs=in_specs, out_specs=out_specs, check_vma=False
    )
```

profile of v0, /device:TPU:1, one launch (start us, length us, event | category | flops | bytes accessed | tf_op | source)
XLA Modules:
  0.0 748.6 jit_solution(15913105121603829944)
XLA Ops:
  13.9 5.9 rev.13
  24.4 15.1 %all-to-all-start = ((s32[64,1,1]{2,1,0:T(1,128)}), s32[64,1,1]{2,1,0:T(1,128)S(1)}, u32[]{:S(2)}, u32[]{:S(2)}) async-start(s32[64,1,1]{2,1,0:T(1,128)} %copy.493), calls=%async_computation | async-start | bytes 65536 | tf_op jit(solution)/shard_map/all_to_all | solution.py:199
  43.9 6.4 all-to-all-done
  54.7 6.6 all-to-all-start.4
  63.3 195.7 %all_gather.15 = bf16[512,4,16]{2,1,0:T(4,128)(2,1)S(1)} all-gather(bf16[8,4,16]{2,1,0:T(4,128)(2,1)S(1)} %copy.494), channel_id=1, replica_groups=mesh['tile'=64,'chan'=4] {'tile'}, dimensions={0}, use_global_device_ids=true | all-gather | bytes 66560 | tf_op jit(solution)/shard_map/all_gather | solution.py:140
  265.0 33.2 %all-to-all-start.5 = ((bf16[8,16,1024]{2,1,0:T(8,128)(2,1)}), bf16[8,16,1024]{2,1,0:T(8,128)(2,1)S(1)}, u32[]{:S(2)}, u32[]{:S(2)}) async-start(bf16[8,16,1024]{2,1,0:T(8,128)(2,1)} %copy.529), calls=%async_computation.5 | async-start | bytes 524288 | tf_op jit(solution)/shard_map/all_to_all | solution.py:215
  306.8 6.7 pad_maximum_fusion
  313.5 4.3 reshape.71
  321.7 16.4 %all_gather.19 = bf16[64,256]{0,1:T(8,128)(2,1)S(1)} all-gather(bf16[64,64]{0,1:T(8,128)(2,1)S(1)} %copy.516), channel_id=1, replica_groups=mesh['tile'=64,'chan'=4] {'chan'}, dimensions={1}, use_global_device_ids=true | all-gather | bytes 40960 | tf_op jit(solution)/shard_map/all_gather | solution.py:161
  338.2 5.3 all_gather.17
  345.9 5.2 all-reduce
  355.6 4.8 reshape.80
  360.3 9.4 %copy.532 = f32[2,64,32,2,32,2]{1,5,4,3,2,0:T(2,128)} copy(f32[2,64,32,2,32,2]{4,2,5,3,1,0:T(8,128)} %bitcast.187) | data formatting | bytes 4194304 | tf_op jit(solution)/shard_map/transpose | solution.py:91
  374.5 4.5 copy.585
  383.8 7.7 %copy.510 = bf16[64,66,2,8,11]{0,3,2,4,1:T(8,128)(2,1)} copy(bf16[64,66,2,8,11]{1,0,4,3,2:T(8,128)(2,1)} %fusion.5) | data formatting | bytes 2973696 | tf_op jit(solution)/shard_map/conv_general_dilated | solution.py:166
  391.6 6.1 add_multiply_fusion
  405.2 9.5 %copy.515 = bf16[2,64,2,2,32,32]{5,4,3,2,1,0:T(8,128)(2,1)} copy(bf16[2,64,2,2,32,32]{1,3,5,2,4,0:T(2,128)(2,1)} %bitcast.193) | data formatting | bytes 2097152 | tf_op jit(solution)/shard_map/transpose | solution.py:82
  414.7 6.2 reshape.75
  422.2 5.2 all-to-all-start.2
  427.4 7.6 %convert_reduce_fusion = (f32[64]{0:T(128)S(1)}, bf16[2,64,64,64]{1,3,2,0:T(8,128)(2,1)}) fusion(f32[2,64,64,64]{1,3,2,0:T(8,128)} %bitcast.189, f32[64,2,64,64]{3,0,2,1:T(8,128)} %slice.125), kind=kLoop, calls=%fused_computation.11 | loop fusion | flops 2097088 | bytes 5243136 | tf_op jit(solution)/shard_map/reduce_sum | solution.py:222
  439.3 8.5 %all-to-all-start.3 = ((bf16[64,16,1024]{2,1,0:T(8,128)(2,1)}), bf16[64,16,1024]{2,1,0:T(8,128)(2,1)}, u32[]{:S(2)}, u32[]{:S(2)}) async-start(bf16[64,16,1024]{2,1,0:T(8,128)(2,1)} %copy.522), calls=%async_computation.3 | async-start | bytes 4194304 | tf_op jit(solution)/shard_map/all_to_all | solution.py:198
  447.9 7.2 fusion.121
  481.1 79.2 %psum.22 = f32[64]{0:T(128)S(1)} all-reduce(f32[64]{0:T(128)S(1)} %get-tuple-element.46), channel_id=1, replica_groups=mesh['tile'=64,'chan'=4] {'tile','chan'}, use_global_device_ids=true, to_apply=%region_4.5 | all-reduce | flops 64 | bytes 512 | tf_op jit(solution)/shard_map/psum | solution.py:231
  560.9 169.8 %all-reduce.4.cloned.1.call-done = (f32[64,576]{0,1:T(8,128)}, f32[64,256]{1,0:T(8,128)}) async-done(((f32[64,576]{0,1:T(8,128)}, f32[64,256]{1,0:T(8,128)}), (f32[64,576]{0,1:T(8,128)}, f32[64,256]{1,0:T(8,128)})) %all-reduce.4.cloned.1.call-update) | async-done | bytes 213008 | tf_op jit(solution)/shard_map/psum | solution.py:231
  (144 shorter events, 106.7 us)
Async XLA Ops:
  7.2 291.1 %all-gather.2.cloned.1.call-start = ((), (), s32[]{:S(2)}) async-start(), calls=%async_computation.6 | async-start | bytes 8519680 | tf_op jit(solution)/shard_map/all_gather | solution.py:139
  19.8 3.6 copy-start.14
  19.8 19.7 %copy-start.6 = (bf16[2,16,4096]{2,1,0:T(8,128)(2,1)S(1)}, bf16[2,16,4096]{2,1,0:T(8,128)(2,1)}, u32[]{:S(2)}) copy-start(bf16[2,16,4096]{2,1,0:T(8,128)(2,1)} %param.14) | copy-start | bytes 786436
  24.4 25.9 %all-to-all-start = ((s32[64,1,1]{2,1,0:T(1,128)}), s32[64,1,1]{2,1,0:T(1,128)S(1)}, u32[]{:S(2)}, u32[]{:S(2)}) async-start(s32[64,1,1]{2,1,0:T(1,128)} %copy.493), calls=%async_computation | async-start | bytes 65536 | tf_op jit(solution)/shard_map/all_to_all | solution.py:199
  54.7 6.6 copy-start.10
  54.7 6.7 copy-start.11
  54.7 6.7 copy-start.12
  54.7 6.7 copy-start.13
  54.7 205.6 %all-to-all-start.4 = ((bf16[64,16,1024]{2,1,0:T(8,128)(2,1)}), bf16[64,16,1024]{2,1,0:T(8,128)(2,1)}, u32[]{:S(2)}, u32[]{:S(2)}) async-start(bf16[64,16,1024]{2,1,0:T(8,128)(2,1)} %copy.527), calls=%async_computation.4 | async-start | bytes 4194304 | tf_op jit(solution)/shard_map/all_to_all | solution.py:211
  265.0 52.9 %all-to-all-start.5 = ((bf16[8,16,1024]{2,1,0:T(8,128)(2,1)}), bf16[8,16,1024]{2,1,0:T(8,128)(2,1)S(1)}, u32[]{:S(2)}, u32[]{:S(2)}) async-start(bf16[8,16,1024]{2,1,0:T(8,128)(2,1)} %copy.529), calls=%async_computation.5 | async-start | bytes 524288 | tf_op jit(solution)/shard_map/all_to_all | solution.py:215
  313.5 8.1 %copy-start.9 = (bf16[64,64]{1,0:T(8,128)(2,1)S(1)}, bf16[64,64]{1,0:T(8,128)(2,1)}, u32[]{:S(2)}) copy-start(bf16[64,64]{1,0:T(8,128)(2,1)} %param.13) | copy-start | bytes 24580
  317.9 20.3 %copy-start.8 = (bf16[16,576]{1,0:T(8,128)(2,1)S(1)}, bf16[16,576]{1,0:T(8,128)(2,1)}, u32[]{:S(2)}) copy-start(bf16[16,576]{1,0:T(8,128)(2,1)} %param.11) | copy-start | bytes 55300
  317.9 26.6 %copy-start.16 = (u32[256]{0:T(256)S(1)}, u32[256]{0:T(256)}, u32[]{:S(2)}) copy-start(u32[256]{0:T(256)} %constant.119) | copy-start | bytes 3076
  317.9 27.8 %copy-start.15 = (f32[16]{0:T(128)S(1)}, f32[16]{0:T(128)}, u32[]{:S(2)}) copy-start(f32[16]{0:T(128)} %param.12) | copy-start | bytes 196
  317.9 51.8 %all-to-all-start.1 = ((bf16[8,16,4356]{2,1,0:T(8,128)(2,1)}), bf16[8,16,4356]{2,1,0:T(8,128)(2,1)S(1)}, u32[]{:S(2)}, u32[]{:S(2)}) async-start(bf16[8,16,4356]{2,1,0:T(8,128)(2,1)} %reshape.71), calls=%async_computation.1 | async-start | bytes 2293760 | tf_op jit(solution)/shard_map/all_to_all | solution.py:155
  383.8 7.8 %copy-start.7 = (bf16[64,64,3,3]{0,3,2,1:T(4,128)(2,1)S(1)}, bf16[64,64,3,3]{0,3,2,1:T(4,128)(2,1)}, u32[]{:S(2)}) copy-start(bf16[64,64,3,3]{0,3,2,1:T(4,128)(2,1)} %reshape.73) | copy-start | bytes 221188
  383.8 7.8 %copy-start.17 = (pred[16,9]{0,1:T(8,128)(4,1)S(1)}, pred[16,9]{0,1:T(8,128)(4,1)}, u32[]{:S(2)}) copy-start(pred[16,9]{0,1:T(8,128)(4,1)} %constant.90) | copy-start | bytes 436
  422.2 12.8 %all-to-all-start.2 = ((bf16[2,64,1024]{2,0,1:T(2,128)(2,1)}), bf16[2,64,1024]{2,0,1:T(2,128)(2,1)}, u32[]{:S(2)}, u32[]{:S(2)}) async-start(bf16[2,64,1024]{2,0,1:T(2,128)(2,1)} %copy.518), calls=%async_computation.2 | async-start | bytes 524288 | tf_op jit(solution)/shard_map/all_to_all | solution.py:180
  439.3 294.7 %all-to-all-start.3 = ((bf16[64,16,1024]{2,1,0:T(8,128)(2,1)}), bf16[64,16,1024]{2,1,0:T(8,128)(2,1)}, u32[]{:S(2)}, u32[]{:S(2)}) async-start(bf16[64,16,1024]{2,1,0:T(8,128)(2,1)} %copy.522), calls=%async_computation.3 | async-start | bytes 4194304 | tf_op jit(solution)/shard_map/all_to_all | solution.py:198
  447.9 282.8 %all-reduce.4.cloned.1.call-start = ((), (), s32[]{:S(2)}) async-start(), calls=%async_computation.7 | async-start | bytes 720896 | tf_op jit(solution)/shard_map/psum | solution.py:231
  455.1 4.3 copy-start.4
  455.1 4.3 copy-start.5
  459.5 2.4 copy-start.3
  476.5 3.5 copy-start.1
  (2 other events, 3.1 us)
Sparse Core Ops, SparseCore 0:
  23.5 160.1 all-gather.1
  481.2 249.4 all-reduce.3
where the time goes:
time: 764 us; the launch traced here: 749 us
  blocking collectives  302 us (40%)
  waiting for transfers between devices  176 us (23%)
  local copies, waits for them, and re-layouts  119 us (16%)
  starting transfers between devices  72.5 us (9%)
  matrix products  42.3 us (6%)
  other arithmetic  21.5 us (3%)
  between operations  15.5 us (2%)
    all_gather x1, blocking collectives, on_device(): lax.all_gather(corners, 'tile', axis=0, tiled=True)  196 us
    psum x1, waiting for transfers between devices, on_device(): lax.psum((grad_conv, grad_bias, grad_down), ('tile', 'chan'))  170 us
    psum x1, blocking collectives, on_device(): lax.psum((grad_conv, grad_bias, grad_down), ('tile', 'chan'))  79.2 us
    all_to_all x1, starting transfers between devices, on_device(): lax.all_to_all(cot_tile, 'chan', split_axis=0, concat_axis=1, tiled=True)  33.2 us
    dot_general x9, matrix products, on_device(): jnp.einsum('toyx,tiyx->oi', grad_pre, window, preferred_element_type=jnp....  23.7 us
    all_gather x1, blocking collectives, on_device(): lax.all_gather(down_weight.astype(jnp.float32), 'chan', axis=1, tiled=True)  16.4 us
  transfers between devices with their start and end apart: 8, of which 2 were waited for; matrix products, arithmetic and copies ran while one was open for 14% of the time, Pallas kernels for 0%

commit v1 on v0

v1 whole, which is shorter than its diff:
```python
import jax
import jax.numpy as jnp
from jax import lax
from jax.experimental import pallas as pl
from jax.experimental.pallas import tpu as pltpu
from jax.sharding import PartitionSpec as P

BF = jnp.bfloat16
F32 = jnp.float32
NODES = 64
MSG = (NODES * 8, 384)


def iota(shape, dim):
    return lax.broadcasted_iota(jnp.int32, shape, dim)


def ones_where(mask):
    return jnp.where(mask, 1.0, 0.0).astype(BF)


def keep(mask, x):
    return jnp.where(mask, x, 0.0).astype(BF)


def mm(a, b):
    return jnp.dot(a, b, preferred_element_type=F32)


def mm_nt(a, b):
    return lax.dot_general(a, b, (((1,), (1,)), ((), ())), preferred_element_type=F32)


def halves(x):
    high = x.astype(BF)
    return high, (x - high.astype(F32)).astype(BF)


def call(body, out_shape, grid, in_specs, out_specs, scratch=(), flops=0, moved=0):
    return pl.pallas_call(
        body,
        out_shape=out_shape,
        grid=grid,
        in_specs=in_specs,
        out_specs=out_specs,
        scratch_shapes=scratch,
        compiler_params=pltpu.CompilerParams(vmem_limit_bytes=48 << 20),
        cost_estimate=pl.CostEstimate(flops=flops, bytes_accessed=moved, transcendentals=0),
    )


def whole(shape):
    return pl.BlockSpec(shape, lambda i: (0,) * len(shape))


def send_body(feat_ref, cot_ref, small_ref, out_ref):
    step = pl.program_id(0)
    cot = cot_ref[...]
    stack = jnp.concatenate([cot[:, q * 256 : q * 256 + 256] for q in range(16)], axis=0)
    row = iota((128, 512), 0) + step * 128
    col = iota((128, 512), 1)
    k, g, a, qr, hf = row >> 5, (row >> 3) & 3, (row >> 2) & 1, (row >> 1) & 1, row & 1
    source = (qr << 8) | (g << 6) | (hf << 5) | (a << 4) | k
    out_ref[:, 0:256] = mm(ones_where(col == source), stack).astype(BF)

    first = feat_ref[:, 0:128]
    last = feat_ref[:, 3968:4096]
    p = iota((16, 128), 0) + step * 16
    lane = iota((16, 128), 1)
    rim_n = mm_nt(ones_where(lane == 63 - p), first)
    rim_s = mm_nt(ones_where(lane == 64 + p), last)
    pc = iota((32, 4096), 0)
    px = iota((32, 4096), 1)
    pos = (pc & 15) + step * 16
    want = jnp.where(pc < 16, pos * 64, (63 - pos) * 64 + 63)
    rim_we = mm_nt(ones_where(px == want), feat_ref[...])
    cr = iota((16, 128), 0)
    corners = mm_nt(
        ones_where(((cr == 0) & (lane == 0)) | ((cr == 3) & (lane == 63))), first
    ) + mm_nt(ones_where(((cr == 1) & (lane == 64)) | ((cr == 2) & (lane == 127))), last)
    tc = iota((128, 128), 0)
    to = iota((128, 128), 1)
    by_chan = jnp.zeros((16, 128), F32)
    for c in range(4):
        spread = jnp.broadcast_to(corners[c : c + 1, :], (16, 128))
        by_chan = by_chan + mm(keep((lane & 15) == cr, spread), ones_where(to == (tc >> 4) * 4 + c))
    parts = [rim_n, rim_we[0:16], rim_s, rim_we[16:32], by_chan]
    stack = jnp.concatenate([x.astype(BF) for x in parts] + [small_ref[...]], axis=0)
    r, node = tc & 7, tc >> 3
    source = jnp.where(r < 5, r * 16 + node, jnp.where(r == 5, 80, jnp.where(r == 6, 81 + step, -1)))
    out_ref[:, 256:384] = mm(ones_where(to == source), stack).astype(BF)


def pick_body(msg_ref, out_ref, slot_ref):
    step = pl.program_id(0)
    cot = msg_ref[:, 0:256]
    misc = msg_ref[:, 256:384]
    row = iota((128, 512), 0) + step * 128
    col = iota((128, 512), 1)
    lane = iota((128, 128), 1)
    sub = iota((128, 128), 0)
    base = (row >> 3) << 3
    both = mm(ones_where((col == base + 5) | (col == base + 6)), misc)
    fields = mm(keep((lane & 7) == (sub & 7), both), ones_where((sub >> 3) == lane))
    flip = fields.T
    slot_ref[...] = jnp.broadcast_to(flip[12:13, :] * 8.0 + flip[13:14, :], (8, 128))
    num = fields.astype(jnp.int32)

    def field(f):
        return num[:, f : f + 1]

    slot_row = field(12) * 8 + ((field(13) >> 1) << 1)
    lane2 = iota((128, 256), 1)
    fold_r = iota((256, 128), 0)
    fold_c = iota((256, 128), 1)
    fold = ones_where(((fold_r >> 6) == (fold_c >> 5)) & ((fold_r & 31) == (fold_c & 31)))
    mine = ((lane2 >> 5) & 1) == (field(13) & 1)
    for hf in range(2):
        got = mm(ones_where(col == slot_row + hf), cot)
        out_ref[:, hf * 128 : hf * 128 + 128] = mm(keep(mine, got), fold).astype(BF)
    total = jnp.zeros((128, 128), F32)
    for k in range(4):
        got = mm(ones_where(col == field(k) * 8 + field(4 + k)), misc)
        place = ones_where(lane == k * 16 + (sub & 15))
        total = total + mm(keep((lane >> 4) == field(8 + k), got), place)
    got = mm(ones_where(col == field(14) * 8 + 4), misc)
    total = total + mm(keep(lane == field(15), got), ones_where(lane == 64))
    out_ref[:, 256:384] = total.astype(BF)


def regroup_body(msg_ref, out_ref):
    step = pl.program_id(0)
    row = iota((128, 512), 0)
    col = iota((128, 512), 1)
    pair, g, k, p = row >> 6, (row >> 4) & 3, row & 15, row & 63
    tile = (step << 1) | pair
    out_ref[:, 0:256] = mm(ones_where(col == ((k << 5) | (g << 3) | tile)), msg_ref[:, 0:256]).astype(BF)
    out_ref[:, 256:384] = mm(ones_where(col == ((p << 3) | tile)), msg_ref[:, 256:384]).astype(BF)


def level_body(feat_ref, msg_ref, w_ref, bias_ref, down_ref, down_t_ref, out_ref, win_ref, gc_ref, gd_ref, gb_ref):
    step = pl.program_id(0)
    x = jnp.concatenate([feat_ref[c, 0] for c in range(4)], axis=0)
    stack = jnp.concatenate([x[:, q * 512 : q * 512 + 512] for q in range(8)], axis=0)
    l_in = iota((512, 512), 0)
    l_out = iota((512, 512), 1)
    to = (
        (((l_in >> 6) & 1) << 8)
        | ((l_in & 1) << 7)
        | ((l_in >> 7) << 5)
        | ((l_in >> 1) & 31)
    )
    split = mm(stack, ones_where(l_out == to))

    def plane(a, b):
        s = (a * 2 + b) * 128
        return jnp.concatenate([split[q * 64 : q * 64 + 64, s : s + 128] for q in range(8)], axis=1)

    rim = [msg_ref[c, 0, :, 256:384].astype(F32) for c in range(4)]
    flip = [r.T.astype(BF) for r in rim]

    def strip(k):
        return jnp.concatenate([f[k * 16 : k * 16 + 16, :] for f in flip], axis=0)

    def corner(k):
        return jnp.concatenate([r[k * 16 : k * 16 + 16, 64:65] for r in rim], axis=0)

    lane = iota((64, 1024), 1)
    v = lane & 31
    pos = iota((64, 1024), 0)
    cols = []
    for a in range(2):
        y = ((lane >> 5) << 1) + a
        side = mm(strip(1), ones_where((v == 0) & (y == 63 - pos))) + mm(
            strip(3), ones_where((v == 31) & (y == pos))
        )
        even, odd = plane(a, 0), plane(a, 1)
        cols.append(
            [
                jnp.where(v == 0, side, pltpu.roll(odd, 1, axis=1)),
                even,
                odd,
                jnp.where(v == 31, side, pltpu.roll(even, 1023, axis=1)),
            ]
        )
    lane_e = iota((64, 512), 1)
    pos_e = iota((64, 512), 0)
    inner = lane_e & 127
    at = ((inner & 31) << 1) + (lane_e >> 7)
    ends = mm(strip(0), ones_where((inner < 32) & (pos_e == at - 1))) + mm(
        strip(2), ones_where((inner >= 96) & (pos_e == 64 - at))
    )
    for spot, k in ((0, 0), (96, 1), (384 + 31, 3), (384 + 127, 2)):
        ends = jnp.where(lane_e == spot, corner(k), ends)
    blank = jnp.zeros((64, 896), F32)
    for cx in range(4):
        end = ends[:, cx * 128 : cx * 128 + 128]
        top = jnp.where(lane < 32, jnp.concatenate([end, blank], axis=1), pltpu.roll(cols[1][cx], 32, axis=1))
        low = jnp.where(lane >= 992, jnp.concatenate([blank, end], axis=1), pltpu.roll(cols[0][cx], 992, axis=1))
        for ry, w in enumerate((top, cols[0][cx], cols[1][cx], low)):
            at_row = (ry * 4 + cx) * 64
            win_ref[at_row : at_row + 64, :] = w.astype(BF)

    pre = mm(w_ref[...], win_ref[...]) + bias_ref[...]
    sig = 1.0 / (1.0 + jnp.exp(-pre))
    hidden = (pre * sig).astype(BF)
    quarter = mm(down_ref[...], hidden).astype(BF)
    for c in range(4):
        out_ref[c, pl.ds(pl.multiple_of(step * 16, 16), 16), :] = quarter[c * 16 : c * 16 + 16, :]
    back = jnp.concatenate(
        [
            jnp.concatenate([msg_ref[c, 0, g * 16 : g * 16 + 16, 0:256] for c in range(4)], axis=0)
            for g in range(4)
        ],
        axis=1,
    )
    grad_hidden = mm(down_t_ref[...], back)
    grad_pre = (grad_hidden * (sig * (1.0 + pre * (1.0 - sig)))).astype(BF)

    @pl.when(step == 0)
    def _():
        gc_ref[...] = jnp.zeros_like(gc_ref)
        gd_ref[...] = jnp.zeros_like(gd_ref)
        gb_ref[...] = jnp.zeros_like(gb_ref)

    gb_ref[...] += jnp.broadcast_to(jnp.sum(grad_pre.astype(F32), axis=1, keepdims=True), (256, 128))
    gd_ref[...] += mm_nt(back, hidden)
    gc_ref[...] += mm_nt(win_ref[...], grad_pre)

    @pl.when(step == 1)
    def _():
        rows = []
        for dy in range(3):
            for cx in range(4):
                r0, r1 = (dy * 4 + cx) * 64, ((dy + 1) * 4 + cx) * 64
                rows.append(gc_ref[r0 : r0 + 64, 0:128] + gc_ref[r1 : r1 + 64, 128:256])
        taps = []
        for dy in range(3):
            for dx in range(3):
                taps.append(rows[dy * 4 + dx] + pltpu.roll(rows[dy * 4 + dx + 1], 64, axis=1))
        taps.append(jnp.zeros((64, 128), F32))
        conv = jnp.concatenate(taps, axis=0)
        conv = jnp.concatenate([conv[q * 128 : q * 128 + 128, :].T for q in range(5)], axis=1)[0:64, :]
        kk = iota((640, 1024), 0)
        cc = iota((640, 1024), 1)
        i, tap = kk & 63, kk >> 6
        place = ones_where((cc == ((i >> 4) << 8) + (i & 15) * 9 + tap) & (tap < 9))
        conv = [mm(h, place) for h in halves(conv)]
        kk = iota((256, 1024), 0)
        cc = iota((256, 1024), 1)
        i, ab = kk & 63, kk >> 6
        place = ones_where(cc == ((i >> 4) << 8) + 144 + (i & 15) * 4 + ab)
        down = [mm(h, place) for h in halves(gd_ref[...])]
        gb = gb_ref[0:64, :] + gb_ref[64:128, :] + gb_ref[128:192, :] + gb_ref[192:256, :]
        bias = [h.astype(F32)[:, 0:1] for h in halves(gb)]
        lane16 = iota((16, 1024), 1)
        for part in range(2):
            for c in range(4):
                d = jnp.concatenate(
                    [down[part][s * 16 : s * 16 + 16, c * 256 : c * 256 + 256] for s in range(4)], axis=1
                )
                both = conv[part][c * 16 : c * 16 + 16, :] + d
                both = jnp.where(lane16 == 208, bias[part][c * 16 : c * 16 + 16, :], both)
                out_ref[c, 32 + part * 16 : 48 + part * 16, :] = both.astype(BF)


def spread_body(msg_ref, out_ref):
    step = pl.program_id(0)
    stack = jnp.concatenate(
        [msg_ref[c, 0:32, g * 256 : g * 256 + 256] for g in range(4) for c in range(4)], axis=0
    )
    row = iota((128, 512), 0) + step * 128
    col = iota((128, 512), 1)
    source = (((row >> 3) & 3) << 7) | (((row >> 1) & 3) << 5) | ((row & 1) << 4) | (row >> 5)
    out_ref[:, 0:256] = mm(ones_where(col == source), stack).astype(BF)
    total = jnp.zeros((16, 1024), F32)
    for c in range(4):
        total = total + (msg_ref[c, 32:48, :].astype(F32) + msg_ref[c, 48:64, :].astype(F32))
    parts = [
        h[:, s * 256 + o : s * 256 + o + 128] for h in halves(total) for o in (0, 128) for s in range(4)
    ]
    stack = jnp.concatenate(parts, axis=0)
    row = iota((128, 256), 0) + step * 128
    col = iota((128, 256), 1)
    r, p = row & 7, row >> 3
    out_ref[:, 256:384] = mm(ones_where((col == (r << 6) + p) & (r < 4)), stack).astype(BF)


def place_body(msg_ref, slot_ref, out_ref):
    step = pl.program_id(0)
    quarter = msg_ref[:, 0:256]
    slot = slot_ref[0:1, :].astype(jnp.int32)
    row = iota((128, 512), 0) + step * 128
    lane = iota((128, 256), 1)
    half = iota((128, 256), 0) & 1
    li = iota((256, 256), 0)
    lo = iota((256, 256), 1)
    same = ((lo >> 6) == ((li >> 5) & 3)) & ((lo & 31) == (li & 31))
    total = jnp.zeros((128, 256), F32)
    for qc in range(2):
        got = mm(ones_where(slot == ((row >> 1) << 1) + qc), quarter)
        total = total + mm(keep((lane >> 7) == half, got), ones_where(same & (((lo >> 5) & 1) == qc)))
    out_ref[:, 0:256] = total.astype(BF)
    r = iota((16, 512), 0)
    src = iota((16, 512), 1) & 7
    summed = mm(ones_where((src < 4) & ((src & 1) == (r & 1)) & (r < 4)), msg_ref[:, 256:384])
    high, low = halves(summed)
    both = jnp.where(iota((16, 128), 0) < 2, high.astype(F32), low.astype(F32)).astype(BF)
    r = iota((128, 16), 0) & 7
    c = iota((128, 16), 1)
    out_ref[:, 256:384] = mm(ones_where((r == c) & (r < 4)), both).astype(BF)


def finish_body(msg_ref, coarse_ref, conv_ref, down_ref, bias_ref):
    step = pl.program_id(0)
    row = iota((128, 512), 0) + step * 128
    col = iota((128, 512), 1)
    qr, g, hf, a, k = row >> 8, (row >> 6) & 3, (row >> 5) & 1, (row >> 4) & 1, row & 15
    source = (k << 5) | (g << 3) | (a << 2) | (qr << 1) | hf
    got = mm(ones_where(col == source), msg_ref[:, 0:256]).astype(BF)
    coarse_ref[...] = jnp.concatenate([got[q * 32 : q * 32 + 32, :] for q in range(4)], axis=1)

    @pl.when(step == 0)
    def _():
        row = iota((256, 512), 0)
        col = iota((256, 512), 1)
        got = mm(ones_where(col == ((row & 63) << 3) + (row >> 6)), msg_ref[:, 256:384])
        near = iota((1024, 576), 0)
        at = iota((1024, 576), 1)
        place = ones_where((at == (near >> 8) * 144 + (near & 255)) & ((near & 255) < 144))
        sub = iota((128, 128), 0)
        lane = iota((128, 128), 1)
        shift = ones_where((sub == lane + 16) & (lane < 64))
        conv = jnp.zeros((16, 576), F32)
        down = jnp.zeros((64, 128), F32)
        for h in range(2):
            low, high = got[h * 128 : h * 128 + 64, :], got[h * 128 + 64 : h * 128 + 128, :]
            wide = jnp.concatenate(
                [x[s * 16 : s * 16 + 16, :] for s in range(4) for x in (low, high)], axis=1
            )
            conv = conv + mm(wide.astype(BF), place)
            down = down + mm(high.astype(BF), shift)
        conv_ref[...] = conv
        down_ref[...] = down[:, 0:64]
        bias_ref[...] = got[64:80, 80:81] + got[192:208, 80:81]


def index_rows(edge_links, edge_turns, corner_links, corner_turns, child_slot):
    side = jnp.arange(4, dtype=jnp.int32)[None, :]
    slot = child_slot[None, :]
    edge = jnp.concatenate(
        [
            (edge_links >> 3).T,
            ((side + 2 + edge_turns) & 3).T,
            (edge_links & 7).T,
            slot >> 3,
            slot & 7,
            jnp.zeros((2, 8), jnp.int32),
        ],
        axis=0,
    ).reshape(1, 128)
    node = jnp.where(corner_links < 0, 127, corner_links >> 3).T
    pixel = ((corner_links & 7) * 4 + ((side + 2 + corner_turns) & 3)).T
    corner = jnp.concatenate([jnp.zeros((4, 112), jnp.int32), node, pixel], axis=1)
    return jnp.concatenate([edge, corner, jnp.zeros((43, 128), jnp.int32)], axis=0).astype(BF)


def gather_weights(conv_weight, conv_bias, down_weight):
    b0 = conv_bias.astype(BF)
    rest = conv_bias - b0.astype(F32)
    b1 = rest.astype(BF)
    b2 = (rest - b1.astype(F32)).astype(BF)
    packed = jnp.concatenate(
        [conv_weight, down_weight.reshape(16, 256), jnp.stack([b0, b1, b2], axis=1), jnp.zeros((16, 61), BF)],
        axis=1,
    )
    every = lax.all_gather(packed, "chan", axis=0, tiled=True)
    taps = every[:, :576].reshape(64, 64, 3, 3).transpose(0, 2, 3, 1)
    weights = jnp.concatenate(
        [
            jnp.pad(taps, ((0, 0), (a, 1 - a), (b, 1 - b), (0, 0))).reshape(64, 1024)
            for a in range(2)
            for b in range(2)
        ],
        axis=0,
    )
    down = every[:, 576:832].reshape(4, 64, 16, 4).transpose(1, 3, 0, 2).reshape(64, 256)
    bias = every[:, 832:835].astype(F32)
    bias = (bias[:, 0] + bias[:, 1]) + bias[:, 2]
    return weights, down, jnp.concatenate([bias] * 4)[:, None]


def on_device(
    features,
    conv_weight,
    conv_bias,
    down_weight,
    cotangent,
    edge_links,
    edge_turns,
    corner_links,
    corner_turns,
    child_slot,
):
    msg_spec = whole(MSG)
    block = pl.BlockSpec((128, 384), lambda i: (i, 0))
    msg = jax.ShapeDtypeStruct(MSG, BF)

    def to_nodes(x):
        return lax.all_to_all(x.reshape(64, 8, 384), "tile", 0, 0, tiled=True).reshape(MSG)

    small = index_rows(edge_links, edge_turns, corner_links, corner_turns, child_slot)
    pieces = call(
        send_body,
        msg,
        (4,),
        [whole((128, 4096)), whole((32, 4096)), whole((48, 128))],
        block,
        flops=10**9,
        moved=2 * 10**6,
    )(features.reshape(128, 4096), cotangent.reshape(32, 4096), small)
    pieces = to_nodes(pieces)
    tiles = lax.all_to_all(features.reshape(4, 2, 16, 4096), "chan", 0, 0, tiled=True)
    weights, down, bias = gather_weights(conv_weight, conv_bias, down_weight)
    picked, slots = call(
        pick_body,
        (msg, jax.ShapeDtypeStruct((8, 512), F32)),
        (4,),
        [msg_spec],
        (block, pl.BlockSpec((8, 128), lambda i: (0, i))),
        flops=10**9,
        moved=10**6,
    )(pieces)
    picked = to_nodes(picked)
    picked = call(regroup_body, msg, (4,), [msg_spec], block, flops=4 * 10**8, moved=10**6)(picked)
    picked = lax.all_to_all(picked.reshape(4, 128, 384), "chan", 0, 0, tiled=True)
    local = call(
        level_body,
        jax.ShapeDtypeStruct((4, 64, 1024), BF),
        (2,),
        [
            pl.BlockSpec((4, 1, 16, 4096), lambda i: (0, i, 0, 0)),
            pl.BlockSpec((4, 1, 64, 384), lambda i: (0, i, 0, 0)),
            whole((256, 1024)),
            whole((256, 1)),
            whole((64, 256)),
            whole((256, 64)),
        ],
        whole((4, 64, 1024)),
        (
            pltpu.VMEM((1024, 1024), BF),
            pltpu.VMEM((1024, 256), F32),
            pltpu.VMEM((64, 256), F32),
            pltpu.VMEM((256, 128), F32),
        ),
        flops=4 * 10**9,
        moved=4 * 10**6,
    )(tiles, picked.reshape(4, 2, 64, 384), weights, bias, down, down.T)
    local = lax.all_to_all(local, "chan", 0, 0, tiled=True)
    out = call(spread_body, msg, (4,), [whole((4, 64, 1024))], block, flops=4 * 10**8, moved=10**6)(local)
    out = to_nodes(out)
    out = call(place_body, msg, (4,), [msg_spec, whole((8, 512))], block, flops=5 * 10**8, moved=10**6)(
        out, slots
    )
    out = to_nodes(out)
    coarse, grad_conv, grad_down, grad_bias = call(
        finish_body,
        (
            jax.ShapeDtypeStruct((32, 4096), BF),
            jax.ShapeDtypeStruct((16, 576), F32),
            jax.ShapeDtypeStruct((64, 64), F32),
            jax.ShapeDtypeStruct((16, 1), F32),
        ),
        (4,),
        [msg_spec],
        (
            pl.BlockSpec((32, 1024), lambda i: (0, i)),
            whole((16, 576)),
            whole((64, 64)),
            whole((16, 1)),
        ),
        flops=4 * 10**8,
        moved=10**6,
    )(out)
    return (coarse.reshape(2, 16, 4096), grad_conv, grad_bias.reshape(16), grad_down)


def solution(mesh):
    in_specs = (
        P("tile", "chan", None),
        P("chan", None),
        P("chan"),
        P(None, "chan"),
        P("tile", "chan", None),
        P("tile", None),
        P("tile", None),
        P("tile", None),
        P("tile", None),
        P("tile"),
    )
    out_specs = (P("tile", "chan", None), P("chan", None), P("chan"), P(None, "chan"))
    return jax.shard_map(
        on_device, mesh=mesh, in_specs=in_specs, out_specs=out_specs, check_vma=False
    )
```

time: 764 us -> 174 us (0.23); the launches traced: 749 us -> 170 us
  blocking collectives: 302 us -> 115 us
  waiting for transfers between devices: 176 us -> 5.59 us
  local copies, waits for them, and re-layouts: 119 us -> 10.5 us
  starting transfers between devices: 72.5 us -> 11.6 us
  matrix products: 42.3 us -> 0 us
  Pallas kernels: 0 us -> 25.3 us
  other arithmetic: 21.5 us -> 1.86 us
  between operations: 15.5 us -> 0.82 us
    all_gather x3 -> x1, blocking collectives: 217 us -> 14.8 us  [gather_weights(): every = lax.all_gather(packed, 'chan', axis=0, tiled=True)]
    psum x1 -> x0, waiting for transfers between devices: 170 us -> none  [on_device(): lax.psum((grad_conv, grad_bias, grad_down), ('tile', 'chan'))]
    all_to_all x0 -> x5, blocking collectives: none -> 99.9 us  [the longest x4 88.8 us: to_nodes(): lax.all_to_all(x.reshape(64, 8, 384), 'tile', 0, 0, tiled=True).reshape(MSG)]
    psum x1 -> x0, blocking collectives: 79.2 us -> none  [on_device(): lax.psum((grad_conv, grad_bias, grad_down), ('tile', 'chan'))]
    all_to_all x6 -> x2, starting transfers between devices: 72.4 us -> 11.6 us  [the longest x1 7.87 us: on_device(): lax.all_to_all(features.reshape(4, 2, 16, 4096), 'chan', 0, 0, tiled=True)]
    dot_general x16 -> x0, matrix products: 36.2 us -> none  [the longest x9 23.7 us: on_device(): jnp.einsum('toyx,tiyx->oi', grad_pre, window, preferred_element_type=jnp....]
    reshape x13 -> x9, local copies, waits for them, and re-layouts: 33 us -> 5.37 us  [the longest x4 2.75 us: gather_weights(): jnp.pad(taps, ((0, 0), (a, 1 - a), (b, 1 - b), (0, 0))).reshape(64, 1024)]
    pallas_call x0 -> x7, Pallas kernels: none -> 25.3 us  [the longest x1 7.67 us: on_device(): call(level_body, jax.ShapeDtypeStruct((4, 64, 1024), BF), (2,), [pl.Block...]
  transfers between devices with their start and end apart: 8 -> 2, of which waited for: 2 -> 1; matrix products, arithmetic and copies ran while one was open for 14% -> 5% of each run, Pallas kernels for 0% -> 1%
where the time goes in v1:
time: 174 us; the launch traced here: 170 us
  blocking collectives  115 us (66%)
  Pallas kernels  25.3 us (15%)
  starting transfers between devices  11.6 us (7%)
  local copies, waits for them, and re-layouts  10.5 us (6%)
  waiting for transfers between devices  5.59 us (3%)
  other arithmetic  1.86 us (1%)
    all_to_all x4, blocking collectives, to_nodes(): lax.all_to_all(x.reshape(64, 8, 384), 'tile', 0, 0, tiled=True).reshape(MSG)  88.8 us
    all_gather x1, blocking collectives, gather_weights(): every = lax.all_gather(packed, 'chan', axis=0, tiled=True)  14.8 us
    all_to_all x1, blocking collectives, on_device(): local = lax.all_to_all(local, 'chan', 0, 0, tiled=True)  11.1 us
    all_to_all x1, starting transfers between devices, on_device(): lax.all_to_all(features.reshape(4, 2, 16, 4096), 'chan', 0, 0, tiled=True)  7.87 us
    pallas_call x1, Pallas kernels, on_device(): call(level_body, jax.ShapeDtypeStruct((4, 64, 1024), BF), (2,), [pl.Block...  7.67 us
    pallas_call x1, Pallas kernels, on_device(): call(pick_body, (msg, jax.ShapeDtypeStruct((8, 512), F32)), (4,), [msg_sp...  5.78 us
    all_to_all x1, waiting for transfers between devices, on_device(): lax.all_to_all(picked.reshape(4, 128, 384), 'chan', 0, 0, tiled=True)  5.59 us
    pallas_call x1, Pallas kernels, on_device(): call(send_body, msg, (4,), [whole((128, 4096)), whole((32, 4096)), whole(...  4.44 us
  transfers between devices with their start and end apart: 2, of which 1 were waited for; matrix products, arithmetic and copies ran while one was open for 5% of the time, Pallas kernels for 1%

profile of v1, /device:TPU:1, one launch (start us, length us, event | category | flops | bytes accessed | tf_op | source)
XLA Modules:
  0.0 170.4 jit_solution(2930284299201039515)
XLA Ops:
  1.3 0.8 fusion.3
  2.5 0.9 copy-done
  3.4 4.4 %shard_map.129 = bf16[512,384]{1,0:T(8,128)(2,1)S(1)} custom-call(bf16[128,4096]{1,0:T(8,128)(2,1)} %bitcast.1.feat_ref, bf16[32,4096]{1,0:T(8,128)(2,1)S(1)} %bitcast.53, bf16[48,128]{1,0:T(8,128)(2,1)S(1)} %maximum_maximum_fusion.small_ref), custom_call_target="tpu_custom_call" | custom-call | flops 1000000000 | bytes 2000000 | tf_op jit(solution)/shard_map/pallas_call | solution.py:413
  7.9 29.3 %all_to_all.35 = bf16[64,8,384]{2,1,0:T(8,128)(2,1)S(1)} all-to-all(bf16[64,8,384]{2,1,0:T(8,128)(2,1)S(1)} %bitcast.49), channel_id=1, replica_groups=mesh['tile'=64,'chan'=4] {'tile'}, dimensions={0} | all-to-all | bytes 786432 | tf_op jit(solution)/shard_map/all_to_all | solution.py:410
  37.1 5.8 %shard_map.130 = (bf16[512,384]{1,0:T(8,128)(2,1)S(1)}, f32[8,512]{1,0:T(8,128)S(1)}) custom-call(bf16[512,384]{1,0:T(8,128)(2,1)S(1)} %bitcast.45), custom_call_target="tpu_custom_call" | custom-call | flops 1000000000 | bytes 1000000 | tf_op jit(solution)/shard_map/pallas_call | solution.py:425
  42.9 20.3 %all_to_all.36 = bf16[64,8,384]{2,1,0:T(8,128)(2,1)S(1)} all-to-all(bf16[64,8,384]{2,1,0:T(8,128)(2,1)S(1)} %bitcast.46), channel_id=1, replica_groups=mesh['tile'=64,'chan'=4] {'tile'}, dimensions={0} | all-to-all | bytes 786432 | tf_op jit(solution)/shard_map/all_to_all | solution.py:410
  63.3 7.9 %all-to-all-start = ((bf16[4,2,16,4096]{3,2,1,0:T(8,128)(2,1)}), bf16[4,2,16,4096]{3,2,1,0:T(8,128)(2,1)S(1)}, u32[]{:S(2)}, u32[]{:S(2)}) async-start(bf16[4,2,16,4096]{3,2,1,0:T(8,128)(2,1)} %bitcast), calls=%async_computation | async-start | bytes 2097152 | tf_op jit(solution)/shard_map/all_to_all | solution.py:423
  72.1 14.8 %all_gather.3 = bf16[64,896]{1,0:T(8,128)(2,1)S(1)} all-gather(bf16[16,896]{1,0:T(8,128)(2,1)S(1)} %concatenate.24), channel_id=1, replica_groups=mesh['tile'=64,'chan'=4] {'chan'}, dimensions={0}, use_global_device_ids=true | all-gather | bytes 143360 | tf_op jit(solution)/shard_map/all_gather | solution.py:377
  88.2 0.8 reshape.105
  89.0 0.8 reshape.106
  89.9 0.9 reshape.107
  90.7 2.2 %reshape.108 = bf16[4,64,16,4]{3,2,1,0:T(8,128)(2,1)S(1)} reshape(bf16[64,256]{1,0:T(8,128)(2,1)S(1)} %slice.29) | data formatting | bytes 65536 | tf_op jit(solution)/shard_map/reshape | solution.py:387
  93.0 0.9 copy.28
  94.1 2.0 %shard_map.131 = bf16[512,384]{1,0:T(8,128)(2,1)} custom-call(bf16[512,384]{1,0:T(8,128)(2,1)S(1)} %bitcast.42), custom_call_target="tpu_custom_call" | custom-call | flops 400000000 | bytes 1000000 | tf_op jit(solution)/shard_map/pallas_call | solution.py:435
  96.1 3.8 %all-to-all-start.3 = ((bf16[4,128,384]{2,1,0:T(8,128)(2,1)}), bf16[4,128,384]{2,1,0:T(8,128)(2,1)S(1)}, u32[]{:S(2)}, u32[]{:S(2)}) async-start(bf16[4,128,384]{2,1,0:T(8,128)(2,1)} %bitcast.14), calls=%async_computation.3 | async-start | bytes 786432 | tf_op jit(solution)/shard_map/all_to_all | solution.py:436
  100.8 5.6 %all-to-all-done.3 = bf16[4,128,384]{2,1,0:T(8,128)(2,1)S(1)} async-done(((bf16[4,128,384]{2,1,0:T(8,128)(2,1)}), bf16[4,128,384]{2,1,0:T(8,128)(2,1)S(1)}, u32[]{:S(2)}, u32[]{:S(2)}) %all-to-all-start.3) | async-done | bytes 393248 | tf_op jit(solution)/shard_map/all_to_all | solution.py:436
  106.4 7.7 %shard_map.132 = bf16[4,64,1024]{2,1,0:T(8,128)(2,1)S(1)} custom-call(bf16[4,2,16,4096]{3,2,1,0:T(8,128)(2,1)S(1)} %all-to-all-done.feat_ref, bf16[4,2,64,384]{3,2,1,0:T(8,128)(2,1)S(1)} %bitcast.43, bf16[256,1024]{1,0:T(8,128)(2,1)S(1)} %pad_maximum_fusion.w_ref, f32[256,1]{1,0:T(8,128)S(1)} %copy.29.bias_ref, bf16[64,256]{1,0:T(8,128)(2,1)S(1)} %copy.30.down_ref, ...), custom_call_target="tpu_custom_call" | custom-call | flops 4000000000 | bytes 4000000 | tf_op jit(solution)/shard_map/pallas_call | solution.py:437
  114.1 11.1 %all_to_all.37.msg_ref = bf16[4,64,1024]{2,1,0:T(8,128)(2,1)S(1)} all-to-all(bf16[4,64,1024]{2,1,0:T(8,128)(2,1)S(1)} %shard_map.132), channel_id=1, replica_groups=mesh['tile'=64,'chan'=4] {'chan'}, dimensions={0} | all-to-all | bytes 1048576 | tf_op jit(solution)/shard_map/all_to_all | solution.py:459
  125.2 1.1 shard_map.133
  126.2 19.0 %all_to_all.38 = bf16[64,8,384]{2,1,0:T(8,128)(2,1)S(1)} all-to-all(bf16[64,8,384]{2,1,0:T(8,128)(2,1)S(1)} %bitcast.50), channel_id=1, replica_groups=mesh['tile'=64,'chan'=4] {'tile'}, dimensions={0} | all-to-all | bytes 786432 | tf_op jit(solution)/shard_map/all_to_all | solution.py:410
  145.2 1.7 shard_map.134
  146.9 20.2 %all_to_all.39 = bf16[64,8,384]{2,1,0:T(8,128)(2,1)S(1)} all-to-all(bf16[64,8,384]{2,1,0:T(8,128)(2,1)S(1)} %bitcast.48), channel_id=1, replica_groups=mesh['tile'=64,'chan'=4] {'tile'}, dimensions={0} | all-to-all | bytes 786432 | tf_op jit(solution)/shard_map/all_to_all | solution.py:410
  167.1 2.6 %shard_map.135 = (bf16[32,4096]{1,0:T(8,128)(2,1)}, f32[16,576]{1,0:T(8,128)}, f32[64,64]{1,0:T(8,128)}, f32[16,1]{1,0:T(8,128)S(1)}) custom-call(bf16[512,384]{1,0:T(8,128)(2,1)S(1)} %bitcast.44), custom_call_target="tpu_custom_call" | custom-call | flops 400000000 | bytes 1000000 | tf_op jit(solution)/shard_map/pallas_call | solution.py:466
  169.7 0.6 reduce.1
  (47 shorter events, 4.3 us)
Async XLA Ops:
  0.6 0.7 copy-start.8
  0.6 0.7 copy-start.6
  2.4 1.0 copy-start
  63.3 7.9 %copy-start.7 = (f32[16]{0:T(128)S(1)}, f32[16]{0:T(128)}, u32[]{:S(2)}) copy-start(f32[16]{0:T(128)} %param.12) | copy-start | bytes 196
  63.3 32.8 %all-to-all-start = ((bf16[4,2,16,4096]{3,2,1,0:T(8,128)(2,1)}), bf16[4,2,16,4096]{3,2,1,0:T(8,128)(2,1)S(1)}, u32[]{:S(2)}, u32[]{:S(2)}) async-start(bf16[4,2,16,4096]{3,2,1,0:T(8,128)(2,1)} %bitcast), calls=%async_computation | async-start | bytes 2097152 | tf_op jit(solution)/shard_map/all_to_all | solution.py:423
  71.1 0.7 copy-start.5
  71.2 0.7 copy-start.4
  96.1 4.2 %copy-start.2 = (bf16[64,1024]{1,0:T(8,128)(2,1)S(1)}, bf16[64,1024]{1,0:T(8,128)(2,1)}, u32[]{:S(2)}) copy-start(bf16[64,1024]{1,0:T(8,128)(2,1)} %reshape.106) | copy-start | bytes 393220
  96.1 4.2 %copy-start.3 = (bf16[64,1024]{1,0:T(8,128)(2,1)S(1)}, bf16[64,1024]{1,0:T(8,128)(2,1)}, u32[]{:S(2)}) copy-start(bf16[64,1024]{1,0:T(8,128)(2,1)} %reshape.107) | copy-start | bytes 393220
  96.1 10.3 %all-to-all-start.3 = ((bf16[4,128,384]{2,1,0:T(8,128)(2,1)}), bf16[4,128,384]{2,1,0:T(8,128)(2,1)S(1)}, u32[]{:S(2)}, u32[]{:S(2)}) async-start(bf16[4,128,384]{2,1,0:T(8,128)(2,1)} %bitcast.14), calls=%async_computation.3 | async-start | bytes 786432 | tf_op jit(solution)/shard_map/all_to_all | solution.py:436
  99.9 0.9 copy-start.1

commit v2 on v1

v2 whole, which is shorter than its diff:
```python
import jax
import jax.numpy as jnp
from jax import lax
from jax.experimental import pallas as pl
from jax.experimental.pallas import tpu as pltpu
from jax.sharding import PartitionSpec as P

BF = jnp.bfloat16
F32 = jnp.float32
NODES = 64
MSG = (NODES * 8, 384)


def iota(shape, dim):
    return lax.broadcasted_iota(jnp.int32, shape, dim)


def down_col(n, start=0):
    return iota((n, 1), 0) + start


def lane_row(n):
    return iota((1, n), 1)


def ones_where(mask):
    return jnp.where(mask, 1.0, 0.0).astype(BF)


def keep(mask, x):
    return jnp.where(mask, x, 0.0).astype(BF)


def mm(a, b):
    return jnp.dot(a, b, preferred_element_type=F32)


def mm_nt(a, b):
    return lax.dot_general(a, b, (((1,), (1,)), ((), ())), preferred_element_type=F32)


def halves(x):
    high = x.astype(BF)
    return high, (x - high.astype(F32)).astype(BF)


def call(body, out_shape, grid, in_specs, out_specs, scratch=(), flops=0, moved=0):
    return pl.pallas_call(
        body,
        out_shape=out_shape,
        grid=grid,
        in_specs=in_specs,
        out_specs=out_specs,
        scratch_shapes=scratch,
        compiler_params=pltpu.CompilerParams(vmem_limit_bytes=48 << 20),
        cost_estimate=pl.CostEstimate(flops=flops, bytes_accessed=moved, transcendentals=0),
    )


def whole(shape):
    return pl.BlockSpec(shape, lambda *i: (0,) * len(shape))


def send_body(me_ref, feat_ref, cot_ref, el_ref, et_ref, cl_ref, ct_ref, slot_ref, out_ref, *peer_refs):
    step = pl.program_id(0)
    for d in range(1, 4):

        @pl.when(step == d)
        def _():
            peer = me_ref[0] ^ d
            peer_refs[d - 1][...] = feat_ref[pl.ds(pl.multiple_of(peer * 32, 32), 32), :]

    cot = cot_ref[...]
    stack = jnp.concatenate([cot[:, q * 256 : q * 256 + 256] for q in range(16)], axis=0)
    row = down_col(128, step * 128)
    k, g, a, qr, hf = row >> 5, (row >> 3) & 3, (row >> 2) & 1, (row >> 1) & 1, row & 1
    source = (qr << 8) | (g << 6) | (hf << 5) | (a << 4) | k
    out_ref[:, 0:256] = mm(ones_where(lane_row(512) == source), stack).astype(BF)

    first = feat_ref[:, 0:128]
    last = feat_ref[:, 3968:4096]
    p = down_col(16, step * 16)
    lane = lane_row(128)
    rim_n = mm_nt(ones_where(lane == 63 - p), first)
    rim_s = mm_nt(ones_where(lane == 64 + p), last)
    pc = down_col(32)
    pos = (pc & 15) + step * 16
    want = jnp.where(pc < 16, pos * 64, (63 - pos) * 64 + 63)
    rim_we = mm_nt(ones_where(lane_row(4096) == want), feat_ref[...])
    cr = down_col(16)
    at_first = jnp.where(cr == 0, 0, jnp.where(cr == 3, 63, -1))
    at_last = jnp.where(cr == 1, 64, jnp.where(cr == 2, 127, -1))
    corners = mm_nt(ones_where(lane == at_first), first) + mm_nt(ones_where(lane == at_last), last)
    tc = down_col(128)
    by_chan = jnp.zeros((16, 128), F32)
    for c in range(4):
        spread = jnp.broadcast_to(corners[c : c + 1, :], (16, 128))
        by_chan = by_chan + mm(keep((lane & 15) == cr, spread), ones_where(lane == (tc >> 4) * 4 + c))

    def over_lanes(x):
        rows = jnp.zeros((x.shape[0], 128), jnp.int32)
        for t in range(8):
            rows = jnp.where((lane & 7) == t, x[:, t : t + 1], rows)
        return rows

    def in_row(x, first_field):
        rows = over_lanes(x)
        side = iota(rows.shape, 0)
        mine = (iota(rows.shape, 1) >> 3) == side + first_field
        return jnp.sum(jnp.where(mine, rows, 0).astype(F32), axis=0, keepdims=True)

    side = iota((4, 8), 0)
    el, cl, slot = el_ref[...], cl_ref[...], slot_ref[...]
    edge = in_row(el >> 3, 0) + in_row((side + 2 + et_ref[...]) & 3, 4) + in_row(el & 7, 8)
    edge = edge + in_row(slot >> 3, 12) + in_row(slot & 7, 13)
    node = over_lanes(jnp.where(cl < 0, 127, cl >> 3)).astype(F32)
    pixel = over_lanes((cl & 7) * 4 + ((side + 2 + ct_ref[...]) & 3)).astype(F32)
    field = lane >> 3
    sub = down_col(16)
    small = jnp.where(sub == 0, edge, 0.0)
    for part in range(4):
        line = jnp.where(field == 14, node[part : part + 1, :], 0.0)
        line = jnp.where(field == 15, pixel[part : part + 1, :], line)
        small = small + jnp.where(sub == part + 1, line, 0.0)
    parts = [rim_n, rim_we[0:16], rim_s, rim_we[16:32], by_chan, small, jnp.zeros((32, 128), F32)]
    stack = jnp.concatenate([x.astype(BF) for x in parts], axis=0)
    r, node = tc & 7, tc >> 3
    source = jnp.where(r < 5, r * 16 + node, jnp.where(r == 5, 80, jnp.where(r == 6, 81 + step, -1)))
    out_ref[:, 256:384] = mm(ones_where(lane == source), stack).astype(BF)


def pick_body(msg_ref, out_ref, slot_ref):
    step = pl.program_id(0)
    cot = msg_ref[:, 0:256]
    misc = msg_ref[:, 256:384]
    col = lane_row(512)
    lane = lane_row(128)
    sub = down_col(128)
    base = ((sub + step * 128) >> 3) << 3
    both = mm(ones_where((col == base + 5) | (col == base + 6)), misc)
    fields = mm(keep((lane & 7) == (sub & 7), both), ones_where((sub >> 3) == lane))
    flip = fields.T
    slot_ref[...] = jnp.broadcast_to(flip[12:13, :] * 8.0 + flip[13:14, :], (8, 128))
    num = fields.astype(jnp.int32)

    def field(f):
        return num[:, f : f + 1]

    slot_row = field(12) * 8 + ((field(13) >> 1) << 1)
    lane2 = lane_row(256)
    fold_r = down_col(256)
    fold = ones_where(lane == (((fold_r >> 6) << 5) | (fold_r & 31)))
    mine = ((lane2 >> 5) & 1) == (field(13) & 1)
    for hf in range(2):
        got = mm(ones_where(col == slot_row + hf), cot)
        out_ref[:, hf * 128 : hf * 128 + 128] = mm(keep(mine, got), fold).astype(BF)
    total = jnp.zeros((128, 128), F32)
    for k in range(4):
        got = mm(ones_where(col == field(k) * 8 + field(4 + k)), misc)
        place = ones_where(lane == k * 16 + (sub & 15))
        total = total + mm(keep((lane >> 4) == field(8 + k), got), place)
    got = mm(ones_where(col == field(14) * 8 + 4), misc)
    total = total + mm(keep(lane == field(15), got), ones_where(jnp.broadcast_to(lane == 64, (128, 128))))
    out_ref[:, 256:384] = total.astype(BF)


def regroup_body(me_ref, msg_ref, conv_ref, bias_ref, down_ref, *out_refs):
    row = down_col(128)
    col = lane_row(512)
    pair, g, k, p = row >> 6, (row >> 4) & 3, row & 15, row & 63
    zero = jnp.zeros((64, 64), BF)
    lane = lane_row(128)
    bias = jnp.where(lane_row(16) == down_col(16), bias_ref[...], 0.0)
    bias = jnp.sum(bias, axis=1, keepdims=True)
    b0 = bias.astype(BF).astype(F32)
    b1 = (bias - b0).astype(BF).astype(F32)
    b2 = (bias - b0) - b1
    bias = jnp.where(lane == 0, b0, jnp.where(lane == 1, b1, jnp.where(lane == 2, b2, 0.0))).astype(BF)
    for d in range(4):
        out_ref = out_refs[d]
        tile = ((me_ref[0] ^ d) << 1) | pair
        out_ref[0:128, 0:256] = mm(
            ones_where(col == ((k << 5) | (g << 3) | tile)), msg_ref[:, 0:256]
        ).astype(BF)
        out_ref[0:128, 256:384] = mm(ones_where(col == ((p << 3) | tile)), msg_ref[:, 256:384]).astype(BF)
        out_ref[128:192, 0:128] = jnp.concatenate([down_ref[...], zero], axis=1)
        out_ref[128:144, 128:384] = conv_ref[:, 0:256]
        out_ref[144:160, 128:384] = conv_ref[:, 256:512]
        out_ref[160:176, 128:256] = jnp.concatenate([conv_ref[:, 512:576], zero[0:16]], axis=1)
        out_ref[160:176, 256:384] = bias
        out_ref[176:192, 128:384] = jnp.zeros((16, 256), BF)


def lay_weights(raw_ref, w_ref, down_ref, down_t_ref, bias_ref):
    raw = jnp.concatenate(
        [
            jnp.concatenate([raw_ref[c, 128 + q * 16 : 144 + q * 16, 128 : 128 + n] for c in range(4)], axis=0)
            for q, n in ((0, 256), (1, 256), (2, 128))
        ],
        axis=1,
    )
    e = iota((640, 1), 0)
    i = (e * 7282) >> 16
    tap = e - i * 9
    dy = (tap * 86) >> 8
    to = jnp.where(e < 576, dy * 256 + (tap - dy * 3) * 64 + i, -9999)
    col = lane_row(1536)
    shifted = mm(raw, ones_where(jnp.where(col < 768, col, col - 832) == to)).astype(BF)
    zero = jnp.zeros((64, 256), BF)
    for a in range(2):
        for b in range(2):
            part = shifted[:, b * 768 : b * 768 + 768]
            row = (a * 2 + b) * 64
            w_ref[row : row + 64, :] = jnp.concatenate([zero, part] if a else [part, zero], axis=1)
    down = jnp.zeros((64, 256), F32)
    down_t = jnp.zeros((256, 64), F32)
    for c in range(4):
        mine = raw_ref[c, 128:192, 0:128]
        l = down_col(128)
        to = jnp.where(l < 64, (l & 3) * 64 + c * 16 + (l >> 2), -1)
        down = down + mm(mine, ones_where(lane_row(256) == to))
        l = lane_row(128)
        to = jnp.where(l < 64, (l & 3) * 64 + c * 16 + (l >> 2), -1)
        down_t = down_t + mm_nt(ones_where(down_col(256) == to), mine)
    down_ref[...] = down.astype(BF)
    down_t_ref[...] = down_t.astype(BF)
    bias = jnp.concatenate([raw_ref[c, 160:176, 256:259].astype(F32) for c in range(4)], axis=0)
    bias = (bias[:, 0:1] + bias[:, 1:2]) + bias[:, 2:3]
    bias_ref[...] = jnp.broadcast_to(jnp.concatenate([bias] * 4, axis=0), (256, 128))


def level_body(me_ref, *refs):
    feat_refs, in_refs, out_refs = refs[0:4], refs[4:8], refs[8:12]
    x_ref, msg_ref, sum_ref, win_ref, gc_ref, gd_ref, gb_ref, w_ref, down_ref, down_t_ref, bias_ref = refs[12:]
    step = pl.program_id(0)
    me = me_ref[0]

    @pl.when(step == 0)
    def _():
        for d in range(4):
            msg_ref[me ^ d] = in_refs[d][...]
        lay_weights(msg_ref, w_ref, down_ref, down_t_ref, bias_ref)

    for d in range(4):
        x_ref[me ^ d] = feat_refs[d][0]
    half = pl.multiple_of(step * 64, 64)
    x = jnp.concatenate([x_ref[c] for c in range(4)], axis=0)
    stack = jnp.concatenate([x[:, q * 512 : q * 512 + 512] for q in range(8)], axis=0)
    l_in = down_col(512)
    to = (
        (((l_in >> 6) & 1) << 8)
        | ((l_in & 1) << 7)
        | ((l_in >> 7) << 5)
        | ((l_in >> 1) & 31)
    )
    split = mm(stack, ones_where(lane_row(512) == to))

    def plane(a, b):
        s = (a * 2 + b) * 128
        return jnp.concatenate([split[q * 64 : q * 64 + 64, s : s + 128] for q in range(8)], axis=1)

    rim = [msg_ref[c, pl.ds(half, 64), 256:384].astype(F32) for c in range(4)]
    flip = [r.T.astype(BF) for r in rim]

    def strip(k):
        return jnp.concatenate([f[k * 16 : k * 16 + 16, :] for f in flip], axis=0)

    def corner(k):
        return jnp.concatenate([r[k * 16 : k * 16 + 16, 64:65] for r in rim], axis=0)

    lane = lane_row(1024)
    v = lane & 31
    pos = down_col(64)
    cols = []
    for a in range(2):
        y = ((lane >> 5) << 1) + a
        west = jnp.where(v == 0, 63 - y, -1)
        east = jnp.where(v == 31, y, -1)
        side = mm(strip(1), ones_where(west == pos)) + mm(strip(3), ones_where(east == pos))
        even, odd = plane(a, 0), plane(a, 1)
        cols.append(
            [
                jnp.where(v == 0, side, pltpu.roll(odd, 1, axis=1)),
                even,
                odd,
                jnp.where(v == 31, side, pltpu.roll(even, 1023, axis=1)),
            ]
        )
    lane_e = lane_row(512)
    inner = lane_e & 127
    at = ((inner & 31) << 1) + (lane_e >> 7)
    north = jnp.where(inner < 32, at - 1, -1)
    south = jnp.where(inner >= 96, 64 - at, -1)
    ends = mm(strip(0), ones_where(north == pos)) + mm(strip(2), ones_where(south == pos))
    for spot, k in ((0, 0), (96, 1), (384 + 31, 3), (384 + 127, 2)):
        ends = jnp.where(lane_e == spot, corner(k), ends)
    blank = jnp.zeros((64, 896), F32)
    for cx in range(4):
        end = ends[:, cx * 128 : cx * 128 + 128]
        top = jnp.where(lane < 32, jnp.concatenate([end, blank], axis=1), pltpu.roll(cols[1][cx], 32, axis=1))
        low = jnp.where(lane >= 992, jnp.concatenate([blank, end], axis=1), pltpu.roll(cols[0][cx], 992, axis=1))
        for ry, w in enumerate((top, cols[0][cx], cols[1][cx], low)):
            at_row = (ry * 4 + cx) * 64
            win_ref[at_row : at_row + 64, :] = w.astype(BF)

    pre = mm(w_ref[...], win_ref[...]) + bias_ref[:, 0:1]
    sig = 1.0 / (1.0 + jnp.exp(-pre))
    hidden = (pre * sig).astype(BF)
    quarter = mm(down_ref[...], hidden).astype(BF)
    for c in range(4):
        sum_ref[c, pl.ds(pl.multiple_of(step * 16, 16), 16), :] = quarter[c * 16 : c * 16 + 16, :]
    back = jnp.concatenate(
        [
            jnp.concatenate(
                [msg_ref[c, pl.ds(half + g * 16, 16), 0:256] for c in range(4)], axis=0
            )
            for g in range(4)
        ],
        axis=1,
    )
    grad_hidden = mm(down_t_ref[...], back)
    grad_pre = (grad_hidden * (sig * (1.0 + pre * (1.0 - sig)))).astype(BF)

    @pl.when(step == 0)
    def _():
        gc_ref[...] = jnp.zeros_like(gc_ref)
        gd_ref[...] = jnp.zeros_like(gd_ref)
        gb_ref[...] = jnp.zeros_like(gb_ref)

    gb_ref[...] += jnp.broadcast_to(jnp.sum(grad_pre.astype(F32), axis=1, keepdims=True), (256, 128))
    gd_ref[...] += mm_nt(back, hidden)
    gc_ref[...] += mm_nt(win_ref[...], grad_pre)

    @pl.when(step == 1)
    def _():
        rows = []
        for dy in range(3):
            for cx in range(4):
                r0, r1 = (dy * 4 + cx) * 64, ((dy + 1) * 4 + cx) * 64
                rows.append(gc_ref[r0 : r0 + 64, 0:128] + gc_ref[r1 : r1 + 64, 128:256])
        taps = []
        for dy in range(3):
            for dx in range(3):
                taps.append(rows[dy * 4 + dx] + pltpu.roll(rows[dy * 4 + dx + 1], 64, axis=1))
        taps.append(jnp.zeros((64, 128), F32))
        conv = jnp.concatenate(taps, axis=0)
        conv = jnp.concatenate([conv[q * 128 : q * 128 + 128, :].T for q in range(5)], axis=1)[0:64, :]
        kk = down_col(640)
        cc = lane_row(1024)
        i, tap = kk & 63, kk >> 6
        place = ones_where(cc == jnp.where(tap < 9, ((i >> 4) << 8) + (i & 15) * 9 + tap, -1))
        conv = [mm(h, place) for h in halves(conv)]
        kk = down_col(256)
        i, ab = kk & 63, kk >> 6
        place = ones_where(cc == ((i >> 4) << 8) + 144 + (i & 15) * 4 + ab)
        down = [mm(h, place) for h in halves(gd_ref[...])]
        gb = gb_ref[0:64, :] + gb_ref[64:128, :] + gb_ref[128:192, :] + gb_ref[192:256, :]
        bias = [h.astype(F32)[:, 0:1] for h in halves(gb)]
        lane16 = lane_row(1024)
        for part in range(2):
            for c in range(4):
                d = jnp.concatenate(
                    [down[part][s * 16 : s * 16 + 16, c * 256 : c * 256 + 256] for s in range(4)], axis=1
                )
                both = conv[part][c * 16 : c * 16 + 16, :] + d
                both = jnp.where(lane16 == 208, bias[part][c * 16 : c * 16 + 16, :], both)
                sum_ref[c, 32 + part * 16 : 48 + part * 16, :] = both.astype(BF)
        for d in range(4):
            out_refs[d][...] = sum_ref[me ^ d]


def spread_body(me_ref, *refs):
    in_refs, out_ref, msg_ref = refs[0:4], refs[4], refs[5]
    step = pl.program_id(0)

    @pl.when(step == 0)
    def _():
        for d in range(4):
            msg_ref[me_ref[0] ^ d] = in_refs[d][...]

    stack = jnp.concatenate(
        [msg_ref[c, 0:32, g * 256 : g * 256 + 256] for g in range(4) for c in range(4)], axis=0
    )
    row = down_col(128, step * 128)
    source = (((row >> 3) & 3) << 7) | (((row >> 1) & 3) << 5) | ((row & 1) << 4) | (row >> 5)
    out_ref[:, 0:256] = mm(ones_where(lane_row(512) == source), stack).astype(BF)
    total = jnp.zeros((16, 1024), F32)
    for c in range(4):
        total = total + (msg_ref[c, 32:48, :].astype(F32) + msg_ref[c, 48:64, :].astype(F32))
    parts = [
        h[:, s * 256 + o : s * 256 + o + 128] for h in halves(total) for o in (0, 128) for s in range(4)
    ]
    stack = jnp.concatenate(parts, axis=0)
    r, p = row & 7, row >> 3
    source = jnp.where(r < 4, (r << 6) + p, -1)
    out_ref[:, 256:384] = mm(ones_where(lane_row(256) == source), stack).astype(BF)


def place_body(msg_ref, slot_ref, out_ref):
    step = pl.program_id(0)
    quarter = msg_ref[:, 0:256]
    slot = slot_ref[0:1, :].astype(jnp.int32)
    row = down_col(128, step * 128)
    lane = lane_row(256)
    half = row & 1
    li = down_col(256)
    to = (((li >> 5) & 3) << 6) | (li & 31)
    total = jnp.zeros((128, 256), F32)
    for qc in range(2):
        got = mm(ones_where(slot == ((row >> 1) << 1) + qc), quarter)
        total = total + mm(keep((lane >> 7) == half, got), ones_where(lane == to + qc * 32))
    out_ref[:, 0:256] = total.astype(BF)
    r = down_col(16)
    src = lane_row(512) & 7
    src = jnp.where(src < 4, src & 1, -1)
    summed = mm(ones_where(src == jnp.where(r < 4, r & 1, -2)), msg_ref[:, 256:384])
    high, low = halves(summed)
    both = jnp.where(iota((16, 128), 0) < 2, high.astype(F32), low.astype(F32)).astype(BF)
    r = row & 7
    out_ref[:, 256:384] = mm(ones_where(lane_row(16) == jnp.where(r < 4, r, -1)), both).astype(BF)


def finish_body(msg_ref, coarse_ref, conv_ref, down_ref, bias_ref):
    step = pl.program_id(0)
    row = down_col(128, step * 128)
    col = lane_row(512)
    qr, g, hf, a, k = row >> 8, (row >> 6) & 3, (row >> 5) & 1, (row >> 4) & 1, row & 15
    source = (k << 5) | (g << 3) | (a << 2) | (qr << 1) | hf
    got = mm(ones_where(col == source), msg_ref[:, 0:256]).astype(BF)
    coarse_ref[...] = jnp.concatenate([got[q * 32 : q * 32 + 32, :] for q in range(4)], axis=1)

    @pl.when(step == 0)
    def _():
        row = down_col(256)
        got = mm(ones_where(col == ((row & 63) << 3) + (row >> 6)), msg_ref[:, 256:384])
        near = down_col(1024)
        to = jnp.where((near & 255) < 144, (near >> 8) * 144 + (near & 255), -1)
        place = ones_where(lane_row(576) == to)
        lane = lane_row(128)
        shift = ones_where(down_col(128) == jnp.where(lane < 64, lane + 16, -1))
        conv = jnp.zeros((16, 576), F32)
        down = jnp.zeros((64, 128), F32)
        for h in range(2):
            low, high = got[h * 128 : h * 128 + 64, :], got[h * 128 + 64 : h * 128 + 128, :]
            wide = jnp.concatenate(
                [x[s * 16 : s * 16 + 16, :] for s in range(4) for x in (low, high)], axis=1
            )
            conv = conv + mm(wide.astype(BF), place)
            down = down + mm(high.astype(BF), shift)
        conv_ref[...] = conv
        down_ref[...] = down[:, 0:64]
        bias = got[64:80, 80:81] + got[192:208, 80:81]
        bias_ref[...] = jnp.sum(jnp.where(lane_row(16) == down_col(16), bias, 0.0), axis=0, keepdims=True)


def to_peers(parts):
    return [parts[0]] + [
        lax.ppermute(parts[d], "chan", [(i, i ^ d) for i in range(4)]) for d in range(1, 4)
    ]


def on_device(
    features,
    conv_weight,
    conv_bias,
    down_weight,
    cotangent,
    edge_links,
    edge_turns,
    corner_links,
    corner_turns,
    child_slot,
):
    msg_spec = whole(MSG)
    block = pl.BlockSpec((128, 384), lambda i: (i, 0))
    msg = jax.ShapeDtypeStruct(MSG, BF)

    def to_nodes(x):
        return lax.all_to_all(x.reshape(64, 8, 384), "tile", 0, 0, tiled=True).reshape(MSG)

    me = lax.axis_index("chan").astype(jnp.int32).reshape(1)
    scalar = pl.BlockSpec(memory_space=pltpu.SMEM)
    peer_rows = jax.ShapeDtypeStruct((32, 4096), BF)
    pieces, *tiles = call(
        send_body,
        (msg, peer_rows, peer_rows, peer_rows),
        (4,),
        [scalar, whole((128, 4096)), whole((32, 4096))] + [whole((4, 8))] * 4 + [whole((1, 8))],
        (block,) + (whole((32, 4096)),) * 3,
        flops=10**9,
        moved=2 * 10**6,
    )(
        me,
        features.reshape(128, 4096),
        cotangent.reshape(32, 4096),
        edge_links.T,
        edge_turns.T,
        corner_links.T,
        corner_turns.T,
        child_slot.reshape(1, 8),
    )
    tiles = to_peers([None] + list(tiles))[1:]
    pieces, *tiles = lax.optimization_barrier((to_nodes(pieces), *tiles))
    picked, slots = call(
        pick_body,
        (msg, jax.ShapeDtypeStruct((8, 512), F32)),
        (4,),
        [msg_spec],
        (block, pl.BlockSpec((8, 128), lambda i: (0, i))),
        flops=10**9,
        moved=10**6,
    )(pieces)
    picked = to_nodes(picked)
    group = jax.ShapeDtypeStruct((192, 384), BF)
    picked = call(
        regroup_body,
        (group,) * 4,
        (1,),
        [scalar, msg_spec, whole((16, 576)), whole((1, 16)), whole((64, 64))],
        (whole((192, 384)),) * 4,
        flops=4 * 10**8,
        moved=10**6,
    )(me, picked, conv_weight, conv_bias.reshape(1, 16), down_weight)
    picked = to_peers(picked)
    pair = pl.BlockSpec((1, 16, 4096), lambda i, m: (i, 0, 0))
    local = pl.pallas_call(
        level_body,
        out_shape=(jax.ShapeDtypeStruct((64, 1024), BF),) * 4,
        grid_spec=pltpu.PrefetchScalarGridSpec(
            num_scalar_prefetch=1,
            grid=(2,),
            in_specs=[pl.BlockSpec((1, 16, 4096), lambda i, m: (m[0] * 2 + i, 0, 0))]
            + [pair] * 3
            + [whole((192, 384))] * 4,
            out_specs=(whole((64, 1024)),) * 4,
            scratch_shapes=(
                pltpu.VMEM((4, 16, 4096), BF),
                pltpu.VMEM((4, 192, 384), BF),
                pltpu.VMEM((4, 64, 1024), BF),
                pltpu.VMEM((1024, 1024), BF),
                pltpu.VMEM((1024, 256), F32),
                pltpu.VMEM((64, 256), F32),
                pltpu.VMEM((256, 128), F32),
                pltpu.VMEM((256, 1024), BF),
                pltpu.VMEM((64, 256), BF),
                pltpu.VMEM((256, 64), BF),
                pltpu.VMEM((256, 128), F32),
            ),
        ),
        compiler_params=pltpu.CompilerParams(vmem_limit_bytes=48 << 20),
        cost_estimate=pl.CostEstimate(flops=4 * 10**9, bytes_accessed=4 * 10**6, transcendentals=0),
    )(me, features, *[t.reshape(2, 16, 4096) for t in tiles], *picked)
    local = to_peers(local)
    out = call(
        spread_body,
        msg,
        (4,),
        [scalar] + [whole((64, 1024))] * 4,
        block,
        (pltpu.VMEM((4, 64, 1024), BF),),
        flops=4 * 10**8,
        moved=10**6,
    )(me, *local)
    out = to_nodes(out)
    out = call(place_body, msg, (4,), [msg_spec, whole((8, 512))], block, flops=5 * 10**8, moved=10**6)(
        out, slots
    )
    out = to_nodes(out)
    coarse, grad_conv, grad_down, grad_bias = call(
        finish_body,
        (
            jax.ShapeDtypeStruct((32, 4096), BF),
            jax.ShapeDtypeStruct((16, 576), F32),
            jax.ShapeDtypeStruct((64, 64), F32),
            jax.ShapeDtypeStruct((1, 16), F32),
        ),
        (4,),
        [msg_spec],
        (
            pl.BlockSpec((32, 1024), lambda i: (0, i)),
            whole((16, 576)),
            whole((64, 64)),
            whole((1, 16)),
        ),
        flops=4 * 10**8,
        moved=10**6,
    )(out)
    return (coarse.reshape(2, 16, 4096), grad_conv, grad_bias.reshape(16), grad_down)


def solution(mesh):
    in_specs = (
        P("tile", "chan", None),
        P("chan", None),
        P("chan"),
        P(None, "chan"),
        P("tile", "chan", None),
        P("tile", None),
        P("tile", None),
        P("tile", None),
        P("tile", None),
        P("tile"),
    )
    out_specs = (P("tile", "chan", None), P("chan", None), P("chan"), P(None, "chan"))
    return jax.shard_map(
        on_device, mesh=mesh, in_specs=in_specs, out_specs=out_specs, check_vma=False
    )
```

time: 174 us -> 150 us (0.86); the launches traced: 170 us -> 148 us
  blocking collectives: 115 us -> 66.9 us
  waiting for transfers between devices: 5.59 us -> 28.9 us
  starting transfers between devices: 11.6 us -> 24.9 us
  local copies, waits for them, and re-layouts: 10.5 us -> 2.88 us
  other arithmetic: 1.86 us -> 0 us
    ppermute x0 -> x9, waiting for transfers between devices: none -> 28.9 us  [to_peers(): lax.ppermute(parts[d], 'chan', [(i, i ^ d) for i in range(4)])]
    all_to_all x4 -> x3, blocking collectives: 88.8 us -> 66.9 us  [to_nodes(): lax.all_to_all(x.reshape(64, 8, 384), 'tile', 0, 0, tiled=True).reshape(MSG)]
    all_gather x1 -> x0, blocking collectives: 14.8 us -> none  [gather_weights(): every = lax.all_gather(packed, 'chan', axis=0, tiled=True)]
    all_to_all x1 -> x0, blocking collectives: 11.1 us -> none  [on_device(): local = lax.all_to_all(local, 'chan', 0, 0, tiled=True)]
    ppermute x0 -> x9, starting transfers between devices: none -> 9.82 us  [to_peers(): lax.ppermute(parts[d], 'chan', [(i, i ^ d) for i in range(4)])]
    all_to_all x2 -> x1, waiting for transfers between devices: 5.59 us -> 0.01 us  [to_nodes(): lax.all_to_all(x.reshape(64, 8, 384), 'tile', 0, 0, tiled=True).reshape(MSG)]
    reshape x9 -> x0, local copies, waits for them, and re-layouts: 5.37 us -> none  [the longest x4 2.75 us: gather_weights(): jnp.pad(taps, ((0, 0), (a, 1 - a), (b, 1 - b), (0, 0))).reshape(64, 1024)]
    all_to_all x2 -> x1, starting transfers between devices: 11.6 us -> 15.1 us  [to_nodes(): lax.all_to_all(x.reshape(64, 8, 384), 'tile', 0, 0, tiled=True).reshape(MSG)]
  transfers between devices with their start and end apart: 2 -> 10, of which waited for: 1 -> 6; matrix products, arithmetic and copies ran while one was open for 5% -> 0% of each run, Pallas kernels for 1% -> 0%
where the time goes in v2:
time: 150 us; the launch traced here: 148 us
  blocking collectives  66.9 us (45%)
  waiting for transfers between devices  28.9 us (19%)
  starting transfers between devices  24.9 us (17%)
  Pallas kernels  23.9 us (16%)
  local copies, waits for them, and re-layouts  2.88 us (2%)
    all_to_all x3, blocking collectives, to_nodes(): lax.all_to_all(x.reshape(64, 8, 384), 'tile', 0, 0, tiled=True).reshape(MSG)  66.9 us
    ppermute x9, waiting for transfers between devices, to_peers(): lax.ppermute(parts[d], 'chan', [(i, i ^ d) for i in range(4)])  28.9 us
    all_to_all x1, starting transfers between devices, to_nodes(): lax.all_to_all(x.reshape(64, 8, 384), 'tile', 0, 0, tiled=True).reshape(MSG)  15.1 us
    ppermute x9, starting transfers between devices, to_peers(): lax.ppermute(parts[d], 'chan', [(i, i ^ d) for i in range(4)])  9.82 us
    pallas_call x1, Pallas kernels, on_device(): pl.pallas_call(level_body, out_shape=(jax.ShapeDtypeStruct((64, 1024), BF...  8.36 us
    pallas_call x1, Pallas kernels, on_device(): call(pick_body, (msg, jax.ShapeDtypeStruct((8, 512), F32)), (4,), [msg_sp...  5.79 us
    pallas_call x1, Pallas kernels, on_device(): call(send_body, (msg, peer_rows, peer_rows, peer_rows), (4,), [scalar, wh...  3.95 us
  transfers between devices with their start and end apart: 10, of which 6 were waited for; matrix products, arithmetic and copies ran while one was open for 0% of the time, Pallas kernels for 0%

profile of v2, /device:TPU:1, one launch (start us, length us, event | category | flops | bytes accessed | tf_op | source)
XLA Modules:
  0.0 148.3 jit_solution(15935562098621207900)
XLA Ops:
  0.7 0.6 copy-done.8
  1.4 1.2 copy-done
  2.6 0.9 copy-done.2
  3.5 3.9 %shard_map.129 = (bf16[512,384]{1,0:T(8,128)(2,1)}, bf16[32,4096]{1,0:T(8,128)(2,1)S(1)}, bf16[32,4096]{1,0:T(8,128)(2,1)S(1)}, bf16[32,4096]{1,0:T(8,128)(2,1)S(1)}) custom-call(s32[1]{0:T(128)} %bitcast.me_ref, bf16[128,4096]{1,0:T(8,128)(2,1)S(1)} %bitcast.29, bf16[32,4096]{1,0:T(8,128)(2,1)S(1)} %bitcast.30, s32[4,8]{1,0:T(4,128)S(1)} %bitcast.34, ...), custom_call_target="tpu_custom_call" | custom-call | flops 1000000000 | bytes 2000000 | tf_op jit(solution)/shard_map/pallas_call | solution.py:484
  7.5 15.1 %all-to-all-start = ((bf16[64,8,384]{2,1,0:T(8,128)(2,1)}), bf16[64,8,384]{2,1,0:T(8,128)(2,1)S(1)}, u32[]{:S(2)}, u32[]{:S(2)}) async-start(bf16[64,8,384]{2,1,0:T(8,128)(2,1)} %bitcast.8), calls=%async_computation | async-start | bytes 786432 | tf_op jit(solution)/shard_map/all_to_all | solution.py:479
  22.6 1.0 collective-permute-start
  24.1 1.3 collective-permute-start.2
  25.4 9.7 %collective-permute-done.1 = bf16[32,4096]{1,0:T(8,128)(2,1)S(1)} collective-permute-done((bf16[32,4096]{1,0:T(8,128)(2,1)S(1)}, bf16[32,4096]{1,0:T(8,128)(2,1)S(1)}, u32[]{:S(2)}, u32[]{:S(2)}) %collective-permute-start.1) | collective-permute-done | bytes 262176 | tf_op jit(solution)/shard_map/ppermute | solution.py:458
  35.0 6.1 %collective-permute-done.2 = bf16[32,4096]{1,0:T(8,128)(2,1)S(1)} collective-permute-done((bf16[32,4096]{1,0:T(8,128)(2,1)S(1)}, bf16[32,4096]{1,0:T(8,128)(2,1)S(1)}, u32[]{:S(2)}, u32[]{:S(2)}) %collective-permute-start.2) | collective-permute-done | bytes 262176 | tf_op jit(solution)/shard_map/ppermute | solution.py:458
  41.2 5.8 %shard_map.130 = (bf16[512,384]{1,0:T(8,128)(2,1)S(1)}, f32[8,512]{1,0:T(8,128)S(1)}) custom-call(bf16[512,384]{1,0:T(8,128)(2,1)S(1)} %bitcast.22), custom_call_target="tpu_custom_call" | custom-call | flops 1000000000 | bytes 1000000 | tf_op jit(solution)/shard_map/pallas_call | solution.py:504
  47.0 26.2 %all_to_all.20 = bf16[64,8,384]{2,1,0:T(8,128)(2,1)S(1)} all-to-all(bf16[64,8,384]{2,1,0:T(8,128)(2,1)S(1)} %bitcast.26), channel_id=1, replica_groups=mesh['tile'=64,'chan'=4] {'tile'}, dimensions={0} | all-to-all | bytes 786432 | tf_op jit(solution)/shard_map/all_to_all | solution.py:479
  73.7 2.9 %collective-permute-start.3 = (bf16[192,384]{1,0:T(8,128)(2,1)S(1)}, bf16[192,384]{1,0:T(8,128)(2,1)S(1)}, u32[]{:S(2)}, u32[]{:S(2)}) collective-permute-start(bf16[192,384]{1,0:T(8,128)(2,1)S(1)} %get-tuple-element.36), channel_id=1, source_target_pairs={{0,1},{1,0},{2,3},{3,2},{4,5},{5,4},{6,7},{7,6},{8,9},{9,8},{10,11... | collective-permute-start | bytes 442376 | tf_op jit(solution)/shard_map/ppermute | solution.py:458
  76.6 1.7 %collective-permute-start.5 = (bf16[192,384]{1,0:T(8,128)(2,1)S(1)}, bf16[192,384]{1,0:T(8,128)(2,1)S(1)}, u32[]{:S(2)}, u32[]{:S(2)}) collective-permute-start(bf16[192,384]{1,0:T(8,128)(2,1)S(1)} %get-tuple-element.38), channel_id=1, source_target_pairs={{0,3},{1,2},{2,1},{3,0},{4,7},{5,6},{6,5},{7,4},{8,11},{9,10},{10,... | collective-permute-start | bytes 442376 | tf_op jit(solution)/shard_map/ppermute | solution.py:458
  78.3 3.7 %collective-permute-done.4.refs_6_ = bf16[192,384]{1,0:T(8,128)(2,1)S(1)} collective-permute-done((bf16[192,384]{1,0:T(8,128)(2,1)S(1)}, bf16[192,384]{1,0:T(8,128)(2,1)S(1)}, u32[]{:S(2)}, u32[]{:S(2)}) %collective-permute-start.4) | collective-permute-done | bytes 147488 | tf_op jit(solution)/shard_map/ppermute | solution.py:458
  82.0 3.3 %collective-permute-done.5.refs_7_ = bf16[192,384]{1,0:T(8,128)(2,1)S(1)} collective-permute-done((bf16[192,384]{1,0:T(8,128)(2,1)S(1)}, bf16[192,384]{1,0:T(8,128)(2,1)S(1)}, u32[]{:S(2)}, u32[]{:S(2)}) %collective-permute-start.5) | collective-permute-done | bytes 147488 | tf_op jit(solution)/shard_map/ppermute | solution.py:458
  85.3 8.4 %shard_map.132 = (bf16[64,1024]{1,0:T(8,128)(2,1)S(1)}, bf16[64,1024]{1,0:T(8,128)(2,1)S(1)}, bf16[64,1024]{1,0:T(8,128)(2,1)S(1)}, bf16[64,1024]{1,0:T(8,128)(2,1)S(1)}) custom-call(s32[1]{0:T(128)} %bitcast.me_ref, bf16[8,16,4096]{2,1,0:T(8,128)(2,1)S(1)} %copy-done.1, bf16[2,16,4096]{2,1,0:T(8,128)(2,1)S(1)} %bitcast.31, ...), custom_call_target="tpu_custom_call" | custom-call | flops 4000000000 | bytes 4000000 | tf_op jit(solution)/shard_map/pallas_call | solution.py:526
  94.2 1.9 %collective-permute-start.8 = (bf16[64,1024]{1,0:T(8,128)(2,1)S(1)}, bf16[64,1024]{1,0:T(8,128)(2,1)S(1)}, u32[]{:S(2)}, u32[]{:S(2)}) collective-permute-start(bf16[64,1024]{1,0:T(8,128)(2,1)S(1)} %get-tuple-element.42), channel_id=1, source_target_pairs={{0,3},{1,2},{2,1},{3,0},{4,7},{5,6},{6,5},{7,4},{8,11},{9,10},{10,... | collective-permute-start | bytes 393224 | tf_op jit(solution)/shard_map/ppermute | solution.py:458
  96.1 2.9 %collective-permute-done.7.refs_2_ = bf16[64,1024]{1,0:T(8,128)(2,1)S(1)} collective-permute-done((bf16[64,1024]{1,0:T(8,128)(2,1)S(1)}, bf16[64,1024]{1,0:T(8,128)(2,1)S(1)}, u32[]{:S(2)}, u32[]{:S(2)}) %collective-permute-start.7) | collective-permute-done | bytes 131104 | tf_op jit(solution)/shard_map/ppermute | solution.py:458
  99.0 3.2 %collective-permute-done.8.refs_3_ = bf16[64,1024]{1,0:T(8,128)(2,1)S(1)} collective-permute-done((bf16[64,1024]{1,0:T(8,128)(2,1)S(1)}, bf16[64,1024]{1,0:T(8,128)(2,1)S(1)}, u32[]{:S(2)}, u32[]{:S(2)}) %collective-permute-start.8) | collective-permute-done | bytes 131104 | tf_op jit(solution)/shard_map/ppermute | solution.py:458
  102.2 1.1 shard_map.133
  103.3 20.4 %all_to_all.21 = bf16[64,8,384]{2,1,0:T(8,128)(2,1)S(1)} all-to-all(bf16[64,8,384]{2,1,0:T(8,128)(2,1)S(1)} %bitcast.24), channel_id=1, replica_groups=mesh['tile'=64,'chan'=4] {'tile'}, dimensions={0} | all-to-all | bytes 786432 | tf_op jit(solution)/shard_map/all_to_all | solution.py:479
  123.7 1.6 %shard_map.134 = bf16[512,384]{1,0:T(8,128)(2,1)S(1)} custom-call(bf16[512,384]{1,0:T(8,128)(2,1)S(1)} %bitcast.27, f32[8,512]{1,0:T(8,128)S(1)} %get-tuple-element.43.slot_ref), custom_call_target="tpu_custom_call" | custom-call | flops 500000000 | bytes 1000000 | tf_op jit(solution)/shard_map/pallas_call | solution.py:565
  125.4 20.3 %all_to_all.22 = bf16[64,8,384]{2,1,0:T(8,128)(2,1)S(1)} all-to-all(bf16[64,8,384]{2,1,0:T(8,128)(2,1)S(1)} %bitcast.28), channel_id=1, replica_groups=mesh['tile'=64,'chan'=4] {'tile'}, dimensions={0} | all-to-all | bytes 786432 | tf_op jit(solution)/shard_map/all_to_all | solution.py:479
  145.7 2.6 %shard_map.135 = (bf16[32,4096]{1,0:T(8,128)(2,1)}, f32[16,576]{1,0:T(8,128)}, f32[64,64]{1,0:T(8,128)}, f32[1,16]{1,0:T(1,128)}) custom-call(bf16[512,384]{1,0:T(8,128)(2,1)S(1)} %bitcast.25), custom_call_target="tpu_custom_call" | custom-call | flops 400000000 | bytes 1000000 | tf_op jit(solution)/shard_map/pallas_call | solution.py:569
  (28 shorter events, 1.6 us)
Async XLA Ops:
  0.6 0.7 copy-start.8
  0.6 0.7 copy-start.7
  0.7 0.7 copy-start.6
  0.7 0.7 copy-start.5
  0.7 0.7 copy-start.9
  1.4 1.2 copy-start
  2.6 0.9 copy-start.2
  7.5 33.7 %all-to-all-start = ((bf16[64,8,384]{2,1,0:T(8,128)(2,1)}), bf16[64,8,384]{2,1,0:T(8,128)(2,1)S(1)}, u32[]{:S(2)}, u32[]{:S(2)}) async-start(bf16[64,8,384]{2,1,0:T(8,128)(2,1)} %bitcast.8), calls=%async_computation | async-start | bytes 786432 | tf_op jit(solution)/shard_map/all_to_all | solution.py:479
  22.6 2.8 %collective-permute-start = (bf16[32,4096]{1,0:T(8,128)(2,1)S(1)}, bf16[32,4096]{1,0:T(8,128)(2,1)S(1)}, u32[]{:S(2)}, u32[]{:S(2)}) collective-permute-start(bf16[32,4096]{1,0:T(8,128)(2,1)S(1)} %get-tuple-element.27), channel_id=1, source_target_pairs={{0,1},{1,0},{2,3},{3,2},{4,5},{5,4},{6,7},{7,6},{8,9},{9,8},{10,11... | collective-permute-start | bytes 786440 | tf_op jit(solution)/shard_map/ppermute | solution.py:458
  23.7 11.4 %collective-permute-start.1 = (bf16[32,4096]{1,0:T(8,128)(2,1)S(1)}, bf16[32,4096]{1,0:T(8,128)(2,1)S(1)}, u32[]{:S(2)}, u32[]{:S(2)}) collective-permute-start(bf16[32,4096]{1,0:T(8,128)(2,1)S(1)} %get-tuple-element.28), channel_id=1, source_target_pairs={{0,2},{1,3},{2,0},{3,1},{4,6},{5,7},{6,4},{7,5},{8,10},{9,11},{10,... | collective-permute-start | bytes 786440 | tf_op jit(solution)/shard_map/ppermute | solution.py:458
  24.1 17.1 %collective-permute-start.2 = (bf16[32,4096]{1,0:T(8,128)(2,1)S(1)}, bf16[32,4096]{1,0:T(8,128)(2,1)S(1)}, u32[]{:S(2)}, u32[]{:S(2)}) collective-permute-start(bf16[32,4096]{1,0:T(8,128)(2,1)S(1)} %get-tuple-element.29), channel_id=1, source_target_pairs={{0,3},{1,2},{2,1},{3,0},{4,7},{5,6},{6,5},{7,4},{8,11},{9,10},{10,... | collective-permute-start | bytes 786440 | tf_op jit(solution)/shard_map/ppermute | solution.py:458
  41.2 32.0 %copy-start.3 = (bf16[16,576]{1,0:T(8,128)(2,1)S(1)}, bf16[16,576]{1,0:T(8,128)(2,1)}, u32[]{:S(2)}) copy-start(bf16[16,576]{1,0:T(8,128)(2,1)} %conv_ref.1) | copy-start | bytes 55300
  41.2 32.0 %copy-start.4 = (bf16[64,64]{1,0:T(8,128)(2,1)S(1)}, bf16[64,64]{1,0:T(8,128)(2,1)}, u32[]{:S(2)}) copy-start(bf16[64,64]{1,0:T(8,128)(2,1)} %down_ref.1) | copy-start | bytes 24580
  41.2 32.0 %copy-start.10 = (f32[16]{0:T(128)S(1)}, f32[16]{0:T(128)}, u32[]{:S(2)}) copy-start(f32[16]{0:T(128)} %param.12) | copy-start | bytes 196
  47.0 38.3 %copy-start.1 = (bf16[8,16,4096]{2,1,0:T(8,128)(2,1)S(1)}, bf16[8,16,4096]{2,1,0:T(8,128)(2,1)}, u32[]{:S(2)}) copy-start(bf16[8,16,4096]{2,1,0:T(8,128)(2,1)} %refs_0_.1) | copy-start | bytes 3145732
  73.7 4.6 %collective-permute-start.3 = (bf16[192,384]{1,0:T(8,128)(2,1)S(1)}, bf16[192,384]{1,0:T(8,128)(2,1)S(1)}, u32[]{:S(2)}, u32[]{:S(2)}) collective-permute-start(bf16[192,384]{1,0:T(8,128)(2,1)S(1)} %get-tuple-element.36), channel_id=1, source_target_pairs={{0,1},{1,0},{2,3},{3,2},{4,5},{5,4},{6,7},{7,6},{8,9},{9,8},{10,11... | collective-permute-start | bytes 442376 | tf_op jit(solution)/shard_map/ppermute | solution.py:458
  76.6 5.4 %collective-permute-start.4 = (bf16[192,384]{1,0:T(8,128)(2,1)S(1)}, bf16[192,384]{1,0:T(8,128)(2,1)S(1)}, u32[]{:S(2)}, u32[]{:S(2)}) collective-permute-start(bf16[192,384]{1,0:T(8,128)(2,1)S(1)} %get-tuple-element.37), channel_id=1, source_target_pairs={{0,2},{1,3},{2,0},{3,1},{4,6},{5,7},{6,4},{7,5},{8,10},{9,11},{10,... | collective-permute-start | bytes 442376 | tf_op jit(solution)/shard_map/ppermute | solution.py:458
  76.6 8.7 %collective-permute-start.5 = (bf16[192,384]{1,0:T(8,128)(2,1)S(1)}, bf16[192,384]{1,0:T(8,128)(2,1)S(1)}, u32[]{:S(2)}, u32[]{:S(2)}) collective-permute-start(bf16[192,384]{1,0:T(8,128)(2,1)S(1)} %get-tuple-element.38), channel_id=1, source_target_pairs={{0,3},{1,2},{2,1},{3,0},{4,7},{5,6},{6,5},{7,4},{8,11},{9,10},{10,... | collective-permute-start | bytes 442376 | tf_op jit(solution)/shard_map/ppermute | solution.py:458
  93.7 2.4 %collective-permute-start.6 = (bf16[64,1024]{1,0:T(8,128)(2,1)S(1)}, bf16[64,1024]{1,0:T(8,128)(2,1)S(1)}, u32[]{:S(2)}, u32[]{:S(2)}) collective-permute-start(bf16[64,1024]{1,0:T(8,128)(2,1)S(1)} %get-tuple-element.40), channel_id=1, source_target_pairs={{0,1},{1,0},{2,3},{3,2},{4,5},{5,4},{6,7},{7,6},{8,9},{9,8},{10,11... | collective-permute-start | bytes 393224 | tf_op jit(solution)/shard_map/ppermute | solution.py:458
  94.2 4.8 %collective-permute-start.7 = (bf16[64,1024]{1,0:T(8,128)(2,1)S(1)}, bf16[64,1024]{1,0:T(8,128)(2,1)S(1)}, u32[]{:S(2)}, u32[]{:S(2)}) collective-permute-start(bf16[64,1024]{1,0:T(8,128)(2,1)S(1)} %get-tuple-element.41), channel_id=1, source_target_pairs={{0,2},{1,3},{2,0},{3,1},{4,6},{5,7},{6,4},{7,5},{8,10},{9,11},{10,... | collective-permute-start | bytes 393224 | tf_op jit(solution)/shard_map/ppermute | solution.py:458
  94.2 8.0 %collective-permute-start.8 = (bf16[64,1024]{1,0:T(8,128)(2,1)S(1)}, bf16[64,1024]{1,0:T(8,128)(2,1)S(1)}, u32[]{:S(2)}, u32[]{:S(2)}) collective-permute-start(bf16[64,1024]{1,0:T(8,128)(2,1)S(1)} %get-tuple-element.42), channel_id=1, source_target_pairs={{0,3},{1,2},{2,1},{3,0},{4,7},{5,6},{6,5},{7,4},{8,11},{9,10},{10,... | collective-permute-start | bytes 393224 | tf_op jit(solution)/shard_map/ppermute | solution.py:458

commit v3 on v2

--- a/solution.py
+++ b/solution.py
@@ -62,30 +62,26 @@
 
 
 def send_body(me_ref, feat_ref, cot_ref, el_ref, et_ref, cl_ref, ct_ref, slot_ref, out_ref, *peer_refs):
-    step = pl.program_id(0)
     for d in range(1, 4):
-
-        @pl.when(step == d)
-        def _():
-            peer = me_ref[0] ^ d
-            peer_refs[d - 1][...] = feat_ref[pl.ds(pl.multiple_of(peer * 32, 32), 32), :]
+        peer = me_ref[0] ^ d
+        peer_refs[d - 1][...] = feat_ref[pl.ds(pl.multiple_of(peer * 32, 32), 32), :]
 
     cot = cot_ref[...]
     stack = jnp.concatenate([cot[:, q * 256 : q * 256 + 256] for q in range(16)], axis=0)
-    row = down_col(128, step * 128)
+    row = down_col(512)
     k, g, a, qr, hf = row >> 5, (row >> 3) & 3, (row >> 2) & 1, (row >> 1) & 1, row & 1
     source = (qr << 8) | (g << 6) | (hf << 5) | (a << 4) | k
     out_ref[:, 0:256] = mm(ones_where(lane_row(512) == source), stack).astype(BF)
 
     first = feat_ref[:, 0:128]
     last = feat_ref[:, 3968:4096]
-    p = down_col(16, step * 16)
+    p = down_col(64)
     lane = lane_row(128)
     rim_n = mm_nt(ones_where(lane == 63 - p), first)
     rim_s = mm_nt(ones_where(lane == 64 + p), last)
-    pc = down_col(32)
-    pos = (pc & 15) + step * 16
-    want = jnp.where(pc < 16, pos * 64, (63 - pos) * 64 + 63)
+    pc = down_col(128)
+    pos = pc & 63
+    want = jnp.where(pc < 64, pos * 64, (63 - pos) * 64 + 63)
     rim_we = mm_nt(ones_where(lane_row(4096) == want), feat_ref[...])
     cr = down_col(16)
     at_first = jnp.where(cr == 0, 0, jnp.where(cr == 3, 63, -1))
@@ -122,25 +118,26 @@
         line = jnp.where(field == 14, node[part : part + 1, :], 0.0)
         line = jnp.where(field == 15, pixel[part : part + 1, :], line)
         small = small + jnp.where(sub == part + 1, line, 0.0)
-    parts = [rim_n, rim_we[0:16], rim_s, rim_we[16:32], by_chan, small, jnp.zeros((32, 128), F32)]
+    parts = [rim_n, rim_we[0:64], rim_s, rim_we[64:128], by_chan, small, jnp.zeros((96, 128), F32)]
     stack = jnp.concatenate([x.astype(BF) for x in parts], axis=0)
-    r, node = tc & 7, tc >> 3
-    source = jnp.where(r < 5, r * 16 + node, jnp.where(r == 5, 80, jnp.where(r == 6, 81 + step, -1)))
-    out_ref[:, 256:384] = mm(ones_where(lane == source), stack).astype(BF)
+    r, node = row & 7, row >> 3
+    source = jnp.where(r == 4, 256 + (node & 15), jnp.where(r == 5, 272, jnp.where(r == 6, 273 + (node >> 4), -1)))
+    source = jnp.where(r < 4, r * 64 + node, source)
+    out_ref[:, 256:384] = mm(ones_where(lane_row(384) == source), stack).astype(BF)
 
 
 def pick_body(msg_ref, out_ref, slot_ref):
-    step = pl.program_id(0)
     cot = msg_ref[:, 0:256]
     misc = msg_ref[:, 256:384]
     col = lane_row(512)
     lane = lane_row(128)
-    sub = down_col(128)
-    base = ((sub + step * 128) >> 3) << 3
+    sub = down_col(512)
+    near = down_col(128)
+    base = (sub >> 3) << 3
     both = mm(ones_where((col == base + 5) | (col == base + 6)), misc)
-    fields = mm(keep((lane & 7) == (sub & 7), both), ones_where((sub >> 3) == lane))
+    fields = mm(keep((lane & 7) == (sub & 7), both), ones_where((near >> 3) == lane))
     flip = fields.T
-    slot_ref[...] = jnp.broadcast_to(flip[12:13, :] * 8.0 + flip[13:14, :], (8, 128))
+    slot_ref[...] = jnp.broadcast_to(flip[12:13, :] * 8.0 + flip[13:14, :], (8, 512))
     num = fields.astype(jnp.int32)
 
     def field(f):
@@ -154,10 +151,10 @@
     for hf in range(2):
         got = mm(ones_where(col == slot_row + hf), cot)
         out_ref[:, hf * 128 : hf * 128 + 128] = mm(keep(mine, got), fold).astype(BF)
-    total = jnp.zeros((128, 128), F32)
+    total = jnp.zeros((512, 128), F32)
     for k in range(4):
         got = mm(ones_where(col == field(k) * 8 + field(4 + k)), misc)
-        place = ones_where(lane == k * 16 + (sub & 15))
+        place = ones_where(lane == k * 16 + (near & 15))
         total = total + mm(keep((lane >> 4) == field(8 + k), got), place)
     got = mm(ones_where(col == field(14) * 8 + 4), misc)
     total = total + mm(keep(lane == field(15), got), ones_where(jnp.broadcast_to(lane == 64, (128, 128))))
@@ -371,17 +368,12 @@
 
 def spread_body(me_ref, *refs):
     in_refs, out_ref, msg_ref = refs[0:4], refs[4], refs[5]
-    step = pl.program_id(0)
-
-    @pl.when(step == 0)
-    def _():
-        for d in range(4):
-            msg_ref[me_ref[0] ^ d] = in_refs[d][...]
-
+    for d in range(4):
+        msg_ref[me_ref[0] ^ d] = in_refs[d][...]
     stack = jnp.concatenate(
         [msg_ref[c, 0:32, g * 256 : g * 256 + 256] for g in range(4) for c in range(4)], axis=0
     )
-    row = down_col(128, step * 128)
+    row = down_col(512)
     source = (((row >> 3) & 3) << 7) | (((row >> 1) & 3) << 5) | ((row & 1) << 4) | (row >> 5)
     out_ref[:, 0:256] = mm(ones_where(lane_row(512) == source), stack).astype(BF)
     total = jnp.zeros((16, 1024), F32)
@@ -397,15 +389,14 @@
 
 
 def place_body(msg_ref, slot_ref, out_ref):
-    step = pl.program_id(0)
     quarter = msg_ref[:, 0:256]
     slot = slot_ref[0:1, :].astype(jnp.int32)
-    row = down_col(128, step * 128)
+    row = down_col(512)
     lane = lane_row(256)
     half = row & 1
     li = down_col(256)
     to = (((li >> 5) & 3) << 6) | (li & 31)
-    total = jnp.zeros((128, 256), F32)
+    total = jnp.zeros((512, 256), F32)
     for qc in range(2):
         got = mm(ones_where(slot == ((row >> 1) << 1) + qc), quarter)
         total = total + mm(keep((lane >> 7) == half, got), ones_where(lane == to + qc * 32))
@@ -421,36 +412,34 @@
 
 
 def finish_body(msg_ref, coarse_ref, conv_ref, down_ref, bias_ref):
-    step = pl.program_id(0)
-    row = down_col(128, step * 128)
+    row = down_col(512)
     col = lane_row(512)
     qr, g, hf, a, k = row >> 8, (row >> 6) & 3, (row >> 5) & 1, (row >> 4) & 1, row & 15
     source = (k << 5) | (g << 3) | (a << 2) | (qr << 1) | hf
     got = mm(ones_where(col == source), msg_ref[:, 0:256]).astype(BF)
-    coarse_ref[...] = jnp.concatenate([got[q * 32 : q * 32 + 32, :] for q in range(4)], axis=1)
-
-    @pl.when(step == 0)
-    def _():
-        row = down_col(256)
-        got = mm(ones_where(col == ((row & 63) << 3) + (row >> 6)), msg_ref[:, 256:384])
-        near = down_col(1024)
-        to = jnp.where((near & 255) < 144, (near >> 8) * 144 + (near & 255), -1)
-        place = ones_where(lane_row(576) == to)
-        lane = lane_row(128)
-        shift = ones_where(down_col(128) == jnp.where(lane < 64, lane + 16, -1))
-        conv = jnp.zeros((16, 576), F32)
-        down = jnp.zeros((64, 128), F32)
-        for h in range(2):
-            low, high = got[h * 128 : h * 128 + 64, :], got[h * 128 + 64 : h * 128 + 128, :]
-            wide = jnp.concatenate(
-                [x[s * 16 : s * 16 + 16, :] for s in range(4) for x in (low, high)], axis=1
-            )
-            conv = conv + mm(wide.astype(BF), place)
-            down = down + mm(high.astype(BF), shift)
-        conv_ref[...] = conv
-        down_ref[...] = down[:, 0:64]
-        bias = got[64:80, 80:81] + got[192:208, 80:81]
-        bias_ref[...] = jnp.sum(jnp.where(lane_row(16) == down_col(16), bias, 0.0), axis=0, keepdims=True)
+    for q in range(16):
+        coarse_ref[:, q * 256 : q * 256 + 256] = got[q * 32 : q * 32 + 32, :]
+
+    row = down_col(256)
+    got = mm(ones_where(col == ((row & 63) << 3) + (row >> 6)), msg_ref[:, 256:384])
+    near = down_col(1024)
+    to = jnp.where((near & 255) < 144, (near >> 8) * 144 + (near & 255), -1)
+    place = ones_where(lane_row(576) == to)
+    lane = lane_row(128)
+    shift = ones_where(down_col(128) == jnp.where(lane < 64, lane + 16, -1))
+    conv = jnp.zeros((16, 576), F32)
+    down = jnp.zeros((64, 128), F32)
+    for h in range(2):
+        low, high = got[h * 128 : h * 128 + 64, :], got[h * 128 + 64 : h * 128 + 128, :]
+        wide = jnp.concatenate(
+            [x[s * 16 : s * 16 + 16, :] for s in range(4) for x in (low, high)], axis=1
+        )
+        conv = conv + mm(wide.astype(BF), place)
+        down = down + mm(high.astype(BF), shift)
+    conv_ref[...] = conv
+    down_ref[...] = down[:, 0:64]
+    bias = got[64:80, 80:81] + got[192:208, 80:81]
+    bias_ref[...] = jnp.sum(jnp.where(lane_row(16) == down_col(16), bias, 0.0), axis=0, keepdims=True)
 
 
 def to_peers(parts):
@@ -472,7 +461,6 @@
     child_slot,
 ):
     msg_spec = whole(MSG)
-    block = pl.BlockSpec((128, 384), lambda i: (i, 0))
     msg = jax.ShapeDtypeStruct(MSG, BF)
 
     def to_nodes(x):
@@ -484,9 +472,9 @@
     pieces, *tiles = call(
         send_body,
         (msg, peer_rows, peer_rows, peer_rows),
-        (4,),
+        (1,),
         [scalar, whole((128, 4096)), whole((32, 4096))] + [whole((4, 8))] * 4 + [whole((1, 8))],
-        (block,) + (whole((32, 4096)),) * 3,
+        (msg_spec,) + (whole((32, 4096)),) * 3,
         flops=10**9,
         moved=2 * 10**6,
     )(
@@ -504,9 +492,9 @@
     picked, slots = call(
         pick_body,
         (msg, jax.ShapeDtypeStruct((8, 512), F32)),
-        (4,),
+        (1,),
         [msg_spec],
-        (block, pl.BlockSpec((8, 128), lambda i: (0, i))),
+        (msg_spec, whole((8, 512))),
         flops=10**9,
         moved=10**6,
     )(pieces)
@@ -554,15 +542,15 @@
     out = call(
         spread_body,
         msg,
-        (4,),
+        (1,),
         [scalar] + [whole((64, 1024))] * 4,
-        block,
+        msg_spec,
         (pltpu.VMEM((4, 64, 1024), BF),),
         flops=4 * 10**8,
         moved=10**6,
     )(me, *local)
     out = to_nodes(out)
-    out = call(place_body, msg, (4,), [msg_spec, whole((8, 512))], block, flops=5 * 10**8, moved=10**6)(
+    out = call(place_body, msg, (1,), [msg_spec, whole((8, 512))], msg_spec, flops=5 * 10**8, moved=10**6)(
         out, slots
     )
     out = to_nodes(out)
@@ -574,10 +562,10 @@
             jax.ShapeDtypeStruct((64, 64), F32),
             jax.ShapeDtypeStruct((1, 16), F32),
         ),
-        (4,),
+        (1,),
         [msg_spec],
         (
-            pl.BlockSpec((32, 1024), lambda i: (0, i)),
+            whole((32, 4096)),
             whole((16, 576)),
             whole((64, 64)),
             whole((1, 16)),

time: 150 us -> 142 us (0.947)
  Pallas kernels: 23.9 us -> 16 us
    pallas_call x4, Pallas kernels: 12.5 us -> 5.73 us  [the longest x1 2.48 us: on_device(): call(pick_body, (msg, jax.ShapeDtypeStruct((8, 512), F32)), (1,), [msg_sp...]
where the time goes in v3:
time: 142 us; the launch traced here: 140 us
  blocking collectives  66.9 us (47%)
  waiting for transfers between devices  28.9 us (20%)
  starting transfers between devices  24.8 us (17%)
  Pallas kernels  16 us (11%)
  local copies, waits for them, and re-layouts  2.88 us (2%)
    all_to_all x3, blocking collectives, to_nodes(): lax.all_to_all(x.reshape(64, 8, 384), 'tile', 0, 0, tiled=True).reshape(MSG)  66.9 us
    ppermute x9, waiting for transfers between devices, to_peers(): lax.ppermute(parts[d], 'chan', [(i, i ^ d) for i in range(4)])  28.9 us
    all_to_all x1, starting transfers between devices, to_nodes(): lax.all_to_all(x.reshape(64, 8, 384), 'tile', 0, 0, tiled=True).reshape(MSG)  15.1 us
    ppermute x9, starting transfers between devices, to_peers(): lax.ppermute(parts[d], 'chan', [(i, i ^ d) for i in range(4)])  9.63 us
    pallas_call x1, Pallas kernels, on_device(): pl.pallas_call(level_body, out_shape=(jax.ShapeDtypeStruct((64, 1024), BF...  8.39 us
    unnamed x22, local copies, waits for them, and re-layouts  2.88 us
  transfers between devices with their start and end apart: 10, of which 6 were waited for; matrix products, arithmetic and copies ran while one was open for 0% of the time, Pallas kernels for 0%

profile of v3, /device:TPU:1, one launch (start us, length us, event | category | flops | bytes accessed | tf_op | source)
XLA Modules:
  0.0 140.2 jit_solution(9523199400175741711)
XLA Ops:
  0.7 0.6 copy-done.8
  1.4 1.2 copy-done
  2.6 0.9 copy-done.2
  3.5 2.0 %shard_map.129 = (bf16[512,384]{1,0:T(8,128)(2,1)}, bf16[32,4096]{1,0:T(8,128)(2,1)S(1)}, bf16[32,4096]{1,0:T(8,128)(2,1)S(1)}, bf16[32,4096]{1,0:T(8,128)(2,1)S(1)}) custom-call(s32[1]{0:T(128)} %bitcast.me_ref, bf16[128,4096]{1,0:T(8,128)(2,1)S(1)} %bitcast.29, bf16[32,4096]{1,0:T(8,128)(2,1)S(1)} %bitcast.30, s32[4,8]{1,0:T(4,128)S(1)} %bitcast.34, ...), custom_call_target="tpu_custom_call" | custom-call | flops 1000000000 | bytes 2000000 | tf_op jit(solution)/shard_map/pallas_call | solution.py:472
  5.5 15.1 %all-to-all-start = ((bf16[64,8,384]{2,1,0:T(8,128)(2,1)}), bf16[64,8,384]{2,1,0:T(8,128)(2,1)S(1)}, u32[]{:S(2)}, u32[]{:S(2)}) async-start(bf16[64,8,384]{2,1,0:T(8,128)(2,1)} %bitcast.8), calls=%async_computation | async-start | bytes 786432 | tf_op jit(solution)/shard_map/all_to_all | solution.py:467
  20.6 1.0 collective-permute-start
  22.1 1.3 collective-permute-start.2
  23.4 9.7 %collective-permute-done.1 = bf16[32,4096]{1,0:T(8,128)(2,1)S(1)} collective-permute-done((bf16[32,4096]{1,0:T(8,128)(2,1)S(1)}, bf16[32,4096]{1,0:T(8,128)(2,1)S(1)}, u32[]{:S(2)}, u32[]{:S(2)}) %collective-permute-start.1) | collective-permute-done | bytes 262176 | tf_op jit(solution)/shard_map/ppermute | solution.py:447
  33.1 6.1 %collective-permute-done.2 = bf16[32,4096]{1,0:T(8,128)(2,1)S(1)} collective-permute-done((bf16[32,4096]{1,0:T(8,128)(2,1)S(1)}, bf16[32,4096]{1,0:T(8,128)(2,1)S(1)}, u32[]{:S(2)}, u32[]{:S(2)}) %collective-permute-start.2) | collective-permute-done | bytes 262176 | tf_op jit(solution)/shard_map/ppermute | solution.py:447
  39.2 2.5 %shard_map.130 = (bf16[512,384]{1,0:T(8,128)(2,1)S(1)}, f32[8,512]{1,0:T(8,128)S(1)}) custom-call(bf16[512,384]{1,0:T(8,128)(2,1)S(1)} %bitcast.22), custom_call_target="tpu_custom_call" | custom-call | flops 1000000000 | bytes 1000000 | tf_op jit(solution)/shard_map/pallas_call | solution.py:492
  41.7 26.2 %all_to_all.20 = bf16[64,8,384]{2,1,0:T(8,128)(2,1)S(1)} all-to-all(bf16[64,8,384]{2,1,0:T(8,128)(2,1)S(1)} %bitcast.26), channel_id=1, replica_groups=mesh['tile'=64,'chan'=4] {'tile'}, dimensions={0} | all-to-all | bytes 786432 | tf_op jit(solution)/shard_map/all_to_all | solution.py:467
  68.4 2.9 %collective-permute-start.3 = (bf16[192,384]{1,0:T(8,128)(2,1)S(1)}, bf16[192,384]{1,0:T(8,128)(2,1)S(1)}, u32[]{:S(2)}, u32[]{:S(2)}) collective-permute-start(bf16[192,384]{1,0:T(8,128)(2,1)S(1)} %get-tuple-element.36), channel_id=1, source_target_pairs={{0,1},{1,0},{2,3},{3,2},{4,5},{5,4},{6,7},{7,6},{8,9},{9,8},{10,11... | collective-permute-start | bytes 442376 | tf_op jit(solution)/shard_map/ppermute | solution.py:447
  71.3 1.7 %collective-permute-start.5 = (bf16[192,384]{1,0:T(8,128)(2,1)S(1)}, bf16[192,384]{1,0:T(8,128)(2,1)S(1)}, u32[]{:S(2)}, u32[]{:S(2)}) collective-permute-start(bf16[192,384]{1,0:T(8,128)(2,1)S(1)} %get-tuple-element.38), channel_id=1, source_target_pairs={{0,3},{1,2},{2,1},{3,0},{4,7},{5,6},{6,5},{7,4},{8,11},{9,10},{10,... | collective-permute-start | bytes 442376 | tf_op jit(solution)/shard_map/ppermute | solution.py:447
  73.0 3.7 %collective-permute-done.4.refs_6_ = bf16[192,384]{1,0:T(8,128)(2,1)S(1)} collective-permute-done((bf16[192,384]{1,0:T(8,128)(2,1)S(1)}, bf16[192,384]{1,0:T(8,128)(2,1)S(1)}, u32[]{:S(2)}, u32[]{:S(2)}) %collective-permute-start.4) | collective-permute-done | bytes 147488 | tf_op jit(solution)/shard_map/ppermute | solution.py:447
  76.7 3.3 %collective-permute-done.5.refs_7_ = bf16[192,384]{1,0:T(8,128)(2,1)S(1)} collective-permute-done((bf16[192,384]{1,0:T(8,128)(2,1)S(1)}, bf16[192,384]{1,0:T(8,128)(2,1)S(1)}, u32[]{:S(2)}, u32[]{:S(2)}) %collective-permute-start.5) | collective-permute-done | bytes 147488 | tf_op jit(solution)/shard_map/ppermute | solution.py:447
  80.0 8.4 %shard_map.132 = (bf16[64,1024]{1,0:T(8,128)(2,1)S(1)}, bf16[64,1024]{1,0:T(8,128)(2,1)S(1)}, bf16[64,1024]{1,0:T(8,128)(2,1)S(1)}, bf16[64,1024]{1,0:T(8,128)(2,1)S(1)}) custom-call(s32[1]{0:T(128)} %bitcast.me_ref, bf16[8,16,4096]{2,1,0:T(8,128)(2,1)S(1)} %copy-done.1, bf16[2,16,4096]{2,1,0:T(8,128)(2,1)S(1)} %bitcast.31, ...), custom_call_target="tpu_custom_call" | custom-call | flops 4000000000 | bytes 4000000 | tf_op jit(solution)/shard_map/pallas_call | solution.py:514
  88.7 1.9 %collective-permute-start.8 = (bf16[64,1024]{1,0:T(8,128)(2,1)S(1)}, bf16[64,1024]{1,0:T(8,128)(2,1)S(1)}, u32[]{:S(2)}, u32[]{:S(2)}) collective-permute-start(bf16[64,1024]{1,0:T(8,128)(2,1)S(1)} %get-tuple-element.42), channel_id=1, source_target_pairs={{0,3},{1,2},{2,1},{3,0},{4,7},{5,6},{6,5},{7,4},{8,11},{9,10},{10,... | collective-permute-start | bytes 393224 | tf_op jit(solution)/shard_map/ppermute | solution.py:447
  90.7 2.8 %collective-permute-done.7.refs_2_ = bf16[64,1024]{1,0:T(8,128)(2,1)S(1)} collective-permute-done((bf16[64,1024]{1,0:T(8,128)(2,1)S(1)}, bf16[64,1024]{1,0:T(8,128)(2,1)S(1)}, u32[]{:S(2)}, u32[]{:S(2)}) %collective-permute-start.7) | collective-permute-done | bytes 131104 | tf_op jit(solution)/shard_map/ppermute | solution.py:447
  93.4 3.3 %collective-permute-done.8.refs_3_ = bf16[64,1024]{1,0:T(8,128)(2,1)S(1)} collective-permute-done((bf16[64,1024]{1,0:T(8,128)(2,1)S(1)}, bf16[64,1024]{1,0:T(8,128)(2,1)S(1)}, u32[]{:S(2)}, u32[]{:S(2)}) %collective-permute-start.8) | collective-permute-done | bytes 131104 | tf_op jit(solution)/shard_map/ppermute | solution.py:447
  96.7 0.5 shard_map.133
  97.2 20.4 %all_to_all.21 = bf16[64,8,384]{2,1,0:T(8,128)(2,1)S(1)} all-to-all(bf16[64,8,384]{2,1,0:T(8,128)(2,1)S(1)} %bitcast.24), channel_id=1, replica_groups=mesh['tile'=64,'chan'=4] {'tile'}, dimensions={0} | all-to-all | bytes 786432 | tf_op jit(solution)/shard_map/all_to_all | solution.py:467
  117.6 0.8 shard_map.134
  118.4 20.3 %all_to_all.22 = bf16[64,8,384]{2,1,0:T(8,128)(2,1)S(1)} all-to-all(bf16[64,8,384]{2,1,0:T(8,128)(2,1)S(1)} %bitcast.28), channel_id=1, replica_groups=mesh['tile'=64,'chan'=4] {'tile'}, dimensions={0} | all-to-all | bytes 786432 | tf_op jit(solution)/shard_map/all_to_all | solution.py:467
  138.7 1.4 %shard_map.135 = (bf16[32,4096]{1,0:T(8,128)(2,1)}, f32[16,576]{1,0:T(8,128)}, f32[64,64]{1,0:T(8,128)}, f32[1,16]{1,0:T(1,128)}) custom-call(bf16[512,384]{1,0:T(8,128)(2,1)S(1)} %bitcast.25), custom_call_target="tpu_custom_call" | custom-call | flops 400000000 | bytes 1000000 | tf_op jit(solution)/shard_map/pallas_call | solution.py:557
  (28 shorter events, 1.4 us)
Async XLA Ops:
  0.6 0.7 copy-start.8
  0.6 0.7 copy-start.7
  0.7 0.7 copy-start.6
  0.7 0.7 copy-start.5
  0.7 0.7 copy-start.9
  1.4 1.2 copy-start
  2.6 0.9 copy-start.2
  5.5 33.7 %all-to-all-start = ((bf16[64,8,384]{2,1,0:T(8,128)(2,1)}), bf16[64,8,384]{2,1,0:T(8,128)(2,1)S(1)}, u32[]{:S(2)}, u32[]{:S(2)}) async-start(bf16[64,8,384]{2,1,0:T(8,128)(2,1)} %bitcast.8), calls=%async_computation | async-start | bytes 786432 | tf_op jit(solution)/shard_map/all_to_all | solution.py:467
  20.6 2.8 %collective-permute-start = (bf16[32,4096]{1,0:T(8,128)(2,1)S(1)}, bf16[32,4096]{1,0:T(8,128)(2,1)S(1)}, u32[]{:S(2)}, u32[]{:S(2)}) collective-permute-start(bf16[32,4096]{1,0:T(8,128)(2,1)S(1)} %get-tuple-element.27), channel_id=1, source_target_pairs={{0,1},{1,0},{2,3},{3,2},{4,5},{5,4},{6,7},{7,6},{8,9},{9,8},{10,11... | collective-permute-start | bytes 786440 | tf_op jit(solution)/shard_map/ppermute | solution.py:447
  21.7 11.4 %collective-permute-start.1 = (bf16[32,4096]{1,0:T(8,128)(2,1)S(1)}, bf16[32,4096]{1,0:T(8,128)(2,1)S(1)}, u32[]{:S(2)}, u32[]{:S(2)}) collective-permute-start(bf16[32,4096]{1,0:T(8,128)(2,1)S(1)} %get-tuple-element.28), channel_id=1, source_target_pairs={{0,2},{1,3},{2,0},{3,1},{4,6},{5,7},{6,4},{7,5},{8,10},{9,11},{10,... | collective-permute-start | bytes 786440 | tf_op jit(solution)/shard_map/ppermute | solution.py:447
  22.1 17.1 %collective-permute-start.2 = (bf16[32,4096]{1,0:T(8,128)(2,1)S(1)}, bf16[32,4096]{1,0:T(8,128)(2,1)S(1)}, u32[]{:S(2)}, u32[]{:S(2)}) collective-permute-start(bf16[32,4096]{1,0:T(8,128)(2,1)S(1)} %get-tuple-element.29), channel_id=1, source_target_pairs={{0,3},{1,2},{2,1},{3,0},{4,7},{5,6},{6,5},{7,4},{8,11},{9,10},{10,... | collective-permute-start | bytes 786440 | tf_op jit(solution)/shard_map/ppermute | solution.py:447
  39.2 28.7 %copy-start.3 = (bf16[16,576]{1,0:T(8,128)(2,1)S(1)}, bf16[16,576]{1,0:T(8,128)(2,1)}, u32[]{:S(2)}) copy-start(bf16[16,576]{1,0:T(8,128)(2,1)} %conv_ref.1) | copy-start | bytes 55300
  39.2 28.7 %copy-start.4 = (bf16[64,64]{1,0:T(8,128)(2,1)S(1)}, bf16[64,64]{1,0:T(8,128)(2,1)}, u32[]{:S(2)}) copy-start(bf16[64,64]{1,0:T(8,128)(2,1)} %down_ref.1) | copy-start | bytes 24580
  39.2 28.7 %copy-start.10 = (f32[16]{0:T(128)S(1)}, f32[16]{0:T(128)}, u32[]{:S(2)}) copy-start(f32[16]{0:T(128)} %param.12) | copy-start | bytes 196
  41.7 38.3 %copy-start.1 = (bf16[8,16,4096]{2,1,0:T(8,128)(2,1)S(1)}, bf16[8,16,4096]{2,1,0:T(8,128)(2,1)}, u32[]{:S(2)}) copy-start(bf16[8,16,4096]{2,1,0:T(8,128)(2,1)} %refs_0_.1) | copy-start | bytes 3145732
  68.4 4.6 %collective-permute-start.3 = (bf16[192,384]{1,0:T(8,128)(2,1)S(1)}, bf16[192,384]{1,0:T(8,128)(2,1)S(1)}, u32[]{:S(2)}, u32[]{:S(2)}) collective-permute-start(bf16[192,384]{1,0:T(8,128)(2,1)S(1)} %get-tuple-element.36), channel_id=1, source_target_pairs={{0,1},{1,0},{2,3},{3,2},{4,5},{5,4},{6,7},{7,6},{8,9},{9,8},{10,11... | collective-permute-start | bytes 442376 | tf_op jit(solution)/shard_map/ppermute | solution.py:447
  71.3 5.4 %collective-permute-start.4 = (bf16[192,384]{1,0:T(8,128)(2,1)S(1)}, bf16[192,384]{1,0:T(8,128)(2,1)S(1)}, u32[]{:S(2)}, u32[]{:S(2)}) collective-permute-start(bf16[192,384]{1,0:T(8,128)(2,1)S(1)} %get-tuple-element.37), channel_id=1, source_target_pairs={{0,2},{1,3},{2,0},{3,1},{4,6},{5,7},{6,4},{7,5},{8,10},{9,11},{10,... | collective-permute-start | bytes 442376 | tf_op jit(solution)/shard_map/ppermute | solution.py:447
  71.3 8.7 %collective-permute-start.5 = (bf16[192,384]{1,0:T(8,128)(2,1)S(1)}, bf16[192,384]{1,0:T(8,128)(2,1)S(1)}, u32[]{:S(2)}, u32[]{:S(2)}) collective-permute-start(bf16[192,384]{1,0:T(8,128)(2,1)S(1)} %get-tuple-element.38), channel_id=1, source_target_pairs={{0,3},{1,2},{2,1},{3,0},{4,7},{5,6},{6,5},{7,4},{8,11},{9,10},{10,... | collective-permute-start | bytes 442376 | tf_op jit(solution)/shard_map/ppermute | solution.py:447
  88.4 2.2 %collective-permute-start.6 = (bf16[64,1024]{1,0:T(8,128)(2,1)S(1)}, bf16[64,1024]{1,0:T(8,128)(2,1)S(1)}, u32[]{:S(2)}, u32[]{:S(2)}) collective-permute-start(bf16[64,1024]{1,0:T(8,128)(2,1)S(1)} %get-tuple-element.40), channel_id=1, source_target_pairs={{0,1},{1,0},{2,3},{3,2},{4,5},{5,4},{6,7},{7,6},{8,9},{9,8},{10,11... | collective-permute-start | bytes 393224 | tf_op jit(solution)/shard_map/ppermute | solution.py:447
  88.7 4.8 %collective-permute-start.7 = (bf16[64,1024]{1,0:T(8,128)(2,1)S(1)}, bf16[64,1024]{1,0:T(8,128)(2,1)S(1)}, u32[]{:S(2)}, u32[]{:S(2)}) collective-permute-start(bf16[64,1024]{1,0:T(8,128)(2,1)S(1)} %get-tuple-element.41), channel_id=1, source_target_pairs={{0,2},{1,3},{2,0},{3,1},{4,6},{5,7},{6,4},{7,5},{8,10},{9,11},{10,... | collective-permute-start | bytes 393224 | tf_op jit(solution)/shard_map/ppermute | solution.py:447
  88.7 8.0 %collective-permute-start.8 = (bf16[64,1024]{1,0:T(8,128)(2,1)S(1)}, bf16[64,1024]{1,0:T(8,128)(2,1)S(1)}, u32[]{:S(2)}, u32[]{:S(2)}) collective-permute-start(bf16[64,1024]{1,0:T(8,128)(2,1)S(1)} %get-tuple-element.42), channel_id=1, source_target_pairs={{0,3},{1,2},{2,1},{3,0},{4,7},{5,6},{6,5},{7,4},{8,11},{9,10},{10,... | collective-permute-start | bytes 393224 | tf_op jit(solution)/shard_map/ppermute | solution.py:447

commit v4 on v3

--- a/solution.py
+++ b/solution.py
@@ -61,7 +61,40 @@
     return pl.BlockSpec(shape, lambda *i: (0,) * len(shape))
 
 
-def send_body(me_ref, feat_ref, cot_ref, el_ref, et_ref, cl_ref, ct_ref, slot_ref, out_ref, *peer_refs):
+def pack_weights(conv_ref, bias_ref, down_ref, raw_ref):
+    zero = jnp.zeros((64, 64), BF)
+    lane = lane_row(128)
+    bias = jnp.where(lane_row(16) == down_col(16), bias_ref[...], 0.0)
+    bias = jnp.sum(bias, axis=1, keepdims=True)
+    b0 = bias.astype(BF).astype(F32)
+    b1 = (bias - b0).astype(BF).astype(F32)
+    b2 = (bias - b0) - b1
+    bias = jnp.where(lane == 0, b0, jnp.where(lane == 1, b1, jnp.where(lane == 2, b2, 0.0))).astype(BF)
+    raw_ref[:, 0:128] = jnp.concatenate([down_ref[...], zero], axis=1)
+    raw_ref[0:16, 128:384] = conv_ref[:, 0:256]
+    raw_ref[16:32, 128:384] = conv_ref[:, 256:512]
+    raw_ref[32:48, 128:256] = jnp.concatenate([conv_ref[:, 512:576], zero[0:16]], axis=1)
+    raw_ref[32:48, 256:384] = bias
+    raw_ref[48:64, 128:384] = jnp.zeros((16, 256), BF)
+
+
+def send_body(
+    me_ref,
+    feat_ref,
+    cot_ref,
+    el_ref,
+    et_ref,
+    cl_ref,
+    ct_ref,
+    slot_ref,
+    conv_ref,
+    bias_ref,
+    down_ref,
+    out_ref,
+    raw_ref,
+    *peer_refs,
+):
+    pack_weights(conv_ref, bias_ref, down_ref, raw_ref)
     for d in range(1, 4):
         peer = me_ref[0] ^ d
         peer_refs[d - 1][...] = feat_ref[pl.ds(pl.multiple_of(peer * 32, 32), 32), :]
@@ -161,37 +194,28 @@
     out_ref[:, 256:384] = total.astype(BF)
 
 
-def regroup_body(me_ref, msg_ref, conv_ref, bias_ref, down_ref, *out_refs):
+def regroup_body(me_ref, msg_ref, *out_refs):
     row = down_col(128)
     col = lane_row(512)
+    lane = lane_row(128)
     pair, g, k, p = row >> 6, (row >> 4) & 3, row & 15, row & 63
-    zero = jnp.zeros((64, 64), BF)
-    lane = lane_row(128)
-    bias = jnp.where(lane_row(16) == down_col(16), bias_ref[...], 0.0)
-    bias = jnp.sum(bias, axis=1, keepdims=True)
-    b0 = bias.astype(BF).astype(F32)
-    b1 = (bias - b0).astype(BF).astype(F32)
-    b2 = (bias - b0) - b1
-    bias = jnp.where(lane == 0, b0, jnp.where(lane == 1, b1, jnp.where(lane == 2, b2, 0.0))).astype(BF)
     for d in range(4):
         out_ref = out_refs[d]
         tile = ((me_ref[0] ^ d) << 1) | pair
-        out_ref[0:128, 0:256] = mm(
-            ones_where(col == ((k << 5) | (g << 3) | tile)), msg_ref[:, 0:256]
-        ).astype(BF)
-        out_ref[0:128, 256:384] = mm(ones_where(col == ((p << 3) | tile)), msg_ref[:, 256:384]).astype(BF)
-        out_ref[128:192, 0:128] = jnp.concatenate([down_ref[...], zero], axis=1)
-        out_ref[128:144, 128:384] = conv_ref[:, 0:256]
-        out_ref[144:160, 128:384] = conv_ref[:, 256:512]
-        out_ref[160:176, 128:256] = jnp.concatenate([conv_ref[:, 512:576], zero[0:16]], axis=1)
-        out_ref[160:176, 256:384] = bias
-        out_ref[176:192, 128:384] = jnp.zeros((16, 256), BF)
+        out_ref[:, 0:256] = mm(ones_where(col == ((k << 5) | (g << 3) | tile)), msg_ref[:, 0:256]).astype(BF)
+        got = mm(ones_where(col == ((p << 3) | tile)), msg_ref[:, 256:384])
+        rims = jnp.where(lane < 64, got[0:64], pltpu.roll(got[64:128], 64, axis=1))
+        pixels = jnp.zeros((16, 128), F32)
+        for q in range(8):
+            pixels = jnp.where(lane == q, got[q * 16 : q * 16 + 16, 64:65], pixels)
+        rest = jnp.zeros((48, 128), F32)
+        out_ref[:, 256:384] = jnp.concatenate([rims, pixels, rest], axis=0).astype(BF)
 
 
 def lay_weights(raw_ref, w_ref, down_ref, down_t_ref, bias_ref):
     raw = jnp.concatenate(
         [
-            jnp.concatenate([raw_ref[c, 128 + q * 16 : 144 + q * 16, 128 : 128 + n] for c in range(4)], axis=0)
+            jnp.concatenate([raw_ref[c, q * 16 : q * 16 + 16, 128 : 128 + n] for c in range(4)], axis=0)
             for q, n in ((0, 256), (1, 256), (2, 128))
         ],
         axis=1,
@@ -212,7 +236,7 @@
     down = jnp.zeros((64, 256), F32)
     down_t = jnp.zeros((256, 64), F32)
     for c in range(4):
-        mine = raw_ref[c, 128:192, 0:128]
+        mine = raw_ref[c, 0:64, 0:128]
         l = down_col(128)
         to = jnp.where(l < 64, (l & 3) * 64 + c * 16 + (l >> 2), -1)
         down = down + mm(mine, ones_where(lane_row(256) == to))
@@ -221,149 +245,157 @@
         down_t = down_t + mm_nt(ones_where(down_col(256) == to), mine)
     down_ref[...] = down.astype(BF)
     down_t_ref[...] = down_t.astype(BF)
-    bias = jnp.concatenate([raw_ref[c, 160:176, 256:259].astype(F32) for c in range(4)], axis=0)
+    bias = jnp.concatenate([raw_ref[c, 32:48, 256:259].astype(F32) for c in range(4)], axis=0)
     bias = (bias[:, 0:1] + bias[:, 1:2]) + bias[:, 2:3]
     bias_ref[...] = jnp.broadcast_to(jnp.concatenate([bias] * 4, axis=0), (256, 128))
 
 
+def ready_body(me_ref, *refs):
+    feat_refs, raw_refs = refs[0:4], refs[4:8]
+    win_ref, w_ref, down_ref, down_t_ref, bias_ref, x_ref, raw_ref = refs[8:]
+    me = me_ref[0]
+    for d in range(4):
+        raw_ref[me ^ d] = raw_refs[d][...]
+        x_ref[me ^ d] = feat_refs[d][...]
+    lay_weights(raw_ref, w_ref, down_ref, down_t_ref, bias_ref)
+    l_in = down_col(512)
+    to = (((l_in >> 6) & 1) << 8) | ((l_in & 1) << 7) | ((l_in >> 7) << 5) | ((l_in >> 1) & 31)
+    order = ones_where(lane_row(512) == to)
+    lane = lane_row(1024)
+    v = lane & 31
+    for t in range(2):
+        x = jnp.concatenate([x_ref[c, t * 16 : t * 16 + 16, :] for c in range(4)], axis=0)
+        stack = jnp.concatenate([x[:, q * 512 : q * 512 + 512] for q in range(8)], axis=0)
+        split = mm(stack, order)
+        cols = []
+        for a in range(2):
+            even, odd = [
+                jnp.concatenate(
+                    [split[q * 64 : q * 64 + 64, (a * 2 + b) * 128 : (a * 2 + b) * 128 + 128] for q in range(8)],
+                    axis=1,
+                )
+                for b in range(2)
+            ]
+            cols.append(
+                [
+                    jnp.where(v == 0, 0.0, pltpu.roll(odd, 1, axis=1)),
+                    even,
+                    odd,
+                    jnp.where(v == 31, 0.0, pltpu.roll(even, 1023, axis=1)),
+                ]
+            )
+        for cx in range(4):
+            top = jnp.where(lane < 32, 0.0, pltpu.roll(cols[1][cx], 32, axis=1))
+            low = jnp.where(lane >= 992, 0.0, pltpu.roll(cols[0][cx], 992, axis=1))
+            for ry, w in enumerate((top, cols[0][cx], cols[1][cx], low)):
+                row = (ry * 4 + cx) * 64
+                win_ref[t, row : row + 64, :] = w.astype(BF)
+
+
 def level_body(me_ref, *refs):
-    feat_refs, in_refs, out_refs = refs[0:4], refs[4:8], refs[8:12]
-    x_ref, msg_ref, sum_ref, win_ref, gc_ref, gd_ref, gb_ref, w_ref, down_ref, down_t_ref, bias_ref = refs[12:]
-    step = pl.program_id(0)
+    in_refs, (base_ref, w_ref, down_ref, down_t_ref, bias_ref) = refs[0:4], refs[4:9]
+    out_refs, (msg_ref, sum_ref, win_ref, gc_ref) = refs[9:13], refs[13:]
     me = me_ref[0]
-
-    @pl.when(step == 0)
-    def _():
-        for d in range(4):
-            msg_ref[me ^ d] = in_refs[d][...]
-        lay_weights(msg_ref, w_ref, down_ref, down_t_ref, bias_ref)
-
     for d in range(4):
-        x_ref[me ^ d] = feat_refs[d][0]
-    half = pl.multiple_of(step * 64, 64)
-    x = jnp.concatenate([x_ref[c] for c in range(4)], axis=0)
-    stack = jnp.concatenate([x[:, q * 512 : q * 512 + 512] for q in range(8)], axis=0)
-    l_in = down_col(512)
-    to = (
-        (((l_in >> 6) & 1) << 8)
-        | ((l_in & 1) << 7)
-        | ((l_in >> 7) << 5)
-        | ((l_in >> 1) & 31)
-    )
-    split = mm(stack, ones_where(lane_row(512) == to))
-
-    def plane(a, b):
-        s = (a * 2 + b) * 128
-        return jnp.concatenate([split[q * 64 : q * 64 + 64, s : s + 128] for q in range(8)], axis=1)
-
-    rim = [msg_ref[c, pl.ds(half, 64), 256:384].astype(F32) for c in range(4)]
-    flip = [r.T.astype(BF) for r in rim]
+        msg_ref[me ^ d] = in_refs[d][...]
+    flip = [msg_ref[c, 0:64, 256:384].astype(F32).T.astype(BF) for c in range(4)]
 
     def strip(k):
-        return jnp.concatenate([f[k * 16 : k * 16 + 16, :] for f in flip], axis=0)
-
-    def corner(k):
-        return jnp.concatenate([r[k * 16 : k * 16 + 16, 64:65] for r in rim], axis=0)
-
+        return jnp.concatenate(
+            [f[t * 64 + k * 16 : t * 64 + k * 16 + 16, :] for t in range(2) for f in flip], axis=0
+        )
+
+    pixels = jnp.concatenate([msg_ref[c, 64:80, 256:384] for c in range(4)], axis=0).astype(F32)
     lane = lane_row(1024)
     v = lane & 31
     pos = down_col(64)
-    cols = []
-    for a in range(2):
-        y = ((lane >> 5) << 1) + a
-        west = jnp.where(v == 0, 63 - y, -1)
-        east = jnp.where(v == 31, y, -1)
-        side = mm(strip(1), ones_where(west == pos)) + mm(strip(3), ones_where(east == pos))
-        even, odd = plane(a, 0), plane(a, 1)
-        cols.append(
-            [
-                jnp.where(v == 0, side, pltpu.roll(odd, 1, axis=1)),
-                even,
-                odd,
-                jnp.where(v == 31, side, pltpu.roll(even, 1023, axis=1)),
-            ]
-        )
+    sides = {}
+    for ry in range(4):
+        y = ((lane >> 5) << 1) + (ry - 1)
+        sides[ry, 0] = mm(strip(1), ones_where(jnp.where(v == 0, 63 - y, -1) == pos)).astype(BF)
+        sides[ry, 3] = mm(strip(3), ones_where(jnp.where(v == 31, y, -1) == pos)).astype(BF)
     lane_e = lane_row(512)
     inner = lane_e & 127
     at = ((inner & 31) << 1) + (lane_e >> 7)
     north = jnp.where(inner < 32, at - 1, -1)
     south = jnp.where(inner >= 96, 64 - at, -1)
     ends = mm(strip(0), ones_where(north == pos)) + mm(strip(2), ones_where(south == pos))
-    for spot, k in ((0, 0), (96, 1), (384 + 31, 3), (384 + 127, 2)):
-        ends = jnp.where(lane_e == spot, corner(k), ends)
-    blank = jnp.zeros((64, 896), F32)
-    for cx in range(4):
-        end = ends[:, cx * 128 : cx * 128 + 128]
-        top = jnp.where(lane < 32, jnp.concatenate([end, blank], axis=1), pltpu.roll(cols[1][cx], 32, axis=1))
-        low = jnp.where(lane >= 992, jnp.concatenate([blank, end], axis=1), pltpu.roll(cols[0][cx], 992, axis=1))
-        for ry, w in enumerate((top, cols[0][cx], cols[1][cx], low)):
-            at_row = (ry * 4 + cx) * 64
-            win_ref[at_row : at_row + 64, :] = w.astype(BF)
-
-    pre = mm(w_ref[...], win_ref[...]) + bias_ref[:, 0:1]
-    sig = 1.0 / (1.0 + jnp.exp(-pre))
-    hidden = (pre * sig).astype(BF)
-    quarter = mm(down_ref[...], hidden).astype(BF)
-    for c in range(4):
-        sum_ref[c, pl.ds(pl.multiple_of(step * 16, 16), 16), :] = quarter[c * 16 : c * 16 + 16, :]
-    back = jnp.concatenate(
-        [
-            jnp.concatenate(
-                [msg_ref[c, pl.ds(half + g * 16, 16), 0:256] for c in range(4)], axis=0
+    gd = jnp.zeros((64, 256), F32)
+    gb = jnp.zeros((256, 1), F32)
+    for t in range(2):
+        end = ends[t * 64 : t * 64 + 64, :]
+        for spot, k in ((0, 0), (96, 1), (384 + 31, 3), (384 + 127, 2)):
+            end = jnp.where(lane_e == spot, pixels[:, t * 4 + k : t * 4 + k + 1], end)
+        for ry in range(4):
+            for cx in range(4):
+                row = (ry * 4 + cx) * 64
+                w = base_ref[t, row : row + 64, :]
+                if (ry, cx) in sides:
+                    w = w + sides[ry, cx][t * 64 : t * 64 + 64, :]
+                win_ref[t, row : row + 64, :] = w
+                edge = end[:, cx * 128 : cx * 128 + 128]
+                if ry == 0:
+                    fix = jnp.where(lane_row(128) < 64, edge, 0.0).astype(BF)
+                    win_ref[t, row : row + 64, 0:128] = w[:, 0:128] + fix
+                if ry == 3:
+                    fix = jnp.where(lane_row(128) >= 64, edge, 0.0).astype(BF)
+                    win_ref[t, row : row + 64, 896:1024] = w[:, 896:1024] + fix
+    for t in range(2):
+        pre = mm(w_ref[...], win_ref[t]) + bias_ref[:, 0:1]
+        sig = 1.0 / (1.0 + jnp.exp(-pre))
+        hidden = (pre * sig).astype(BF)
+        quarter = mm(down_ref[...], hidden).astype(BF)
+        for c in range(4):
+            sum_ref[c, t * 16 : t * 16 + 16, :] = quarter[c * 16 : c * 16 + 16, :]
+        back = jnp.concatenate(
+            [
+                jnp.concatenate(
+                    [msg_ref[c, t * 64 + g * 16 : t * 64 + g * 16 + 16, 0:256] for c in range(4)], axis=0
+                )
+                for g in range(4)
+            ],
+            axis=1,
+        )
+        grad_hidden = mm(down_t_ref[...], back)
+        grad_pre = (grad_hidden * (sig * (1.0 + pre * (1.0 - sig)))).astype(BF)
+        gb = gb + jnp.sum(grad_pre.astype(F32), axis=1, keepdims=True)
+        gd = gd + mm_nt(back, hidden)
+        part = mm_nt(win_ref[t], grad_pre)
+        gc_ref[...] = part if t == 0 else gc_ref[...] + part
+    rows = []
+    for dy in range(3):
+        for cx in range(4):
+            r0, r1 = (dy * 4 + cx) * 64, ((dy + 1) * 4 + cx) * 64
+            rows.append(gc_ref[r0 : r0 + 64, 0:128] + gc_ref[r1 : r1 + 64, 128:256])
+    taps = []
+    for dy in range(3):
+        for dx in range(3):
+            taps.append(rows[dy * 4 + dx] + pltpu.roll(rows[dy * 4 + dx + 1], 64, axis=1))
+    taps.append(jnp.zeros((64, 128), F32))
+    conv = jnp.concatenate(taps, axis=0)
+    conv = jnp.concatenate([conv[q * 128 : q * 128 + 128, :].T for q in range(5)], axis=1)[0:64, :]
+    kk = down_col(640)
+    cc = lane_row(1024)
+    i, tap = kk & 63, kk >> 6
+    place = ones_where(cc == jnp.where(tap < 9, ((i >> 4) << 8) + (i & 15) * 9 + tap, -1))
+    conv = [mm(h, place) for h in halves(conv)]
+    kk = down_col(256)
+    i, ab = kk & 63, kk >> 6
+    place = ones_where(cc == ((i >> 4) << 8) + 144 + (i & 15) * 4 + ab)
+    down = [mm(h, place) for h in halves(gd)]
+    gb = gb[0:64, :] + gb[64:128, :] + gb[128:192, :] + gb[192:256, :]
+    bias = [h.astype(F32) for h in halves(gb)]
+    lane16 = lane_row(1024)
+    for part in range(2):
+        for c in range(4):
+            d = jnp.concatenate(
+                [down[part][s * 16 : s * 16 + 16, c * 256 : c * 256 + 256] for s in range(4)], axis=1
             )
-            for g in range(4)
-        ],
-        axis=1,
-    )
-    grad_hidden = mm(down_t_ref[...], back)
-    grad_pre = (grad_hidden * (sig * (1.0 + pre * (1.0 - sig)))).astype(BF)
-
-    @pl.when(step == 0)
-    def _():
-        gc_ref[...] = jnp.zeros_like(gc_ref)
-        gd_ref[...] = jnp.zeros_like(gd_ref)
-        gb_ref[...] = jnp.zeros_like(gb_ref)
-
-    gb_ref[...] += jnp.broadcast_to(jnp.sum(grad_pre.astype(F32), axis=1, keepdims=True), (256, 128))
-    gd_ref[...] += mm_nt(back, hidden)
-    gc_ref[...] += mm_nt(win_ref[...], grad_pre)
-
-    @pl.when(step == 1)
-    def _():
-        rows = []
-        for dy in range(3):
-            for cx in range(4):
-                r0, r1 = (dy * 4 + cx) * 64, ((dy + 1) * 4 + cx) * 64
-                rows.append(gc_ref[r0 : r0 + 64, 0:128] + gc_ref[r1 : r1 + 64, 128:256])
-        taps = []
-        for dy in range(3):
-            for dx in range(3):
-                taps.append(rows[dy * 4 + dx] + pltpu.roll(rows[dy * 4 + dx + 1], 64, axis=1))
-        taps.append(jnp.zeros((64, 128), F32))
-        conv = jnp.concatenate(taps, axis=0)
-        conv = jnp.concatenate([conv[q * 128 : q * 128 + 128, :].T for q in range(5)], axis=1)[0:64, :]
-        kk = down_col(640)
-        cc = lane_row(1024)
-        i, tap = kk & 63, kk >> 6
-        place = ones_where(cc == jnp.where(tap < 9, ((i >> 4) << 8) + (i & 15) * 9 + tap, -1))
-        conv = [mm(h, place) for h in halves(conv)]
-        kk = down_col(256)
-        i, ab = kk & 63, kk >> 6
-        place = ones_where(cc == ((i >> 4) << 8) + 144 + (i & 15) * 4 + ab)
-        down = [mm(h, place) for h in halves(gd_ref[...])]
-        gb = gb_ref[0:64, :] + gb_ref[64:128, :] + gb_ref[128:192, :] + gb_ref[192:256, :]
-        bias = [h.astype(F32)[:, 0:1] for h in halves(gb)]
-        lane16 = lane_row(1024)
-        for part in range(2):
-            for c in range(4):
-                d = jnp.concatenate(
-                    [down[part][s * 16 : s * 16 + 16, c * 256 : c * 256 + 256] for s in range(4)], axis=1
-                )
-                both = conv[part][c * 16 : c * 16 + 16, :] + d
-                both = jnp.where(lane16 == 208, bias[part][c * 16 : c * 16 + 16, :], both)
-                sum_ref[c, 32 + part * 16 : 48 + part * 16, :] = both.astype(BF)
-        for d in range(4):
-            out_refs[d][...] = sum_ref[me ^ d]
+            both = conv[part][c * 16 : c * 16 + 16, :] + d
+            both = jnp.where(lane16 == 208, bias[part][c * 16 : c * 16 + 16, :], both)
+            sum_ref[c, 32 + part * 16 : 48 + part * 16, :] = both.astype(BF)
+    for d in range(4):
+        out_refs[d][...] = sum_ref[me ^ d]
 
 
 def spread_body(me_ref, *refs):
@@ -469,26 +501,37 @@
     me = lax.axis_index("chan").astype(jnp.int32).reshape(1)
     scalar = pl.BlockSpec(memory_space=pltpu.SMEM)
     peer_rows = jax.ShapeDtypeStruct((32, 4096), BF)
-    pieces, *tiles = call(
+    pieces, raw, *tiles = call(
         send_body,
-        (msg, peer_rows, peer_rows, peer_rows),
+        (msg, jax.ShapeDtypeStruct((64, 384), BF), peer_rows, peer_rows, peer_rows),
         (1,),
-        [scalar, whole((128, 4096)), whole((32, 4096))] + [whole((4, 8))] * 4 + [whole((1, 8))],
-        (msg_spec,) + (whole((32, 4096)),) * 3,
+        [scalar, whole((128, 4096)), whole((32, 4096))]
+        + [whole((4, 8))] * 4
+        + [whole((1, 8)), whole((16, 576)), whole((1, 16)), whole((64, 64))],
+        (msg_spec, whole((64, 384))) + (whole((32, 4096)),) * 3,
         flops=10**9,
         moved=2 * 10**6,
     )(
         me,
-        features.reshape(128, 4096),
-        cotangent.reshape(32, 4096),
-        edge_links.T,
-        edge_turns.T,
-        corner_links.T,
-        corner_turns.T,
-        child_slot.reshape(1, 8),
+        *[
+            pltpu.with_memory_space_constraint(x, pltpu.HBM)
+            for x in (
+                features.reshape(128, 4096),
+                cotangent.reshape(32, 4096),
+                edge_links.T,
+                edge_turns.T,
+                corner_links.T,
+                corner_turns.T,
+                child_slot.reshape(1, 8),
+                conv_weight,
+                conv_bias.reshape(1, 16),
+                down_weight,
+            )
+        ],
     )
+    raw = to_peers([raw] * 4)
     tiles = to_peers([None] + list(tiles))[1:]
-    pieces, *tiles = lax.optimization_barrier((to_nodes(pieces), *tiles))
+    pieces, raw, tiles = lax.optimization_barrier((to_nodes(pieces), raw, tiles))
     picked, slots = call(
         pick_body,
         (msg, jax.ShapeDtypeStruct((8, 512), F32)),
@@ -499,45 +542,52 @@
         moved=10**6,
     )(pieces)
     picked = to_nodes(picked)
-    group = jax.ShapeDtypeStruct((192, 384), BF)
+    own = pl.BlockSpec((32, 4096), lambda i, m: (m[0], 0))
+    vmem = pl.BlockSpec(memory_space=pltpu.VMEM)
+    ready = pl.pallas_call(
+        ready_body,
+        out_shape=(
+            jax.ShapeDtypeStruct((2, 1024, 1024), BF),
+            jax.ShapeDtypeStruct((256, 1024), BF),
+            jax.ShapeDtypeStruct((64, 256), BF),
+            jax.ShapeDtypeStruct((256, 64), BF),
+            jax.ShapeDtypeStruct((256, 128), F32),
+        ),
+        grid_spec=pltpu.PrefetchScalarGridSpec(
+            num_scalar_prefetch=1,
+            grid=(1,),
+            in_specs=[own] + [whole((32, 4096))] * 3 + [whole((64, 384))] * 4,
+            out_specs=(vmem,) * 5,
+            scratch_shapes=(pltpu.VMEM((4, 32, 4096), BF), pltpu.VMEM((4, 64, 384), BF)),
+        ),
+        compiler_params=pltpu.CompilerParams(vmem_limit_bytes=32 << 20),
+        cost_estimate=pl.CostEstimate(flops=10**9, bytes_accessed=4 * 10**6, transcendentals=0),
+    )(me, features.reshape(128, 4096), *tiles, *raw)
+    group = jax.ShapeDtypeStruct((128, 384), BF)
     picked = call(
         regroup_body,
         (group,) * 4,
         (1,),
-        [scalar, msg_spec, whole((16, 576)), whole((1, 16)), whole((64, 64))],
-        (whole((192, 384)),) * 4,
+        [scalar, msg_spec],
+        (whole((128, 384)),) * 4,
         flops=4 * 10**8,
         moved=10**6,
-    )(me, picked, conv_weight, conv_bias.reshape(1, 16), down_weight)
+    )(me, picked)
     picked = to_peers(picked)
-    pair = pl.BlockSpec((1, 16, 4096), lambda i, m: (i, 0, 0))
     local = pl.pallas_call(
         level_body,
         out_shape=(jax.ShapeDtypeStruct((64, 1024), BF),) * 4,
-        grid_spec=pltpu.PrefetchScalarGridSpec(
-            num_scalar_prefetch=1,
-            grid=(2,),
-            in_specs=[pl.BlockSpec((1, 16, 4096), lambda i, m: (m[0] * 2 + i, 0, 0))]
-            + [pair] * 3
-            + [whole((192, 384))] * 4,
-            out_specs=(whole((64, 1024)),) * 4,
-            scratch_shapes=(
-                pltpu.VMEM((4, 16, 4096), BF),
-                pltpu.VMEM((4, 192, 384), BF),
-                pltpu.VMEM((4, 64, 1024), BF),
-                pltpu.VMEM((1024, 1024), BF),
-                pltpu.VMEM((1024, 256), F32),
-                pltpu.VMEM((64, 256), F32),
-                pltpu.VMEM((256, 128), F32),
-                pltpu.VMEM((256, 1024), BF),
-                pltpu.VMEM((64, 256), BF),
-                pltpu.VMEM((256, 64), BF),
-                pltpu.VMEM((256, 128), F32),
-            ),
+        in_specs=[scalar] + [vmem] * 9,
+        out_specs=(vmem,) * 4,
+        scratch_shapes=(
+            pltpu.VMEM((4, 128, 384), BF),
+            pltpu.VMEM((4, 64, 1024), BF),
+            pltpu.VMEM((2, 1024, 1024), BF),
+            pltpu.VMEM((1024, 256), F32),
         ),
-        compiler_params=pltpu.CompilerParams(vmem_limit_bytes=48 << 20),
+        compiler_params=pltpu.CompilerParams(vmem_limit_bytes=32 << 20),
         cost_estimate=pl.CostEstimate(flops=4 * 10**9, bytes_accessed=4 * 10**6, transcendentals=0),
-    )(me, features, *[t.reshape(2, 16, 4096) for t in tiles], *picked)
+    )(me, *picked, *ready)
     local = to_peers(local)
     out = call(
         spread_body,

time: 142 us -> 139 us (0.979)
  waiting for transfers between devices: 28.9 us -> 25.3 us
  local copies, waits for them, and re-layouts: 2.88 us -> 0.01 us
  Pallas kernels: 16 us -> 17.8 us
    pallas_call x2 -> x3, Pallas kernels: 2.44 us -> 6.1 us  [the longest x1 3.35 us: on_device(): call(send_body, (msg, jax.ShapeDtypeStruct((64, 384), BF), peer_rows, pee...]
    ppermute x9 -> x12, waiting for transfers between devices: 28.9 us -> 25.3 us  [to_peers(): lax.ppermute(parts[d], 'chan', [(i, i ^ d) for i in range(4)])]
    unnamed x22 -> x2, local copies, waits for them, and re-layouts: 2.88 us -> 0.01 us
    pallas_call x1, Pallas kernels: 8.39 us -> 6.54 us  [on_device(): pl.pallas_call(level_body, out_shape=(jax.ShapeDtypeStruct((64, 1024), BF...]
    ppermute x9 -> x12, starting transfers between devices: 9.63 us -> 10.8 us  [to_peers(): lax.ppermute(parts[d], 'chan', [(i, i ^ d) for i in range(4)])]
  transfers between devices with their start and end apart: 10 -> 13, of which waited for: 6 -> 7; matrix products, arithmetic and copies ran while one was open for 0% -> 0% of each run, Pallas kernels for 0% -> 2%
where the time goes in v4:
time: 139 us; the launch traced here: 137 us
  blocking collectives  66.7 us (48%)
  starting transfers between devices  26.1 us (19%)
  waiting for transfers between devices  25.3 us (18%)
  Pallas kernels  17.8 us (13%)
    all_to_all x3, blocking collectives, to_nodes(): lax.all_to_all(x.reshape(64, 8, 384), 'tile', 0, 0, tiled=True).reshape(MSG)  66.7 us
    ppermute x12, waiting for transfers between devices, to_peers(): lax.ppermute(parts[d], 'chan', [(i, i ^ d) for i in range(4)])  25.3 us
    all_to_all x1, starting transfers between devices, to_nodes(): lax.all_to_all(x.reshape(64, 8, 384), 'tile', 0, 0, tiled=True).reshape(MSG)  15.2 us
    ppermute x12, starting transfers between devices, to_peers(): lax.ppermute(parts[d], 'chan', [(i, i ^ d) for i in range(4)])  10.8 us
    pallas_call x1, Pallas kernels, on_device(): pl.pallas_call(level_body, out_shape=(jax.ShapeDtypeStruct((64, 1024), BF...  6.54 us
    pallas_call x1, Pallas kernels, on_device(): call(send_body, (msg, jax.ShapeDtypeStruct((64, 384), BF), peer_rows, pee...  3.35 us
  transfers between devices with their start and end apart: 13, of which 7 were waited for; matrix products, arithmetic and copies ran while one was open for 0% of the time, Pallas kernels for 2%

profile of v4, /device:TPU:1, one launch (start us, length us, event | category | flops | bytes accessed | tf_op | source)
XLA Modules:
  0.0 136.6 jit_solution(1529647536965567752)
XLA Ops:
  0.6 3.4 %shard_map.129 = (bf16[512,384]{1,0:T(8,128)(2,1)}, bf16[64,384]{1,0:T(8,128)(2,1)S(1)}, bf16[32,4096]{1,0:T(8,128)(2,1)S(1)}, bf16[32,4096]{1,0:T(8,128)(2,1)S(1)}, bf16[32,4096]{1,0:T(8,128)(2,1)S(1)}) custom-call(s32[1]{0:T(128)} %bitcast.me_ref, bf16[128,4096]{1,0:T(8,128)(2,1)} %bitcast.26, bf16[32,4096]{1,0:T(8,128)(2,1)} %bitcast.28, ...), custom_call_target="tpu_custom_call" | custom-call | flops 1000000000 | bytes 2000000 | tf_op jit(solution)/shard_map/pallas_call | solution.py:504
  4.0 15.2 %all-to-all-start = ((bf16[64,8,384]{2,1,0:T(8,128)(2,1)}), bf16[64,8,384]{2,1,0:T(8,128)(2,1)S(1)}, u32[]{:S(2)}, u32[]{:S(2)}) async-start(bf16[64,8,384]{2,1,0:T(8,128)(2,1)} %bitcast.9), calls=%async_computation | async-start | bytes 786432 | tf_op jit(solution)/shard_map/all_to_all | solution.py:499
  19.2 1.0 collective-permute-start.3
  20.7 1.3 collective-permute-start.5
  22.6 0.7 collective-permute-done.refs_5_
  23.3 0.9 collective-permute-start.2
  24.2 14.6 %collective-permute-done.1.refs_6_ = bf16[64,384]{1,0:T(8,128)(2,1)S(1)} collective-permute-done((bf16[64,384]{1,0:T(8,128)(2,1)S(1)}, bf16[64,384]{1,0:T(8,128)(2,1)S(1)}, u32[]{:S(2)}, u32[]{:S(2)}) %collective-permute-start.1) | collective-permute-done | bytes 49184 | tf_op jit(solution)/shard_map/ppermute | solution.py:479
  38.8 1.1 collective-permute-done.2.refs_7_
  39.9 2.5 %shard_map.130 = (bf16[512,384]{1,0:T(8,128)(2,1)S(1)}, f32[8,512]{1,0:T(8,128)S(1)}) custom-call(bf16[512,384]{1,0:T(8,128)(2,1)S(1)} %bitcast.19), custom_call_target="tpu_custom_call" | custom-call | flops 1000000000 | bytes 1000000 | tf_op jit(solution)/shard_map/pallas_call | solution.py:535
  42.4 26.0 %all_to_all.20 = bf16[64,8,384]{2,1,0:T(8,128)(2,1)S(1)} all-to-all(bf16[64,8,384]{2,1,0:T(8,128)(2,1)S(1)} %bitcast.23), channel_id=1, replica_groups=mesh['tile'=64,'chan'=4] {'tile'}, dimensions={0} | all-to-all | bytes 786432 | tf_op jit(solution)/shard_map/all_to_all | solution.py:499
  68.5 0.5 shard_map.131
  69.0 2.9 %collective-permute-start.6 = (bf16[128,384]{1,0:T(8,128)(2,1)S(1)}, bf16[128,384]{1,0:T(8,128)(2,1)S(1)}, u32[]{:S(2)}, u32[]{:S(2)}) collective-permute-start(bf16[128,384]{1,0:T(8,128)(2,1)S(1)} %get-tuple-element.44), channel_id=1, source_target_pairs={{0,1},{1,0},{2,3},{3,2},{4,5},{5,4},{6,7},{7,6},{8,9},{9,8},{10,11... | collective-permute-start | bytes 294920 | tf_op jit(solution)/shard_map/ppermute | solution.py:479
  72.0 1.7 %collective-permute-start.8 = (bf16[128,384]{1,0:T(8,128)(2,1)S(1)}, bf16[128,384]{1,0:T(8,128)(2,1)S(1)}, u32[]{:S(2)}, u32[]{:S(2)}) collective-permute-start(bf16[128,384]{1,0:T(8,128)(2,1)S(1)} %get-tuple-element.46), channel_id=1, source_target_pairs={{0,3},{1,2},{2,1},{3,0},{4,7},{5,6},{6,5},{7,4},{8,11},{9,10},{10,... | collective-permute-start | bytes 294920 | tf_op jit(solution)/shard_map/ppermute | solution.py:479
  73.6 2.2 %shard_map.132 = (bf16[2,1024,1024]{2,1,0:T(8,128)(2,1)S(1)}, bf16[256,1024]{1,0:T(8,128)(2,1)S(1)}, bf16[64,256]{1,0:T(8,128)(2,1)S(1)}, bf16[256,64]{1,0:T(8,128)(2,1)S(1)}, f32[256,128]{1,0:T(8,128)S(1)}) custom-call(s32[1]{0:T(128)} %bitcast.me_ref, bf16[128,4096]{1,0:T(8,128)(2,1)S(1)} %bitcast.27, bf16[32,4096]{1,0:T(8,128)(2,1)S(1)} %collective-permute-done.3.refs_1_, ...), custom_call_target="tpu_custom_call" | custom-call | flops 1000000000 | bytes 4000000 | tf_op jit(solution)/shard_map/pallas_call | solution.py:547
  76.3 2.3 %collective-permute-done.8.refs_3_ = bf16[128,384]{1,0:T(8,128)(2,1)S(1)} collective-permute-done((bf16[128,384]{1,0:T(8,128)(2,1)S(1)}, bf16[128,384]{1,0:T(8,128)(2,1)S(1)}, u32[]{:S(2)}, u32[]{:S(2)}) %collective-permute-start.8) | collective-permute-done | bytes 98336 | tf_op jit(solution)/shard_map/ppermute | solution.py:479
  78.6 6.5 %shard_map.133 = (bf16[64,1024]{1,0:T(8,128)(2,1)S(1)}, bf16[64,1024]{1,0:T(8,128)(2,1)S(1)}, bf16[64,1024]{1,0:T(8,128)(2,1)S(1)}, bf16[64,1024]{1,0:T(8,128)(2,1)S(1)}) custom-call(s32[1]{0:T(128)} %bitcast.me_ref, bf16[128,384]{1,0:T(8,128)(2,1)S(1)} %get-tuple-element.43.refs_0_, bf16[128,384]{1,0:T(8,128)(2,1)S(1)} %collective-permute-done.6.refs_1_, ...), custom_call_target="tpu_custom_call" | custom-call | flops 4000000000 | bytes 4000000 | tf_op jit(solution)/shard_map/pallas_call | solution.py:577
  85.2 1.8 %collective-permute-start.11 = (bf16[64,1024]{1,0:T(8,128)(2,1)S(1)}, bf16[64,1024]{1,0:T(8,128)(2,1)S(1)}, u32[]{:S(2)}, u32[]{:S(2)}) collective-permute-start(bf16[64,1024]{1,0:T(8,128)(2,1)S(1)} %get-tuple-element.62), channel_id=1, source_target_pairs={{0,3},{1,2},{2,1},{3,0},{4,7},{5,6},{6,5},{7,4},{8,11},{9,10},{10,... | collective-permute-start | bytes 393224 | tf_op jit(solution)/shard_map/ppermute | solution.py:479
  87.0 3.0 %collective-permute-done.10.refs_2_ = bf16[64,1024]{1,0:T(8,128)(2,1)S(1)} collective-permute-done((bf16[64,1024]{1,0:T(8,128)(2,1)S(1)}, bf16[64,1024]{1,0:T(8,128)(2,1)S(1)}, u32[]{:S(2)}, u32[]{:S(2)}) %collective-permute-start.10) | collective-permute-done | bytes 131104 | tf_op jit(solution)/shard_map/ppermute | solution.py:479
  90.1 3.1 %collective-permute-done.11.refs_3_ = bf16[64,1024]{1,0:T(8,128)(2,1)S(1)} collective-permute-done((bf16[64,1024]{1,0:T(8,128)(2,1)S(1)}, bf16[64,1024]{1,0:T(8,128)(2,1)S(1)}, u32[]{:S(2)}, u32[]{:S(2)}) %collective-permute-start.11) | collective-permute-done | bytes 131104 | tf_op jit(solution)/shard_map/ppermute | solution.py:479
  93.2 0.5 shard_map.134
  93.7 20.3 %all_to_all.21 = bf16[64,8,384]{2,1,0:T(8,128)(2,1)S(1)} all-to-all(bf16[64,8,384]{2,1,0:T(8,128)(2,1)S(1)} %bitcast.21), channel_id=1, replica_groups=mesh['tile'=64,'chan'=4] {'tile'}, dimensions={0} | all-to-all | bytes 786432 | tf_op jit(solution)/shard_map/all_to_all | solution.py:499
  114.0 0.8 shard_map.135
  114.8 20.4 %all_to_all.22 = bf16[64,8,384]{2,1,0:T(8,128)(2,1)S(1)} all-to-all(bf16[64,8,384]{2,1,0:T(8,128)(2,1)S(1)} %bitcast.25), channel_id=1, replica_groups=mesh['tile'=64,'chan'=4] {'tile'}, dimensions={0} | all-to-all | bytes 786432 | tf_op jit(solution)/shard_map/all_to_all | solution.py:499
  135.2 1.4 %shard_map.136 = (bf16[32,4096]{1,0:T(8,128)(2,1)}, f32[16,576]{1,0:T(8,128)}, f32[64,64]{1,0:T(8,128)}, f32[1,16]{1,0:T(1,128)}) custom-call(bf16[512,384]{1,0:T(8,128)(2,1)S(1)} %bitcast.22), custom_call_target="tpu_custom_call" | custom-call | flops 400000000 | bytes 1000000 | tf_op jit(solution)/shard_map/pallas_call | solution.py:607
  (15 shorter events, 1.6 us)
Async XLA Ops:
  4.0 69.7 %copy-start = (bf16[8,16,4096]{2,1,0:T(8,128)(2,1)S(1)}, bf16[8,16,4096]{2,1,0:T(8,128)(2,1)}, u32[]{:S(2)}) copy-start(bf16[8,16,4096]{2,1,0:T(8,128)(2,1)} %param.10) | copy-start | bytes 3145732
  4.0 35.9 %all-to-all-start = ((bf16[64,8,384]{2,1,0:T(8,128)(2,1)}), bf16[64,8,384]{2,1,0:T(8,128)(2,1)S(1)}, u32[]{:S(2)}, u32[]{:S(2)}) async-start(bf16[64,8,384]{2,1,0:T(8,128)(2,1)} %bitcast.9), calls=%async_computation | async-start | bytes 786432 | tf_op jit(solution)/shard_map/all_to_all | solution.py:499
  19.2 20.7 %collective-permute-start.3 = (bf16[32,4096]{1,0:T(8,128)(2,1)S(1)}, bf16[32,4096]{1,0:T(8,128)(2,1)S(1)}, u32[]{:S(2)}, u32[]{:S(2)}) collective-permute-start(bf16[32,4096]{1,0:T(8,128)(2,1)S(1)} %get-tuple-element.38), channel_id=1, source_target_pairs={{0,1},{1,0},{2,3},{3,2},{4,5},{5,4},{6,7},{7,6},{8,9},{9,8},{10,11... | collective-permute-start | bytes 786440 | tf_op jit(solution)/shard_map/ppermute | solution.py:479
  20.3 19.6 %collective-permute-start.4 = (bf16[32,4096]{1,0:T(8,128)(2,1)S(1)}, bf16[32,4096]{1,0:T(8,128)(2,1)S(1)}, u32[]{:S(2)}, u32[]{:S(2)}) collective-permute-start(bf16[32,4096]{1,0:T(8,128)(2,1)S(1)} %get-tuple-element.39), channel_id=1, source_target_pairs={{0,2},{1,3},{2,0},{3,1},{4,6},{5,7},{6,4},{7,5},{8,10},{9,11},{10,... | collective-permute-start | bytes 786440 | tf_op jit(solution)/shard_map/ppermute | solution.py:479
  20.7 19.2 %collective-permute-start.5 = (bf16[32,4096]{1,0:T(8,128)(2,1)S(1)}, bf16[32,4096]{1,0:T(8,128)(2,1)S(1)}, u32[]{:S(2)}, u32[]{:S(2)}) collective-permute-start(bf16[32,4096]{1,0:T(8,128)(2,1)S(1)} %get-tuple-element.40), channel_id=1, source_target_pairs={{0,3},{1,2},{2,1},{3,0},{4,7},{5,6},{6,5},{7,4},{8,11},{9,10},{10,... | collective-permute-start | bytes 786440 | tf_op jit(solution)/shard_map/ppermute | solution.py:479
  22.0 1.2 collective-permute-start
  22.2 16.6 %collective-permute-start.1 = (bf16[64,384]{1,0:T(8,128)(2,1)S(1)}, bf16[64,384]{1,0:T(8,128)(2,1)S(1)}, u32[]{:S(2)}, u32[]{:S(2)}) collective-permute-start(bf16[64,384]{1,0:T(8,128)(2,1)S(1)} %get-tuple-element.50.refs_4_), channel_id=1, source_target_pairs={{0,2},{1,3},{2,0},{3,1},{4,6},{5,7},{6,4},{7,5},{8,10},{9,11},{10,... | collective-permute-start | bytes 147464 | tf_op jit(solution)/shard_map/ppermute | solution.py:479
  23.3 16.7 %collective-permute-start.2 = (bf16[64,384]{1,0:T(8,128)(2,1)S(1)}, bf16[64,384]{1,0:T(8,128)(2,1)S(1)}, u32[]{:S(2)}, u32[]{:S(2)}) collective-permute-start(bf16[64,384]{1,0:T(8,128)(2,1)S(1)} %get-tuple-element.50.refs_4_), channel_id=1, source_target_pairs={{0,3},{1,2},{2,1},{3,0},{4,7},{5,6},{6,5},{7,4},{8,11},{9,10},{10,... | collective-permute-start | bytes 147464 | tf_op jit(solution)/shard_map/ppermute | solution.py:479
  69.0 6.9 %collective-permute-start.6 = (bf16[128,384]{1,0:T(8,128)(2,1)S(1)}, bf16[128,384]{1,0:T(8,128)(2,1)S(1)}, u32[]{:S(2)}, u32[]{:S(2)}) collective-permute-start(bf16[128,384]{1,0:T(8,128)(2,1)S(1)} %get-tuple-element.44), channel_id=1, source_target_pairs={{0,1},{1,0},{2,3},{3,2},{4,5},{5,4},{6,7},{7,6},{8,9},{9,8},{10,11... | collective-permute-start | bytes 294920 | tf_op jit(solution)/shard_map/ppermute | solution.py:479
  71.9 4.4 %collective-permute-start.7 = (bf16[128,384]{1,0:T(8,128)(2,1)S(1)}, bf16[128,384]{1,0:T(8,128)(2,1)S(1)}, u32[]{:S(2)}, u32[]{:S(2)}) collective-permute-start(bf16[128,384]{1,0:T(8,128)(2,1)S(1)} %get-tuple-element.45), channel_id=1, source_target_pairs={{0,2},{1,3},{2,0},{3,1},{4,6},{5,7},{6,4},{7,5},{8,10},{9,11},{10,... | collective-permute-start | bytes 294920 | tf_op jit(solution)/shard_map/ppermute | solution.py:479
  72.0 6.6 %collective-permute-start.8 = (bf16[128,384]{1,0:T(8,128)(2,1)S(1)}, bf16[128,384]{1,0:T(8,128)(2,1)S(1)}, u32[]{:S(2)}, u32[]{:S(2)}) collective-permute-start(bf16[128,384]{1,0:T(8,128)(2,1)S(1)} %get-tuple-element.46), channel_id=1, source_target_pairs={{0,3},{1,2},{2,1},{3,0},{4,7},{5,6},{6,5},{7,4},{8,11},{9,10},{10,... | collective-permute-start | bytes 294920 | tf_op jit(solution)/shard_map/ppermute | solution.py:479
  85.1 5.0 %collective-permute-start.10 = (bf16[64,1024]{1,0:T(8,128)(2,1)S(1)}, bf16[64,1024]{1,0:T(8,128)(2,1)S(1)}, u32[]{:S(2)}, u32[]{:S(2)}) collective-permute-start(bf16[64,1024]{1,0:T(8,128)(2,1)S(1)} %get-tuple-element.61), channel_id=1, source_target_pairs={{0,2},{1,3},{2,0},{3,1},{4,6},{5,7},{6,4},{7,5},{8,10},{9,11},{10,... | collective-permute-start | bytes 393224 | tf_op jit(solution)/shard_map/ppermute | solution.py:479
  85.2 8.0 %collective-permute-start.11 = (bf16[64,1024]{1,0:T(8,128)(2,1)S(1)}, bf16[64,1024]{1,0:T(8,128)(2,1)S(1)}, u32[]{:S(2)}, u32[]{:S(2)}) collective-permute-start(bf16[64,1024]{1,0:T(8,128)(2,1)S(1)} %get-tuple-element.62), channel_id=1, source_target_pairs={{0,3},{1,2},{2,1},{3,0},{4,7},{5,6},{6,5},{7,4},{8,11},{9,10},{10,... | collective-permute-start | bytes 393224 | tf_op jit(solution)/shard_map/ppermute | solution.py:479
  87.0 6.2 %collective-permute-start.9 = (bf16[64,1024]{1,0:T(8,128)(2,1)S(1)}, bf16[64,1024]{1,0:T(8,128)(2,1)S(1)}, u32[]{:S(2)}, u32[]{:S(2)}) collective-permute-start(bf16[64,1024]{1,0:T(8,128)(2,1)S(1)} %get-tuple-element.60), channel_id=1, source_target_pairs={{0,1},{1,0},{2,3},{3,2},{4,5},{5,4},{6,7},{7,6},{8,9},{9,8},{10,11... | collective-permute-start | bytes 393224 | tf_op jit(solution)/shard_map/ppermute | solution.py:479

commit v5 on v4

--- a/solution.py
+++ b/solution.py
@@ -97,7 +97,11 @@
     pack_weights(conv_ref, bias_ref, down_ref, raw_ref)
     for d in range(1, 4):
         peer = me_ref[0] ^ d
-        peer_refs[d - 1][...] = feat_ref[pl.ds(pl.multiple_of(peer * 32, 32), 32), :]
+        first_ref, second_ref = peer_refs[d - 1], peer_refs[d + 2]
+        first_ref[:, 0:4096] = feat_ref[pl.ds(pl.multiple_of(peer * 32, 16), 16), :]
+        second_ref[...] = feat_ref[pl.ds(pl.multiple_of(peer * 32 + 16, 16), 16), :]
+        for q in range(4):
+            first_ref[:, 4096 + q * 384 : 4480 + q * 384] = raw_ref[q * 16 : q * 16 + 16, :]
 
     cot = cot_ref[...]
     stack = jnp.concatenate([cot[:, q * 256 : q * 256 + 256] for q in range(16)], axis=0)
@@ -251,12 +255,17 @@
 
 
 def ready_body(me_ref, *refs):
-    feat_refs, raw_refs = refs[0:4], refs[4:8]
+    own_ref, own_raw_ref, first_refs, second_refs = refs[0], refs[1], refs[2:5], refs[5:8]
     win_ref, w_ref, down_ref, down_t_ref, bias_ref, x_ref, raw_ref = refs[8:]
     me = me_ref[0]
-    for d in range(4):
-        raw_ref[me ^ d] = raw_refs[d][...]
-        x_ref[me ^ d] = feat_refs[d][...]
+    raw_ref[me] = own_raw_ref[...]
+    x_ref[me] = own_ref[...]
+    for d in range(1, 4):
+        first_ref = first_refs[d - 1]
+        x_ref[me ^ d, 0:16, :] = first_ref[:, 0:4096]
+        x_ref[me ^ d, 16:32, :] = second_refs[d - 1][...]
+        for q in range(4):
+            raw_ref[me ^ d, q * 16 : q * 16 + 16, :] = first_ref[:, 4096 + q * 384 : 4480 + q * 384]
     lay_weights(raw_ref, w_ref, down_ref, down_t_ref, bias_ref)
     l_in = down_col(512)
     to = (((l_in >> 6) & 1) << 8) | ((l_in & 1) << 7) | ((l_in >> 7) << 5) | ((l_in >> 1) & 31)
@@ -500,15 +509,16 @@
 
     me = lax.axis_index("chan").astype(jnp.int32).reshape(1)
     scalar = pl.BlockSpec(memory_space=pltpu.SMEM)
-    peer_rows = jax.ShapeDtypeStruct((32, 4096), BF)
-    pieces, raw, *tiles = call(
+    first = jax.ShapeDtypeStruct((16, 5632), BF)
+    second = jax.ShapeDtypeStruct((16, 4096), BF)
+    pieces, raw, *peers = call(
         send_body,
-        (msg, jax.ShapeDtypeStruct((64, 384), BF), peer_rows, peer_rows, peer_rows),
+        (msg, jax.ShapeDtypeStruct((64, 384), BF)) + (first,) * 3 + (second,) * 3,
         (1,),
         [scalar, whole((128, 4096)), whole((32, 4096))]
         + [whole((4, 8))] * 4
         + [whole((1, 8)), whole((16, 576)), whole((1, 16)), whole((64, 64))],
-        (msg_spec, whole((64, 384))) + (whole((32, 4096)),) * 3,
+        (msg_spec, whole((64, 384))) + (whole((16, 5632)),) * 3 + (whole((16, 4096)),) * 3,
         flops=10**9,
         moved=2 * 10**6,
     )(
@@ -529,9 +539,9 @@
             )
         ],
     )
-    raw = to_peers([raw] * 4)
-    tiles = to_peers([None] + list(tiles))[1:]
-    pieces, raw, tiles = lax.optimization_barrier((to_nodes(pieces), raw, tiles))
+    first = to_peers([None] + peers[0:3])[1:]
+    second = to_peers([None] + peers[3:6])[1:]
+    pieces, first = lax.optimization_barrier((to_nodes(pieces), first))
     picked, slots = call(
         pick_body,
         (msg, jax.ShapeDtypeStruct((8, 512), F32)),
@@ -556,13 +566,13 @@
         grid_spec=pltpu.PrefetchScalarGridSpec(
             num_scalar_prefetch=1,
             grid=(1,),
-            in_specs=[own] + [whole((32, 4096))] * 3 + [whole((64, 384))] * 4,
+            in_specs=[own, whole((64, 384))] + [whole((16, 5632))] * 3 + [whole((16, 4096))] * 3,
             out_specs=(vmem,) * 5,
             scratch_shapes=(pltpu.VMEM((4, 32, 4096), BF), pltpu.VMEM((4, 64, 384), BF)),
         ),
         compiler_params=pltpu.CompilerParams(vmem_limit_bytes=32 << 20),
         cost_estimate=pl.CostEstimate(flops=10**9, bytes_accessed=4 * 10**6, transcendentals=0),
-    )(me, features.reshape(128, 4096), *tiles, *raw)
+    )(me, features.reshape(128, 4096), raw, *first, *second)
     group = jax.ShapeDtypeStruct((128, 384), BF)
     picked = call(
         regroup_body,

time: 139 us -> 134 us (0.964)
  blocking collectives: 66.7 us -> 40.7 us
  starting transfers between devices: 26.1 us -> 38.4 us
  waiting for transfers between devices: 25.3 us -> 33.5 us
    all_to_all x3 -> x2, blocking collectives: 66.7 us -> 40.7 us  [to_nodes(): lax.all_to_all(x.reshape(64, 8, 384), 'tile', 0, 0, tiled=True).reshape(MSG)]
    all_to_all x1 -> x2, waiting for transfers between devices: 0.01 us -> 12.2 us  [to_nodes(): lax.all_to_all(x.reshape(64, 8, 384), 'tile', 0, 0, tiled=True).reshape(MSG)]
    all_to_all x1 -> x2, starting transfers between devices: 15.2 us -> 26.6 us  [to_nodes(): lax.all_to_all(x.reshape(64, 8, 384), 'tile', 0, 0, tiled=True).reshape(MSG)]
    ppermute x12, waiting for transfers between devices: 25.3 us -> 21.4 us  [to_peers(): lax.ppermute(parts[d], 'chan', [(i, i ^ d) for i in range(4)])]
  transfers between devices with their start and end apart: 13 -> 14, of which waited for: 7 -> 7; matrix products, arithmetic and copies ran while one was open for 0% -> 0% of each run, Pallas kernels for 2% -> 2%
where the time goes in v5:
time: 134 us; the launch traced here: 132 us
  blocking collectives  40.7 us (30%)
  starting transfers between devices  38.4 us (29%)
  waiting for transfers between devices  33.5 us (25%)
  Pallas kernels  18.6 us (14%)
    all_to_all x2, blocking collectives, to_nodes(): lax.all_to_all(x.reshape(64, 8, 384), 'tile', 0, 0, tiled=True).reshape(MSG)  40.7 us
    all_to_all x2, starting transfers between devices, to_nodes(): lax.all_to_all(x.reshape(64, 8, 384), 'tile', 0, 0, tiled=True).reshape(MSG)  26.6 us
    ppermute x12, waiting for transfers between devices, to_peers(): lax.ppermute(parts[d], 'chan', [(i, i ^ d) for i in range(4)])  21.4 us
    all_to_all x2, waiting for transfers between devices, to_nodes(): lax.all_to_all(x.reshape(64, 8, 384), 'tile', 0, 0, tiled=True).reshape(MSG)  12.2 us
    ppermute x12, starting transfers between devices, to_peers(): lax.ppermute(parts[d], 'chan', [(i, i ^ d) for i in range(4)])  11.9 us
    pallas_call x1, Pallas kernels, on_device(): pl.pallas_call(level_body, out_shape=(jax.ShapeDtypeStruct((64, 1024), BF...  6.54 us
    pallas_call x1, Pallas kernels, on_device(): call(send_body, (msg, jax.ShapeDtypeStruct((64, 384), BF)) + (first,) * 3...  3.41 us
    pallas_call x1, Pallas kernels, on_device(): call(pick_body, (msg, jax.ShapeDtypeStruct((8, 512), F32)), (1,), [msg_sp...  3.24 us
  transfers between devices with their start and end apart: 14, of which 7 were waited for; matrix products, arithmetic and copies ran while one was open for 0% of the time, Pallas kernels for 2%

profile of v5, /device:TPU:1, one launch (start us, length us, event | category | flops | bytes accessed | tf_op | source)
XLA Modules:
  0.0 132.0 jit_solution(9557741895225033149)
XLA Ops:
  0.6 3.4 %shard_map.129 = (bf16[512,384]{1,0:T(8,128)(2,1)}, bf16[64,384]{1,0:T(8,128)(2,1)S(1)}, bf16[16,5632]{1,0:T(8,128)(2,1)S(1)}, bf16[16,5632]{1,0:T(8,128)(2,1)S(...) custom-call(s32[1]{0:T(128)} %bitcast.me_ref, ...), custom_call_target="tpu_custom_call" | custom-call | flops 1000000000 | bytes 2000000 | tf_op jit(solution)/shard_map/pallas_call | solution.py:514
  4.0 15.2 %all-to-all-start = ((bf16[64,8,384]{2,1,0:T(8,128)(2,1)}), bf16[64,8,384]{2,1,0:T(8,128)(2,1)S(1)}, u32[]{:S(2)}, u32[]{:S(2)}) async-start(bf16[64,8,384]{2,1,0:T(8,128)(2,1)} %bitcast.9), calls=%async_computation | async-start | bytes 786432 | tf_op jit(solution)/shard_map/all_to_all | solution.py:508
  19.3 1.0 collective-permute-start
  20.8 1.3 collective-permute-start.2
  22.1 6.9 %collective-permute-done.1.refs_3_ = bf16[16,5632]{1,0:T(8,128)(2,1)S(1)} collective-permute-done((bf16[16,5632]{1,0:T(8,128)(2,1)S(1)}, bf16[16,5632]{1,0:T(8,128)(2,1)S(1)}, u32[]{:S(2)}, u32[]{:S(2)}) %collective-permute-start.1) | collective-permute-done | bytes 180256 | tf_op jit(solution)/shard_map/ppermute | solution.py:488
  28.9 5.7 %collective-permute-done.2.refs_4_ = bf16[16,5632]{1,0:T(8,128)(2,1)S(1)} collective-permute-done((bf16[16,5632]{1,0:T(8,128)(2,1)S(1)}, bf16[16,5632]{1,0:T(8,128)(2,1)S(1)}, u32[]{:S(2)}, u32[]{:S(2)}) %collective-permute-start.2) | collective-permute-done | bytes 180256 | tf_op jit(solution)/shard_map/ppermute | solution.py:488
  34.6 3.2 %shard_map.130 = (bf16[512,384]{1,0:T(8,128)(2,1)}, f32[8,512]{1,0:T(8,128)S(1)}) custom-call(bf16[512,384]{1,0:T(8,128)(2,1)S(1)} %bitcast.19), custom_call_target="tpu_custom_call" | custom-call | flops 1000000000 | bytes 1000000 | tf_op jit(solution)/shard_map/pallas_call | solution.py:545
  37.8 11.3 %all-to-all-start.1 = ((bf16[64,8,384]{2,1,0:T(8,128)(2,1)}), bf16[64,8,384]{2,1,0:T(8,128)(2,1)S(1)}, u32[]{:S(2)}, u32[]{:S(2)}) async-start(bf16[64,8,384]{2,1,0:T(8,128)(2,1)} %bitcast.11), calls=%async_computation.1 | async-start | bytes 786432 | tf_op jit(solution)/shard_map/all_to_all | solution.py:508
  49.1 0.8 collective-permute-start.6
  50.0 1.7 %collective-permute-start.8 = (bf16[16,4096]{1,0:T(8,128)(2,1)S(1)}, bf16[16,4096]{1,0:T(8,128)(2,1)S(1)}, u32[]{:S(2)}, u32[]{:S(2)}) collective-permute-start(bf16[16,4096]{1,0:T(8,128)(2,1)S(1)} %get-tuple-element.51), channel_id=1, source_target_pairs={{0,3},{1,2},{2,1},{3,0},{4,7},{5,6},{6,5},{7,4},{8,11},{9,10},{10,... | collective-permute-start | bytes 393224 | tf_op jit(solution)/shard_map/ppermute | solution.py:488
  51.6 12.2 %all-to-all-done.1 = bf16[64,8,384]{2,1,0:T(8,128)(2,1)S(1)} async-done(((bf16[64,8,384]{2,1,0:T(8,128)(2,1)}), bf16[64,8,384]{2,1,0:T(8,128)(2,1)S(1)}, u32[]{:S(2)}, u32[]{:S(2)}) %all-to-all-start.1) | async-done | bytes 393248 | tf_op jit(solution)/shard_map/all_to_all | solution.py:508
  63.8 0.5 shard_map.131
  64.3 2.9 %collective-permute-start.3 = (bf16[128,384]{1,0:T(8,128)(2,1)S(1)}, bf16[128,384]{1,0:T(8,128)(2,1)S(1)}, u32[]{:S(2)}, u32[]{:S(2)}) collective-permute-start(bf16[128,384]{1,0:T(8,128)(2,1)S(1)} %get-tuple-element.42), channel_id=1, source_target_pairs={{0,1},{1,0},{2,3},{3,2},{4,5},{5,4},{6,7},{7,6},{8,9},{9,8},{10,11... | collective-permute-start | bytes 294920 | tf_op jit(solution)/shard_map/ppermute | solution.py:488
  67.3 1.7 %collective-permute-start.5 = (bf16[128,384]{1,0:T(8,128)(2,1)S(1)}, bf16[128,384]{1,0:T(8,128)(2,1)S(1)}, u32[]{:S(2)}, u32[]{:S(2)}) collective-permute-start(bf16[128,384]{1,0:T(8,128)(2,1)S(1)} %get-tuple-element.44), channel_id=1, source_target_pairs={{0,3},{1,2},{2,1},{3,0},{4,7},{5,6},{6,5},{7,4},{8,11},{9,10},{10,... | collective-permute-start | bytes 294920 | tf_op jit(solution)/shard_map/ppermute | solution.py:488
  69.0 2.2 %shard_map.132 = (bf16[2,1024,1024]{2,1,0:T(8,128)(2,1)S(1)}, bf16[256,1024]{1,0:T(8,128)(2,1)S(1)}, bf16[64,256]{1,0:T(8,128)(2,1)S(1)}, bf16[256,64]{1,0:T(8,128)(2,1)S(1)}, f32[256,128]{1,0:T(8,128)S(1)}) custom-call(s32[1]{0:T(128)} %bitcast.me_ref, bf16[128,4096]{1,0:T(8,128)(2,1)S(1)} %bitcast.26, bf16[64,384]{1,0:T(8,128)(2,1)S(1)} %get-tuple-element.45.refs_1_, ...), custom_call_target="tpu_custom_call" | custom-call | flops 1000000000 | bytes 4000000 | tf_op jit(solution)/shard_map/pallas_call | solution.py:557
  71.6 2.3 %collective-permute-done.5.refs_3_ = bf16[128,384]{1,0:T(8,128)(2,1)S(1)} collective-permute-done((bf16[128,384]{1,0:T(8,128)(2,1)S(1)}, bf16[128,384]{1,0:T(8,128)(2,1)S(1)}, u32[]{:S(2)}, u32[]{:S(2)}) %collective-permute-start.5) | collective-permute-done | bytes 98336 | tf_op jit(solution)/shard_map/ppermute | solution.py:488
  73.9 6.5 %shard_map.133 = (bf16[64,1024]{1,0:T(8,128)(2,1)S(1)}, bf16[64,1024]{1,0:T(8,128)(2,1)S(1)}, bf16[64,1024]{1,0:T(8,128)(2,1)S(1)}, bf16[64,1024]{1,0:T(8,128)(2,1)S(1)}) custom-call(s32[1]{0:T(128)} %bitcast.me_ref, bf16[128,384]{1,0:T(8,128)(2,1)S(1)} %get-tuple-element.41.refs_0_, bf16[128,384]{1,0:T(8,128)(2,1)S(1)} %collective-permute-done.3.refs_1_, ...), custom_call_target="tpu_custom_call" | custom-call | flops 4000000000 | bytes 4000000 | tf_op jit(solution)/shard_map/pallas_call | solution.py:587
  80.6 1.8 %collective-permute-start.11 = (bf16[64,1024]{1,0:T(8,128)(2,1)S(1)}, bf16[64,1024]{1,0:T(8,128)(2,1)S(1)}, u32[]{:S(2)}, u32[]{:S(2)}) collective-permute-start(bf16[64,1024]{1,0:T(8,128)(2,1)S(1)} %get-tuple-element.60), channel_id=1, source_target_pairs={{0,3},{1,2},{2,1},{3,0},{4,7},{5,6},{6,5},{7,4},{8,11},{9,10},{10,... | collective-permute-start | bytes 393224 | tf_op jit(solution)/shard_map/ppermute | solution.py:488
  82.4 3.0 %collective-permute-done.10.refs_2_ = bf16[64,1024]{1,0:T(8,128)(2,1)S(1)} collective-permute-done((bf16[64,1024]{1,0:T(8,128)(2,1)S(1)}, bf16[64,1024]{1,0:T(8,128)(2,1)S(1)}, u32[]{:S(2)}, u32[]{:S(2)}) %collective-permute-start.10) | collective-permute-done | bytes 131104 | tf_op jit(solution)/shard_map/ppermute | solution.py:488
  85.4 3.1 %collective-permute-done.11.refs_3_ = bf16[64,1024]{1,0:T(8,128)(2,1)S(1)} collective-permute-done((bf16[64,1024]{1,0:T(8,128)(2,1)S(1)}, bf16[64,1024]{1,0:T(8,128)(2,1)S(1)}, u32[]{:S(2)}, u32[]{:S(2)}) %collective-permute-start.11) | collective-permute-done | bytes 131104 | tf_op jit(solution)/shard_map/ppermute | solution.py:488
  89.1 20.3 %all_to_all.20 = bf16[64,8,384]{2,1,0:T(8,128)(2,1)S(1)} all-to-all(bf16[64,8,384]{2,1,0:T(8,128)(2,1)S(1)} %bitcast.21), channel_id=1, replica_groups=mesh['tile'=64,'chan'=4] {'tile'}, dimensions={0} | all-to-all | bytes 786432 | tf_op jit(solution)/shard_map/all_to_all | solution.py:508
  109.4 0.8 shard_map.135
  110.2 20.4 %all_to_all.21 = bf16[64,8,384]{2,1,0:T(8,128)(2,1)S(1)} all-to-all(bf16[64,8,384]{2,1,0:T(8,128)(2,1)S(1)} %bitcast.24), channel_id=1, replica_groups=mesh['tile'=64,'chan'=4] {'tile'}, dimensions={0} | all-to-all | bytes 786432 | tf_op jit(solution)/shard_map/all_to_all | solution.py:508
  130.6 1.4 %shard_map.136 = (bf16[32,4096]{1,0:T(8,128)(2,1)}, f32[16,576]{1,0:T(8,128)}, f32[64,64]{1,0:T(8,128)}, f32[1,16]{1,0:T(1,128)}) custom-call(bf16[512,384]{1,0:T(8,128)(2,1)S(1)} %bitcast.22), custom_call_target="tpu_custom_call" | custom-call | flops 400000000 | bytes 1000000 | tf_op jit(solution)/shard_map/pallas_call | solution.py:617
  (16 shorter events, 1.6 us)
Async XLA Ops:
  4.0 65.0 %copy-start = (bf16[8,16,4096]{2,1,0:T(8,128)(2,1)S(1)}, bf16[8,16,4096]{2,1,0:T(8,128)(2,1)}, u32[]{:S(2)}) copy-start(bf16[8,16,4096]{2,1,0:T(8,128)(2,1)} %param.10) | copy-start | bytes 3145732
  4.0 30.5 %all-to-all-start = ((bf16[64,8,384]{2,1,0:T(8,128)(2,1)}), bf16[64,8,384]{2,1,0:T(8,128)(2,1)S(1)}, u32[]{:S(2)}, u32[]{:S(2)}) async-start(bf16[64,8,384]{2,1,0:T(8,128)(2,1)} %bitcast.9), calls=%async_computation | async-start | bytes 786432 | tf_op jit(solution)/shard_map/all_to_all | solution.py:508
  19.3 2.8 %collective-permute-start = (bf16[16,5632]{1,0:T(8,128)(2,1)S(1)}, bf16[16,5632]{1,0:T(8,128)(2,1)S(1)}, u32[]{:S(2)}, u32[]{:S(2)}) collective-permute-start(bf16[16,5632]{1,0:T(8,128)(2,1)S(1)} %get-tuple-element.36), channel_id=1, source_target_pairs={{0,1},{1,0},{2,3},{3,2},{4,5},{5,4},{6,7},{7,6},{8,9},{9,8},{10,11... | collective-permute-start | bytes 540680 | tf_op jit(solution)/shard_map/ppermute | solution.py:488
  20.3 8.6 %collective-permute-start.1 = (bf16[16,5632]{1,0:T(8,128)(2,1)S(1)}, bf16[16,5632]{1,0:T(8,128)(2,1)S(1)}, u32[]{:S(2)}, u32[]{:S(2)}) collective-permute-start(bf16[16,5632]{1,0:T(8,128)(2,1)S(1)} %get-tuple-element.37), channel_id=1, source_target_pairs={{0,2},{1,3},{2,0},{3,1},{4,6},{5,7},{6,4},{7,5},{8,10},{9,11},{10,... | collective-permute-start | bytes 540680 | tf_op jit(solution)/shard_map/ppermute | solution.py:488
  20.8 13.8 %collective-permute-start.2 = (bf16[16,5632]{1,0:T(8,128)(2,1)S(1)}, bf16[16,5632]{1,0:T(8,128)(2,1)S(1)}, u32[]{:S(2)}, u32[]{:S(2)}) collective-permute-start(bf16[16,5632]{1,0:T(8,128)(2,1)S(1)} %get-tuple-element.38), channel_id=1, source_target_pairs={{0,3},{1,2},{2,1},{3,0},{4,7},{5,6},{6,5},{7,4},{8,11},{9,10},{10,... | collective-permute-start | bytes 540680 | tf_op jit(solution)/shard_map/ppermute | solution.py:488
  37.8 26.0 %all-to-all-start.1 = ((bf16[64,8,384]{2,1,0:T(8,128)(2,1)}), bf16[64,8,384]{2,1,0:T(8,128)(2,1)S(1)}, u32[]{:S(2)}, u32[]{:S(2)}) async-start(bf16[64,8,384]{2,1,0:T(8,128)(2,1)} %bitcast.11), calls=%async_computation.1 | async-start | bytes 786432 | tf_op jit(solution)/shard_map/all_to_all | solution.py:508
  49.1 18.2 %collective-permute-start.6 = (bf16[16,4096]{1,0:T(8,128)(2,1)S(1)}, bf16[16,4096]{1,0:T(8,128)(2,1)S(1)}, u32[]{:S(2)}, u32[]{:S(2)}) collective-permute-start(bf16[16,4096]{1,0:T(8,128)(2,1)S(1)} %get-tuple-element.49), channel_id=1, source_target_pairs={{0,1},{1,0},{2,3},{3,2},{4,5},{5,4},{6,7},{7,6},{8,9},{9,8},{10,11... | collective-permute-start | bytes 393224 | tf_op jit(solution)/shard_map/ppermute | solution.py:488
  49.9 19.1 %collective-permute-start.7 = (bf16[16,4096]{1,0:T(8,128)(2,1)S(1)}, bf16[16,4096]{1,0:T(8,128)(2,1)S(1)}, u32[]{:S(2)}, u32[]{:S(2)}) collective-permute-start(bf16[16,4096]{1,0:T(8,128)(2,1)S(1)} %get-tuple-element.50), channel_id=1, source_target_pairs={{0,2},{1,3},{2,0},{3,1},{4,6},{5,7},{6,4},{7,5},{8,10},{9,11},{10,... | collective-permute-start | bytes 393224 | tf_op jit(solution)/shard_map/ppermute | solution.py:488
  50.0 19.0 %collective-permute-start.8 = (bf16[16,4096]{1,0:T(8,128)(2,1)S(1)}, bf16[16,4096]{1,0:T(8,128)(2,1)S(1)}, u32[]{:S(2)}, u32[]{:S(2)}) collective-permute-start(bf16[16,4096]{1,0:T(8,128)(2,1)S(1)} %get-tuple-element.51), channel_id=1, source_target_pairs={{0,3},{1,2},{2,1},{3,0},{4,7},{5,6},{6,5},{7,4},{8,11},{9,10},{10,... | collective-permute-start | bytes 393224 | tf_op jit(solution)/shard_map/ppermute | solution.py:488
  64.3 6.9 %collective-permute-start.3 = (bf16[128,384]{1,0:T(8,128)(2,1)S(1)}, bf16[128,384]{1,0:T(8,128)(2,1)S(1)}, u32[]{:S(2)}, u32[]{:S(2)}) collective-permute-start(bf16[128,384]{1,0:T(8,128)(2,1)S(1)} %get-tuple-element.42), channel_id=1, source_target_pairs={{0,1},{1,0},{2,3},{3,2},{4,5},{5,4},{6,7},{7,6},{8,9},{9,8},{10,11... | collective-permute-start | bytes 294920 | tf_op jit(solution)/shard_map/ppermute | solution.py:488
  67.3 4.4 %collective-permute-start.4 = (bf16[128,384]{1,0:T(8,128)(2,1)S(1)}, bf16[128,384]{1,0:T(8,128)(2,1)S(1)}, u32[]{:S(2)}, u32[]{:S(2)}) collective-permute-start(bf16[128,384]{1,0:T(8,128)(2,1)S(1)} %get-tuple-element.43), channel_id=1, source_target_pairs={{0,2},{1,3},{2,0},{3,1},{4,6},{5,7},{6,4},{7,5},{8,10},{9,11},{10,... | collective-permute-start | bytes 294920 | tf_op jit(solution)/shard_map/ppermute | solution.py:488
  67.3 6.6 %collective-permute-start.5 = (bf16[128,384]{1,0:T(8,128)(2,1)S(1)}, bf16[128,384]{1,0:T(8,128)(2,1)S(1)}, u32[]{:S(2)}, u32[]{:S(2)}) collective-permute-start(bf16[128,384]{1,0:T(8,128)(2,1)S(1)} %get-tuple-element.44), channel_id=1, source_target_pairs={{0,3},{1,2},{2,1},{3,0},{4,7},{5,6},{6,5},{7,4},{8,11},{9,10},{10,... | collective-permute-start | bytes 294920 | tf_op jit(solution)/shard_map/ppermute | solution.py:488
  80.4 5.0 %collective-permute-start.10 = (bf16[64,1024]{1,0:T(8,128)(2,1)S(1)}, bf16[64,1024]{1,0:T(8,128)(2,1)S(1)}, u32[]{:S(2)}, u32[]{:S(2)}) collective-permute-start(bf16[64,1024]{1,0:T(8,128)(2,1)S(1)} %get-tuple-element.59), channel_id=1, source_target_pairs={{0,2},{1,3},{2,0},{3,1},{4,6},{5,7},{6,4},{7,5},{8,10},{9,11},{10,... | collective-permute-start | bytes 393224 | tf_op jit(solution)/shard_map/ppermute | solution.py:488
  80.6 8.0 %collective-permute-start.11 = (bf16[64,1024]{1,0:T(8,128)(2,1)S(1)}, bf16[64,1024]{1,0:T(8,128)(2,1)S(1)}, u32[]{:S(2)}, u32[]{:S(2)}) collective-permute-start(bf16[64,1024]{1,0:T(8,128)(2,1)S(1)} %get-tuple-element.60), channel_id=1, source_target_pairs={{0,3},{1,2},{2,1},{3,0},{4,7},{5,6},{6,5},{7,4},{8,11},{9,10},{10,... | collective-permute-start | bytes 393224 | tf_op jit(solution)/shard_map/ppermute | solution.py:488
  82.4 6.2 %collective-permute-start.9 = (bf16[64,1024]{1,0:T(8,128)(2,1)S(1)}, bf16[64,1024]{1,0:T(8,128)(2,1)S(1)}, u32[]{:S(2)}, u32[]{:S(2)}) collective-permute-start(bf16[64,1024]{1,0:T(8,128)(2,1)S(1)} %get-tuple-element.58), channel_id=1, source_target_pairs={{0,1},{1,0},{2,3},{3,2},{4,5},{5,4},{6,7},{7,6},{8,9},{9,8},{10,11... | collective-permute-start | bytes 393224 | tf_op jit(solution)/shard_map/ppermute | solution.py:488

commit v6 on v5

--- a/solution.py
+++ b/solution.py
@@ -254,10 +254,34 @@
     bias_ref[...] = jnp.broadcast_to(jnp.concatenate([bias] * 4, axis=0), (256, 128))
 
 
+def lay_places(side_ref, end_ref, place_ref):
+    lane = lane_row(1024)
+    v = lane & 31
+    pos = down_col(64)
+    for ry in range(4):
+        y = ((lane >> 5) << 1) + (ry - 1)
+        side_ref[ry] = ones_where(jnp.where(v == 0, 63 - y, -1) == pos)
+        side_ref[4 + ry] = ones_where(jnp.where(v == 31, y, -1) == pos)
+    lane_e = lane_row(512)
+    inner = lane_e & 127
+    at = ((inner & 31) << 1) + (lane_e >> 7)
+    end_ref[0] = ones_where(jnp.where(inner < 32, at - 1, -1) == pos)
+    end_ref[1] = ones_where(jnp.where(inner >= 96, 64 - at, -1) == pos)
+    kk = down_col(640)
+    i, tap = kk & 63, kk >> 6
+    to = jnp.where(tap < 9, ((i >> 4) << 8) + (i & 15) * 9 + tap, -1)
+    place_ref[0:640, :] = ones_where(lane == to)
+    kk = down_col(256)
+    i, ab = kk & 63, kk >> 6
+    place_ref[640:896, :] = ones_where(lane == ((i >> 4) << 8) + 144 + (i & 15) * 4 + ab)
+
+
 def ready_body(me_ref, *refs):
     own_ref, own_raw_ref, first_refs, second_refs = refs[0], refs[1], refs[2:5], refs[5:8]
-    win_ref, w_ref, down_ref, down_t_ref, bias_ref, x_ref, raw_ref = refs[8:]
+    win_ref, w_ref, down_ref, down_t_ref, bias_ref = refs[8:13]
+    side_ref, end_ref, place_ref, x_ref, raw_ref = refs[13:]
     me = me_ref[0]
+    lay_places(side_ref, end_ref, place_ref)
     raw_ref[me] = own_raw_ref[...]
     x_ref[me] = own_ref[...]
     for d in range(1, 4):
@@ -302,8 +326,8 @@
 
 
 def level_body(me_ref, *refs):
-    in_refs, (base_ref, w_ref, down_ref, down_t_ref, bias_ref) = refs[0:4], refs[4:9]
-    out_refs, (msg_ref, sum_ref, win_ref, gc_ref) = refs[9:13], refs[13:]
+    in_refs, (base_ref, w_ref, down_ref, down_t_ref, bias_ref, side_ref, end_ref, place_ref) = refs[0:4], refs[4:12]
+    out_refs, (msg_ref, sum_ref, win_ref, gc_ref) = refs[12:16], refs[16:]
     me = me_ref[0]
     for d in range(4):
         msg_ref[me ^ d] = in_refs[d][...]
@@ -315,20 +339,12 @@
         )
 
     pixels = jnp.concatenate([msg_ref[c, 64:80, 256:384] for c in range(4)], axis=0).astype(F32)
-    lane = lane_row(1024)
-    v = lane & 31
-    pos = down_col(64)
     sides = {}
     for ry in range(4):
-        y = ((lane >> 5) << 1) + (ry - 1)
-        sides[ry, 0] = mm(strip(1), ones_where(jnp.where(v == 0, 63 - y, -1) == pos)).astype(BF)
-        sides[ry, 3] = mm(strip(3), ones_where(jnp.where(v == 31, y, -1) == pos)).astype(BF)
+        sides[ry, 0] = mm(strip(1), side_ref[ry]).astype(BF)
+        sides[ry, 3] = mm(strip(3), side_ref[4 + ry]).astype(BF)
     lane_e = lane_row(512)
-    inner = lane_e & 127
-    at = ((inner & 31) << 1) + (lane_e >> 7)
-    north = jnp.where(inner < 32, at - 1, -1)
-    south = jnp.where(inner >= 96, 64 - at, -1)
-    ends = mm(strip(0), ones_where(north == pos)) + mm(strip(2), ones_where(south == pos))
+    ends = mm(strip(0), end_ref[0]) + mm(strip(2), end_ref[1])
     gd = jnp.zeros((64, 256), F32)
     gb = jnp.zeros((256, 1), F32)
     for t in range(2):
@@ -383,14 +399,9 @@
     taps.append(jnp.zeros((64, 128), F32))
     conv = jnp.concatenate(taps, axis=0)
     conv = jnp.concatenate([conv[q * 128 : q * 128 + 128, :].T for q in range(5)], axis=1)[0:64, :]
-    kk = down_col(640)
-    cc = lane_row(1024)
-    i, tap = kk & 63, kk >> 6
-    place = ones_where(cc == jnp.where(tap < 9, ((i >> 4) << 8) + (i & 15) * 9 + tap, -1))
+    place = place_ref[0:640, :]
     conv = [mm(h, place) for h in halves(conv)]
-    kk = down_col(256)
-    i, ab = kk & 63, kk >> 6
-    place = ones_where(cc == ((i >> 4) << 8) + 144 + (i & 15) * 4 + ab)
+    place = place_ref[640:896, :]
     down = [mm(h, place) for h in halves(gd)]
     gb = gb[0:64, :] + gb[64:128, :] + gb[128:192, :] + gb[192:256, :]
     bias = [h.astype(F32) for h in halves(gb)]
@@ -501,7 +512,7 @@
     corner_turns,
     child_slot,
 ):
-    msg_spec = whole(MSG)
+    vmem = pl.BlockSpec(memory_space=pltpu.VMEM)
     msg = jax.ShapeDtypeStruct(MSG, BF)
 
     def to_nodes(x):
@@ -518,7 +529,7 @@
         [scalar, whole((128, 4096)), whole((32, 4096))]
         + [whole((4, 8))] * 4
         + [whole((1, 8)), whole((16, 576)), whole((1, 16)), whole((64, 64))],
-        (msg_spec, whole((64, 384))) + (whole((16, 5632)),) * 3 + (whole((16, 4096)),) * 3,
+        (vmem,) * 8,
         flops=10**9,
         moved=2 * 10**6,
     )(
@@ -546,14 +557,13 @@
         pick_body,
         (msg, jax.ShapeDtypeStruct((8, 512), F32)),
         (1,),
-        [msg_spec],
-        (msg_spec, whole((8, 512))),
+        [vmem],
+        (vmem, vmem),
         flops=10**9,
         moved=10**6,
     )(pieces)
     picked = to_nodes(picked)
     own = pl.BlockSpec((32, 4096), lambda i, m: (m[0], 0))
-    vmem = pl.BlockSpec(memory_space=pltpu.VMEM)
     ready = pl.pallas_call(
         ready_body,
         out_shape=(
@@ -562,12 +572,15 @@
             jax.ShapeDtypeStruct((64, 256), BF),
             jax.ShapeDtypeStruct((256, 64), BF),
             jax.ShapeDtypeStruct((256, 128), F32),
+            jax.ShapeDtypeStruct((8, 64, 1024), BF),
+            jax.ShapeDtypeStruct((2, 64, 512), BF),
+            jax.ShapeDtypeStruct((896, 1024), BF),
         ),
         grid_spec=pltpu.PrefetchScalarGridSpec(
             num_scalar_prefetch=1,
             grid=(1,),
-            in_specs=[own, whole((64, 384))] + [whole((16, 5632))] * 3 + [whole((16, 4096))] * 3,
-            out_specs=(vmem,) * 5,
+            in_specs=[own] + [vmem] * 7,
+            out_specs=(vmem,) * 8,
             scratch_shapes=(pltpu.VMEM((4, 32, 4096), BF), pltpu.VMEM((4, 64, 384), BF)),
         ),
         compiler_params=pltpu.CompilerParams(vmem_limit_bytes=32 << 20),
@@ -578,8 +591,8 @@
         regroup_body,
         (group,) * 4,
         (1,),
-        [scalar, msg_spec],
-        (whole((128, 384)),) * 4,
+        [scalar, vmem],
+        (vmem,) * 4,
         flops=4 * 10**8,
         moved=10**6,
     )(me, picked)
@@ -587,7 +600,7 @@
     local = pl.pallas_call(
         level_body,
         out_shape=(jax.ShapeDtypeStruct((64, 1024), BF),) * 4,
-        in_specs=[scalar] + [vmem] * 9,
+        in_specs=[scalar] + [vmem] * 12,
         out_specs=(vmem,) * 4,
         scratch_shapes=(
             pltpu.VMEM((4, 128, 384), BF),
@@ -603,14 +616,14 @@
         spread_body,
         msg,
         (1,),
-        [scalar] + [whole((64, 1024))] * 4,
-        msg_spec,
+        [scalar] + [vmem] * 4,
+        vmem,
         (pltpu.VMEM((4, 64, 1024), BF),),
         flops=4 * 10**8,
         moved=10**6,
     )(me, *local)
     out = to_nodes(out)
-    out = call(place_body, msg, (1,), [msg_spec, whole((8, 512))], msg_spec, flops=5 * 10**8, moved=10**6)(
+    out = call(place_body, msg, (1,), [vmem, vmem], vmem, flops=5 * 10**8, moved=10**6)(
         out, slots
     )
     out = to_nodes(out)
@@ -623,7 +636,7 @@
             jax.ShapeDtypeStruct((1, 16), F32),
         ),
         (1,),
-        [msg_spec],
+        [vmem],
         (
             whole((32, 4096)),
             whole((16, 576)),

time: 134 us -> 134 us (level)
  transfers between devices with their start and end apart: 14 -> 14, of which waited for: 7 -> 6; matrix products, arithmetic and copies ran while one was open for 0% -> 0% of each run, Pallas kernels for 2% -> 3%
where the time goes in v6:
time: 134 us; the launch traced here: 132 us
  blocking collectives  40.7 us (30%)
  starting transfers between devices  38.4 us (29%)
  waiting for transfers between devices  32.5 us (24%)
  Pallas kernels  19.6 us (15%)
    all_to_all x2, blocking collectives, to_nodes(): lax.all_to_all(x.reshape(64, 8, 384), 'tile', 0, 0, tiled=True).reshape(MSG)  40.7 us
    all_to_all x2, starting transfers between devices, to_nodes(): lax.all_to_all(x.reshape(64, 8, 384), 'tile', 0, 0, tiled=True).reshape(MSG)  26.6 us
    ppermute x12, waiting for transfers between devices, to_peers(): lax.ppermute(parts[d], 'chan', [(i, i ^ d) for i in range(4)])  20.3 us
    all_to_all x2, waiting for transfers between devices, to_nodes(): lax.all_to_all(x.reshape(64, 8, 384), 'tile', 0, 0, tiled=True).reshape(MSG)  12.2 us
    ppermute x12, starting transfers between devices, to_peers(): lax.ppermute(parts[d], 'chan', [(i, i ^ d) for i in range(4)])  11.9 us
    pallas_call x1, Pallas kernels, on_device(): pl.pallas_call(level_body, out_shape=(jax.ShapeDtypeStruct((64, 1024), BF...  6.45 us
    pallas_call x1, Pallas kernels, on_device(): call(send_body, (msg, jax.ShapeDtypeStruct((64, 384), BF)) + (first,) * 3...  3.41 us
    pallas_call x1, Pallas kernels, on_device(): pl.pallas_call(ready_body, out_shape=(jax.ShapeDtypeStruct((2, 1024, 1024...  3.29 us
  transfers between devices with their start and end apart: 14, of which 6 were waited for; matrix products, arithmetic and copies ran while one was open for 0% of the time, Pallas kernels for 3%

profile of v6, /device:TPU:1, one launch (start us, length us, event | category | flops | bytes accessed | tf_op | source)
XLA Modules:
  0.0 131.9 jit_solution(905247127759380451)
XLA Ops:
  0.6 3.4 %shard_map.129 = (bf16[512,384]{1,0:T(8,128)(2,1)}, bf16[64,384]{1,0:T(8,128)(2,1)S(1)}, bf16[16,5632]{1,0:T(8,128)(2,1)S(1)}, bf16[16,5632]{1,0:T(8,128)(2,1)S(...) custom-call(s32[1]{0:T(128)} %bitcast.me_ref, ...), custom_call_target="tpu_custom_call" | custom-call | flops 1000000000 | bytes 2000000 | tf_op jit(solution)/shard_map/pallas_call | solution.py:525
  4.0 15.2 %all-to-all-start = ((bf16[64,8,384]{2,1,0:T(8,128)(2,1)}), bf16[64,8,384]{2,1,0:T(8,128)(2,1)S(1)}, u32[]{:S(2)}, u32[]{:S(2)}) async-start(bf16[64,8,384]{2,1,0:T(8,128)(2,1)} %bitcast.9), calls=%async_computation | async-start | bytes 786432 | tf_op jit(solution)/shard_map/all_to_all | solution.py:519
  19.3 1.0 collective-permute-start
  20.8 1.3 collective-permute-start.2
  22.1 6.9 %collective-permute-done.1.refs_3_ = bf16[16,5632]{1,0:T(8,128)(2,1)S(1)} collective-permute-done((bf16[16,5632]{1,0:T(8,128)(2,1)S(1)}, bf16[16,5632]{1,0:T(8,128)(2,1)S(1)}, u32[]{:S(2)}, u32[]{:S(2)}) %collective-permute-start.1) | collective-permute-done | bytes 180256 | tf_op jit(solution)/shard_map/ppermute | solution.py:499
  28.9 5.7 %collective-permute-done.2.refs_4_ = bf16[16,5632]{1,0:T(8,128)(2,1)S(1)} collective-permute-done((bf16[16,5632]{1,0:T(8,128)(2,1)S(1)}, bf16[16,5632]{1,0:T(8,128)(2,1)S(1)}, u32[]{:S(2)}, u32[]{:S(2)}) %collective-permute-start.2) | collective-permute-done | bytes 180256 | tf_op jit(solution)/shard_map/ppermute | solution.py:499
  34.6 3.2 %shard_map.130 = (bf16[512,384]{1,0:T(8,128)(2,1)}, f32[8,512]{1,0:T(8,128)S(1)}) custom-call(bf16[512,384]{1,0:T(8,128)(2,1)S(1)} %bitcast.19), custom_call_target="tpu_custom_call" | custom-call | flops 1000000000 | bytes 1000000 | tf_op jit(solution)/shard_map/pallas_call | solution.py:556
  37.8 11.3 %all-to-all-start.1 = ((bf16[64,8,384]{2,1,0:T(8,128)(2,1)}), bf16[64,8,384]{2,1,0:T(8,128)(2,1)S(1)}, u32[]{:S(2)}, u32[]{:S(2)}) async-start(bf16[64,8,384]{2,1,0:T(8,128)(2,1)} %bitcast.11), calls=%async_computation.1 | async-start | bytes 786432 | tf_op jit(solution)/shard_map/all_to_all | solution.py:519
  49.1 0.8 collective-permute-start.6
  50.0 1.7 %collective-permute-start.8 = (bf16[16,4096]{1,0:T(8,128)(2,1)S(1)}, bf16[16,4096]{1,0:T(8,128)(2,1)S(1)}, u32[]{:S(2)}, u32[]{:S(2)}) collective-permute-start(bf16[16,4096]{1,0:T(8,128)(2,1)S(1)} %get-tuple-element.54), channel_id=1, source_target_pairs={{0,3},{1,2},{2,1},{3,0},{4,7},{5,6},{6,5},{7,4},{8,11},{9,10},{10,... | collective-permute-start | bytes 393224 | tf_op jit(solution)/shard_map/ppermute | solution.py:499
  51.6 12.2 %all-to-all-done.1 = bf16[64,8,384]{2,1,0:T(8,128)(2,1)S(1)} async-done(((bf16[64,8,384]{2,1,0:T(8,128)(2,1)}), bf16[64,8,384]{2,1,0:T(8,128)(2,1)S(1)}, u32[]{:S(2)}, u32[]{:S(2)}) %all-to-all-start.1) | async-done | bytes 393248 | tf_op jit(solution)/shard_map/all_to_all | solution.py:519
  63.8 0.5 shard_map.131
  64.3 2.9 %collective-permute-start.3 = (bf16[128,384]{1,0:T(8,128)(2,1)S(1)}, bf16[128,384]{1,0:T(8,128)(2,1)S(1)}, u32[]{:S(2)}, u32[]{:S(2)}) collective-permute-start(bf16[128,384]{1,0:T(8,128)(2,1)S(1)} %get-tuple-element.45), channel_id=1, source_target_pairs={{0,1},{1,0},{2,3},{3,2},{4,5},{5,4},{6,7},{7,6},{8,9},{9,8},{10,11... | collective-permute-start | bytes 294920 | tf_op jit(solution)/shard_map/ppermute | solution.py:499
  67.3 1.7 %collective-permute-start.5 = (bf16[128,384]{1,0:T(8,128)(2,1)S(1)}, bf16[128,384]{1,0:T(8,128)(2,1)S(1)}, u32[]{:S(2)}, u32[]{:S(2)}) collective-permute-start(bf16[128,384]{1,0:T(8,128)(2,1)S(1)} %get-tuple-element.47), channel_id=1, source_target_pairs={{0,3},{1,2},{2,1},{3,0},{4,7},{5,6},{6,5},{7,4},{8,11},{9,10},{10,... | collective-permute-start | bytes 294920 | tf_op jit(solution)/shard_map/ppermute | solution.py:499
  69.0 3.3 %shard_map.132 = (bf16[2,1024,1024]{2,1,0:T(8,128)(2,1)S(1)}, bf16[256,1024]{1,0:T(8,128)(2,1)S(1)}, bf16[64,256]{1,0:T(8,128)(2,1)S(1)}, bf16[256,64]{1,0:T(8,1...) custom-call(s32[1]{0:T(128)} %bitcast.me_ref, ...), custom_call_target="tpu_custom_call" | custom-call | flops 1000000000 | bytes 4000000 | tf_op jit(solution)/shard_map/pallas_call | solution.py:567
  72.3 1.6 %collective-permute-done.5.refs_3_ = bf16[128,384]{1,0:T(8,128)(2,1)S(1)} collective-permute-done((bf16[128,384]{1,0:T(8,128)(2,1)S(1)}, bf16[128,384]{1,0:T(8,128)(2,1)S(1)}, u32[]{:S(2)}, u32[]{:S(2)}) %collective-permute-start.5) | collective-permute-done | bytes 98336 | tf_op jit(solution)/shard_map/ppermute | solution.py:499
  73.9 6.5 %shard_map.133 = (bf16[64,1024]{1,0:T(8,128)(2,1)S(1)}, bf16[64,1024]{1,0:T(8,128)(2,1)S(1)}, bf16[64,1024]{1,0:T(8,128)(2,1)S(1)}, bf16[64,1024]{1,0:T(8,128)(2,1)S(1)}) custom-call(s32[1]{0:T(128)} %bitcast.me_ref, bf16[128,384]{1,0:T(8,128)(2,1)S(1)} %get-tuple-element.44.refs_0_, bf16[128,384]{1,0:T(8,128)(2,1)S(1)} %collective-permute-done.3.refs_1_, ...), custom_call_target="tpu_custom_call" | custom-call | flops 4000000000 | bytes 4000000 | tf_op jit(solution)/shard_map/pallas_call | solution.py:600
  80.5 1.8 %collective-permute-start.11 = (bf16[64,1024]{1,0:T(8,128)(2,1)S(1)}, bf16[64,1024]{1,0:T(8,128)(2,1)S(1)}, u32[]{:S(2)}, u32[]{:S(2)}) collective-permute-start(bf16[64,1024]{1,0:T(8,128)(2,1)S(1)} %get-tuple-element.66), channel_id=1, source_target_pairs={{0,3},{1,2},{2,1},{3,0},{4,7},{5,6},{6,5},{7,4},{8,11},{9,10},{10,... | collective-permute-start | bytes 393224 | tf_op jit(solution)/shard_map/ppermute | solution.py:499
  82.3 3.0 %collective-permute-done.10.refs_2_ = bf16[64,1024]{1,0:T(8,128)(2,1)S(1)} collective-permute-done((bf16[64,1024]{1,0:T(8,128)(2,1)S(1)}, bf16[64,1024]{1,0:T(8,128)(2,1)S(1)}, u32[]{:S(2)}, u32[]{:S(2)}) %collective-permute-start.10) | collective-permute-done | bytes 131104 | tf_op jit(solution)/shard_map/ppermute | solution.py:499
  85.3 3.1 %collective-permute-done.11.refs_3_ = bf16[64,1024]{1,0:T(8,128)(2,1)S(1)} collective-permute-done((bf16[64,1024]{1,0:T(8,128)(2,1)S(1)}, bf16[64,1024]{1,0:T(8,128)(2,1)S(1)}, u32[]{:S(2)}, u32[]{:S(2)}) %collective-permute-start.11) | collective-permute-done | bytes 131104 | tf_op jit(solution)/shard_map/ppermute | solution.py:499
  89.0 20.3 %all_to_all.20 = bf16[64,8,384]{2,1,0:T(8,128)(2,1)S(1)} all-to-all(bf16[64,8,384]{2,1,0:T(8,128)(2,1)S(1)} %bitcast.21), channel_id=1, replica_groups=mesh['tile'=64,'chan'=4] {'tile'}, dimensions={0} | all-to-all | bytes 786432 | tf_op jit(solution)/shard_map/all_to_all | solution.py:519
  109.3 0.8 shard_map.135
  110.1 20.4 %all_to_all.21 = bf16[64,8,384]{2,1,0:T(8,128)(2,1)S(1)} all-to-all(bf16[64,8,384]{2,1,0:T(8,128)(2,1)S(1)} %bitcast.24), channel_id=1, replica_groups=mesh['tile'=64,'chan'=4] {'tile'}, dimensions={0} | all-to-all | bytes 786432 | tf_op jit(solution)/shard_map/all_to_all | solution.py:519
  130.5 1.4 %shard_map.136 = (bf16[32,4096]{1,0:T(8,128)(2,1)}, f32[16,576]{1,0:T(8,128)}, f32[64,64]{1,0:T(8,128)}, f32[1,16]{1,0:T(1,128)}) custom-call(bf16[512,384]{1,0:T(8,128)(2,1)S(1)} %bitcast.22), custom_call_target="tpu_custom_call" | custom-call | flops 400000000 | bytes 1000000 | tf_op jit(solution)/shard_map/pallas_call | solution.py:630
  (16 shorter events, 1.2 us)
Async XLA Ops:
  4.0 65.0 %copy-start = (bf16[8,16,4096]{2,1,0:T(8,128)(2,1)S(1)}, bf16[8,16,4096]{2,1,0:T(8,128)(2,1)}, u32[]{:S(2)}) copy-start(bf16[8,16,4096]{2,1,0:T(8,128)(2,1)} %param.10) | copy-start | bytes 3145732
  4.0 30.5 %all-to-all-start = ((bf16[64,8,384]{2,1,0:T(8,128)(2,1)}), bf16[64,8,384]{2,1,0:T(8,128)(2,1)S(1)}, u32[]{:S(2)}, u32[]{:S(2)}) async-start(bf16[64,8,384]{2,1,0:T(8,128)(2,1)} %bitcast.9), calls=%async_computation | async-start | bytes 786432 | tf_op jit(solution)/shard_map/all_to_all | solution.py:519
  19.3 2.8 %collective-permute-start = (bf16[16,5632]{1,0:T(8,128)(2,1)S(1)}, bf16[16,5632]{1,0:T(8,128)(2,1)S(1)}, u32[]{:S(2)}, u32[]{:S(2)}) collective-permute-start(bf16[16,5632]{1,0:T(8,128)(2,1)S(1)} %get-tuple-element.39), channel_id=1, source_target_pairs={{0,1},{1,0},{2,3},{3,2},{4,5},{5,4},{6,7},{7,6},{8,9},{9,8},{10,11... | collective-permute-start | bytes 540680 | tf_op jit(solution)/shard_map/ppermute | solution.py:499
  20.3 8.6 %collective-permute-start.1 = (bf16[16,5632]{1,0:T(8,128)(2,1)S(1)}, bf16[16,5632]{1,0:T(8,128)(2,1)S(1)}, u32[]{:S(2)}, u32[]{:S(2)}) collective-permute-start(bf16[16,5632]{1,0:T(8,128)(2,1)S(1)} %get-tuple-element.40), channel_id=1, source_target_pairs={{0,2},{1,3},{2,0},{3,1},{4,6},{5,7},{6,4},{7,5},{8,10},{9,11},{10,... | collective-permute-start | bytes 540680 | tf_op jit(solution)/shard_map/ppermute | solution.py:499
  20.8 13.8 %collective-permute-start.2 = (bf16[16,5632]{1,0:T(8,128)(2,1)S(1)}, bf16[16,5632]{1,0:T(8,128)(2,1)S(1)}, u32[]{:S(2)}, u32[]{:S(2)}) collective-permute-start(bf16[16,5632]{1,0:T(8,128)(2,1)S(1)} %get-tuple-element.41), channel_id=1, source_target_pairs={{0,3},{1,2},{2,1},{3,0},{4,7},{5,6},{6,5},{7,4},{8,11},{9,10},{10,... | collective-permute-start | bytes 540680 | tf_op jit(solution)/shard_map/ppermute | solution.py:499
  37.8 26.0 %all-to-all-start.1 = ((bf16[64,8,384]{2,1,0:T(8,128)(2,1)}), bf16[64,8,384]{2,1,0:T(8,128)(2,1)S(1)}, u32[]{:S(2)}, u32[]{:S(2)}) async-start(bf16[64,8,384]{2,1,0:T(8,128)(2,1)} %bitcast.11), calls=%async_computation.1 | async-start | bytes 786432 | tf_op jit(solution)/shard_map/all_to_all | solution.py:519
  49.1 18.2 %collective-permute-start.6 = (bf16[16,4096]{1,0:T(8,128)(2,1)S(1)}, bf16[16,4096]{1,0:T(8,128)(2,1)S(1)}, u32[]{:S(2)}, u32[]{:S(2)}) collective-permute-start(bf16[16,4096]{1,0:T(8,128)(2,1)S(1)} %get-tuple-element.52), channel_id=1, source_target_pairs={{0,1},{1,0},{2,3},{3,2},{4,5},{5,4},{6,7},{7,6},{8,9},{9,8},{10,11... | collective-permute-start | bytes 393224 | tf_op jit(solution)/shard_map/ppermute | solution.py:499
  49.9 19.1 %collective-permute-start.7 = (bf16[16,4096]{1,0:T(8,128)(2,1)S(1)}, bf16[16,4096]{1,0:T(8,128)(2,1)S(1)}, u32[]{:S(2)}, u32[]{:S(2)}) collective-permute-start(bf16[16,4096]{1,0:T(8,128)(2,1)S(1)} %get-tuple-element.53), channel_id=1, source_target_pairs={{0,2},{1,3},{2,0},{3,1},{4,6},{5,7},{6,4},{7,5},{8,10},{9,11},{10,... | collective-permute-start | bytes 393224 | tf_op jit(solution)/shard_map/ppermute | solution.py:499
  50.0 19.0 %collective-permute-start.8 = (bf16[16,4096]{1,0:T(8,128)(2,1)S(1)}, bf16[16,4096]{1,0:T(8,128)(2,1)S(1)}, u32[]{:S(2)}, u32[]{:S(2)}) collective-permute-start(bf16[16,4096]{1,0:T(8,128)(2,1)S(1)} %get-tuple-element.54), channel_id=1, source_target_pairs={{0,3},{1,2},{2,1},{3,0},{4,7},{5,6},{6,5},{7,4},{8,11},{9,10},{10,... | collective-permute-start | bytes 393224 | tf_op jit(solution)/shard_map/ppermute | solution.py:499
  64.3 8.0 %collective-permute-start.3 = (bf16[128,384]{1,0:T(8,128)(2,1)S(1)}, bf16[128,384]{1,0:T(8,128)(2,1)S(1)}, u32[]{:S(2)}, u32[]{:S(2)}) collective-permute-start(bf16[128,384]{1,0:T(8,128)(2,1)S(1)} %get-tuple-element.45), channel_id=1, source_target_pairs={{0,1},{1,0},{2,3},{3,2},{4,5},{5,4},{6,7},{7,6},{8,9},{9,8},{10,11... | collective-permute-start | bytes 294920 | tf_op jit(solution)/shard_map/ppermute | solution.py:499
  67.3 5.1 %collective-permute-start.4 = (bf16[128,384]{1,0:T(8,128)(2,1)S(1)}, bf16[128,384]{1,0:T(8,128)(2,1)S(1)}, u32[]{:S(2)}, u32[]{:S(2)}) collective-permute-start(bf16[128,384]{1,0:T(8,128)(2,1)S(1)} %get-tuple-element.46), channel_id=1, source_target_pairs={{0,2},{1,3},{2,0},{3,1},{4,6},{5,7},{6,4},{7,5},{8,10},{9,11},{10,... | collective-permute-start | bytes 294920 | tf_op jit(solution)/shard_map/ppermute | solution.py:499
  67.3 6.6 %collective-permute-start.5 = (bf16[128,384]{1,0:T(8,128)(2,1)S(1)}, bf16[128,384]{1,0:T(8,128)(2,1)S(1)}, u32[]{:S(2)}, u32[]{:S(2)}) collective-permute-start(bf16[128,384]{1,0:T(8,128)(2,1)S(1)} %get-tuple-element.47), channel_id=1, source_target_pairs={{0,3},{1,2},{2,1},{3,0},{4,7},{5,6},{6,5},{7,4},{8,11},{9,10},{10,... | collective-permute-start | bytes 294920 | tf_op jit(solution)/shard_map/ppermute | solution.py:499
  80.4 5.0 %collective-permute-start.10 = (bf16[64,1024]{1,0:T(8,128)(2,1)S(1)}, bf16[64,1024]{1,0:T(8,128)(2,1)S(1)}, u32[]{:S(2)}, u32[]{:S(2)}) collective-permute-start(bf16[64,1024]{1,0:T(8,128)(2,1)S(1)} %get-tuple-element.65), channel_id=1, source_target_pairs={{0,2},{1,3},{2,0},{3,1},{4,6},{5,7},{6,4},{7,5},{8,10},{9,11},{10,... | collective-permute-start | bytes 393224 | tf_op jit(solution)/shard_map/ppermute | solution.py:499
  80.5 8.0 %collective-permute-start.11 = (bf16[64,1024]{1,0:T(8,128)(2,1)S(1)}, bf16[64,1024]{1,0:T(8,128)(2,1)S(1)}, u32[]{:S(2)}, u32[]{:S(2)}) collective-permute-start(bf16[64,1024]{1,0:T(8,128)(2,1)S(1)} %get-tuple-element.66), channel_id=1, source_target_pairs={{0,3},{1,2},{2,1},{3,0},{4,7},{5,6},{6,5},{7,4},{8,11},{9,10},{10,... | collective-permute-start | bytes 393224 | tf_op jit(solution)/shard_map/ppermute | solution.py:499
  82.3 6.2 %collective-permute-start.9 = (bf16[64,1024]{1,0:T(8,128)(2,1)S(1)}, bf16[64,1024]{1,0:T(8,128)(2,1)S(1)}, u32[]{:S(2)}, u32[]{:S(2)}) collective-permute-start(bf16[64,1024]{1,0:T(8,128)(2,1)S(1)} %get-tuple-element.64), channel_id=1, source_target_pairs={{0,1},{1,0},{2,3},{3,2},{4,5},{5,4},{6,7},{7,6},{8,9},{9,8},{10,11... | collective-permute-start | bytes 393224 | tf_op jit(solution)/shard_map/ppermute | solution.py:499

commit v7 on v6

--- a/solution.py
+++ b/solution.py
@@ -98,10 +98,10 @@
     for d in range(1, 4):
         peer = me_ref[0] ^ d
         first_ref, second_ref = peer_refs[d - 1], peer_refs[d + 2]
-        first_ref[:, 0:4096] = feat_ref[pl.ds(pl.multiple_of(peer * 32, 16), 16), :]
-        second_ref[...] = feat_ref[pl.ds(pl.multiple_of(peer * 32 + 16, 16), 16), :]
+        first_ref[...] = feat_ref[pl.ds(pl.multiple_of(peer * 32, 16), 16), :]
+        second_ref[:, 0:4096] = feat_ref[pl.ds(pl.multiple_of(peer * 32 + 16, 16), 16), :]
         for q in range(4):
-            first_ref[:, 4096 + q * 384 : 4480 + q * 384] = raw_ref[q * 16 : q * 16 + 16, :]
+            second_ref[:, 4096 + q * 384 : 4480 + q * 384] = raw_ref[q * 16 : q * 16 + 16, :]
 
     cot = cot_ref[...]
     stack = jnp.concatenate([cot[:, q * 256 : q * 256 + 256] for q in range(16)], axis=0)
@@ -254,42 +254,41 @@
     bias_ref[...] = jnp.broadcast_to(jnp.concatenate([bias] * 4, axis=0), (256, 128))
 
 
-def lay_places(side_ref, end_ref, place_ref):
+def lay_places(side_ref, end_ref, conv_place_ref, down_place_ref):
     lane = lane_row(1024)
     v = lane & 31
     pos = down_col(64)
     for ry in range(4):
         y = ((lane >> 5) << 1) + (ry - 1)
-        side_ref[ry] = ones_where(jnp.where(v == 0, 63 - y, -1) == pos)
-        side_ref[4 + ry] = ones_where(jnp.where(v == 31, y, -1) == pos)
+        side_ref[ry, 0:64, :] = ones_where(jnp.where(v == 0, 63 - y, -1) == pos)
+        side_ref[ry, 64:128, :] = ones_where(jnp.where(v == 31, y, -1) == pos)
     lane_e = lane_row(512)
     inner = lane_e & 127
     at = ((inner & 31) << 1) + (lane_e >> 7)
-    end_ref[0] = ones_where(jnp.where(inner < 32, at - 1, -1) == pos)
-    end_ref[1] = ones_where(jnp.where(inner >= 96, 64 - at, -1) == pos)
-    kk = down_col(640)
-    i, tap = kk & 63, kk >> 6
-    to = jnp.where(tap < 9, ((i >> 4) << 8) + (i & 15) * 9 + tap, -1)
-    place_ref[0:640, :] = ones_where(lane == to)
+    end_ref[0:64, :] = ones_where(jnp.where(inner < 32, at - 1, -1) == pos)
+    end_ref[64:128, :] = ones_where(jnp.where(inner >= 96, 64 - at, -1) == pos)
+    kk = down_col(256)
+    to = jnp.where(kk < 144, (kk & 15) * 9 + (kk >> 4), -1)
+    conv_place_ref[...] = ones_where(lane_row(256) == to)
     kk = down_col(256)
     i, ab = kk & 63, kk >> 6
-    place_ref[640:896, :] = ones_where(lane == ((i >> 4) << 8) + 144 + (i & 15) * 4 + ab)
+    down_place_ref[...] = ones_where(lane == ((i >> 4) << 8) + 144 + (i & 15) * 4 + ab)
 
 
 def ready_body(me_ref, *refs):
     own_ref, own_raw_ref, first_refs, second_refs = refs[0], refs[1], refs[2:5], refs[5:8]
     win_ref, w_ref, down_ref, down_t_ref, bias_ref = refs[8:13]
-    side_ref, end_ref, place_ref, x_ref, raw_ref = refs[13:]
+    side_ref, end_ref, conv_place_ref, down_place_ref, x_ref, raw_ref = refs[13:]
     me = me_ref[0]
-    lay_places(side_ref, end_ref, place_ref)
+    lay_places(side_ref, end_ref, conv_place_ref, down_place_ref)
     raw_ref[me] = own_raw_ref[...]
     x_ref[me] = own_ref[...]
     for d in range(1, 4):
-        first_ref = first_refs[d - 1]
-        x_ref[me ^ d, 0:16, :] = first_ref[:, 0:4096]
-        x_ref[me ^ d, 16:32, :] = second_refs[d - 1][...]
+        second_ref = second_refs[d - 1]
+        x_ref[me ^ d, 0:16, :] = first_refs[d - 1][...]
+        x_ref[me ^ d, 16:32, :] = second_ref[:, 0:4096]
         for q in range(4):
-            raw_ref[me ^ d, q * 16 : q * 16 + 16, :] = first_ref[:, 4096 + q * 384 : 4480 + q * 384]
+            raw_ref[me ^ d, q * 16 : q * 16 + 16, :] = second_ref[:, 4096 + q * 384 : 4480 + q * 384]
     lay_weights(raw_ref, w_ref, down_ref, down_t_ref, bias_ref)
     l_in = down_col(512)
     to = (((l_in >> 6) & 1) << 8) | ((l_in & 1) << 7) | ((l_in >> 7) << 5) | ((l_in >> 1) & 31)
@@ -326,8 +325,9 @@
 
 
 def level_body(me_ref, *refs):
-    in_refs, (base_ref, w_ref, down_ref, down_t_ref, bias_ref, side_ref, end_ref, place_ref) = refs[0:4], refs[4:12]
-    out_refs, (msg_ref, sum_ref, win_ref, gc_ref) = refs[12:16], refs[16:]
+    in_refs, (base_ref, w_ref, down_ref, down_t_ref, bias_ref) = refs[0:4], refs[4:9]
+    side_ref, end_ref, conv_place_ref, down_place_ref = refs[9:13]
+    out_refs, (msg_ref, sum_ref, win_ref, gc_ref) = refs[13:17], refs[17:]
     me = me_ref[0]
     for d in range(4):
         msg_ref[me ^ d] = in_refs[d][...]
@@ -340,11 +340,14 @@
 
     pixels = jnp.concatenate([msg_ref[c, 64:80, 256:384] for c in range(4)], axis=0).astype(F32)
     sides = {}
+    v = lane_row(1024) & 31
+    west_east = jnp.concatenate([strip(1), strip(3)], axis=1)
     for ry in range(4):
-        sides[ry, 0] = mm(strip(1), side_ref[ry]).astype(BF)
-        sides[ry, 3] = mm(strip(3), side_ref[4 + ry]).astype(BF)
+        both = mm(west_east, side_ref[ry])
+        sides[ry, 0] = keep(v == 0, both)
+        sides[ry, 3] = keep(v == 31, both)
     lane_e = lane_row(512)
-    ends = mm(strip(0), end_ref[0]) + mm(strip(2), end_ref[1])
+    ends = mm(jnp.concatenate([strip(0), strip(2)], axis=1), end_ref[...])
     gd = jnp.zeros((64, 256), F32)
     gb = jnp.zeros((256, 1), F32)
     for t in range(2):
@@ -396,22 +399,27 @@
     for dy in range(3):
         for dx in range(3):
             taps.append(rows[dy * 4 + dx] + pltpu.roll(rows[dy * 4 + dx + 1], 64, axis=1))
-    taps.append(jnp.zeros((64, 128), F32))
-    conv = jnp.concatenate(taps, axis=0)
-    conv = jnp.concatenate([conv[q * 128 : q * 128 + 128, :].T for q in range(5)], axis=1)[0:64, :]
-    place = place_ref[0:640, :]
-    conv = [mm(h, place) for h in halves(conv)]
-    place = place_ref[640:896, :]
-    down = [mm(h, place) for h in halves(gd)]
+    groups = []
+    for q in range(4):
+        rows = jnp.concatenate(
+            [tap[q * 16 : q * 16 + 16, :] for tap in taps] + [jnp.zeros((112, 128), F32)], axis=0
+        )
+        groups.append(jnp.concatenate([rows[0:128].T, rows[128:256].T], axis=1)[0:64, :])
+    conv = mm(jnp.concatenate(halves(jnp.concatenate(groups, axis=0)), axis=0), conv_place_ref[...])
+    down = mm(jnp.concatenate(halves(gd), axis=0), down_place_ref[...])
     gb = gb[0:64, :] + gb[64:128, :] + gb[128:192, :] + gb[192:256, :]
     bias = [h.astype(F32) for h in halves(gb)]
     lane16 = lane_row(1024)
     for part in range(2):
         for c in range(4):
-            d = jnp.concatenate(
-                [down[part][s * 16 : s * 16 + 16, c * 256 : c * 256 + 256] for s in range(4)], axis=1
+            both = jnp.concatenate(
+                [
+                    conv[part * 256 + q * 64 + c * 16 : part * 256 + q * 64 + c * 16 + 16, :]
+                    + down[part * 64 + q * 16 : part * 64 + q * 16 + 16, c * 256 : c * 256 + 256]
+                    for q in range(4)
+                ],
+                axis=1,
             )
-            both = conv[part][c * 16 : c * 16 + 16, :] + d
             both = jnp.where(lane16 == 208, bias[part][c * 16 : c * 16 + 16, :], both)
             sum_ref[c, 32 + part * 16 : 48 + part * 16, :] = both.astype(BF)
     for d in range(4):
@@ -520,8 +528,8 @@
 
     me = lax.axis_index("chan").astype(jnp.int32).reshape(1)
     scalar = pl.BlockSpec(memory_space=pltpu.SMEM)
-    first = jax.ShapeDtypeStruct((16, 5632), BF)
-    second = jax.ShapeDtypeStruct((16, 4096), BF)
+    first = jax.ShapeDtypeStruct((16, 4096), BF)
+    second = jax.ShapeDtypeStruct((16, 5632), BF)
     pieces, raw, *peers = call(
         send_body,
         (msg, jax.ShapeDtypeStruct((64, 384), BF)) + (first,) * 3 + (second,) * 3,
@@ -572,15 +580,16 @@
             jax.ShapeDtypeStruct((64, 256), BF),
             jax.ShapeDtypeStruct((256, 64), BF),
             jax.ShapeDtypeStruct((256, 128), F32),
-            jax.ShapeDtypeStruct((8, 64, 1024), BF),
-            jax.ShapeDtypeStruct((2, 64, 512), BF),
-            jax.ShapeDtypeStruct((896, 1024), BF),
+            jax.ShapeDtypeStruct((4, 128, 1024), BF),
+            jax.ShapeDtypeStruct((128, 512), BF),
+            jax.ShapeDtypeStruct((256, 256), BF),
+            jax.ShapeDtypeStruct((256, 1024), BF),
         ),
         grid_spec=pltpu.PrefetchScalarGridSpec(
             num_scalar_prefetch=1,
             grid=(1,),
             in_specs=[own] + [vmem] * 7,
-            out_specs=(vmem,) * 8,
+            out_specs=(vmem,) * 9,
             scratch_shapes=(pltpu.VMEM((4, 32, 4096), BF), pltpu.VMEM((4, 64, 384), BF)),
         ),
         compiler_params=pltpu.CompilerParams(vmem_limit_bytes=32 << 20),
@@ -600,7 +609,7 @@
     local = pl.pallas_call(
         level_body,
         out_shape=(jax.ShapeDtypeStruct((64, 1024), BF),) * 4,
-        in_specs=[scalar] + [vmem] * 12,
+        in_specs=[scalar] + [vmem] * 13,
         out_specs=(vmem,) * 4,
         scratch_shapes=(
             pltpu.VMEM((4, 128, 384), BF),

time: 134 us -> 132 us (0.985)
    ppermute x12, waiting for transfers between devices: 20.3 us -> 18.2 us  [to_peers(): lax.ppermute(parts[d], 'chan', [(i, i ^ d) for i in range(4)])]
    all_to_all x2, waiting for transfers between devices: 12.2 us -> 13.6 us  [to_nodes(): lax.all_to_all(x.reshape(64, 8, 384), 'tile', 0, 0, tiled=True).reshape(MSG)]
  transfers between devices with their start and end apart: 14 -> 14, of which waited for: 6 -> 7; matrix products, arithmetic and copies ran while one was open for 0% -> 0% of each run, Pallas kernels for 3% -> 3%
where the time goes in v7:
time: 132 us; the launch traced here: 130 us
  blocking collectives  41.1 us (31%)
  starting transfers between devices  37.3 us (28%)
  waiting for transfers between devices  31.8 us (24%)
  Pallas kernels  18.7 us (14%)
    all_to_all x2, blocking collectives, to_nodes(): lax.all_to_all(x.reshape(64, 8, 384), 'tile', 0, 0, tiled=True).reshape(MSG)  41.1 us
    all_to_all x2, starting transfers between devices, to_nodes(): lax.all_to_all(x.reshape(64, 8, 384), 'tile', 0, 0, tiled=True).reshape(MSG)  25.4 us
    ppermute x12, waiting for transfers between devices, to_peers(): lax.ppermute(parts[d], 'chan', [(i, i ^ d) for i in range(4)])  18.2 us
    all_to_all x2, waiting for transfers between devices, to_nodes(): lax.all_to_all(x.reshape(64, 8, 384), 'tile', 0, 0, tiled=True).reshape(MSG)  13.6 us
    ppermute x12, starting transfers between devices, to_peers(): lax.ppermute(parts[d], 'chan', [(i, i ^ d) for i in range(4)])  11.9 us
    pallas_call x1, Pallas kernels, on_device(): pl.pallas_call(level_body, out_shape=(jax.ShapeDtypeStruct((64, 1024), BF...  5.87 us
    pallas_call x1, Pallas kernels, on_device(): call(send_body, (msg, jax.ShapeDtypeStruct((64, 384), BF)) + (first,) * 3...  3.41 us
    pallas_call x1, Pallas kernels, on_device(): call(pick_body, (msg, jax.ShapeDtypeStruct((8, 512), F32)), (1,), [vmem],...  3.23 us
  transfers between devices with their start and end apart: 14, of which 7 were waited for; matrix products, arithmetic and copies ran while one was open for 0% of the time, Pallas kernels for 3%

profile of v7, /device:TPU:1, one launch (start us, length us, event | category | flops | bytes accessed | tf_op | source)
XLA Modules:
  0.0 129.7 jit_solution(8663123364334877651)
XLA Ops:
  0.6 3.4 %shard_map.129 = (bf16[512,384]{1,0:T(8,128)(2,1)}, bf16[64,384]{1,0:T(8,128)(2,1)S(1)}, bf16[16,4096]{1,0:T(8,128)(2,1)S(1)}, bf16[16,4096]{1,0:T(8,128)(2,1)S(...) custom-call(s32[1]{0:T(128)} %bitcast.me_ref, ...), custom_call_target="tpu_custom_call" | custom-call | flops 1000000000 | bytes 2000000 | tf_op jit(solution)/shard_map/pallas_call | solution.py:533
  4.0 15.2 %all-to-all-start = ((bf16[64,8,384]{2,1,0:T(8,128)(2,1)}), bf16[64,8,384]{2,1,0:T(8,128)(2,1)S(1)}, u32[]{:S(2)}, u32[]{:S(2)}) async-start(bf16[64,8,384]{2,1,0:T(8,128)(2,1)} %bitcast.9), calls=%async_computation | async-start | bytes 786432 | tf_op jit(solution)/shard_map/all_to_all | solution.py:527
  19.3 1.0 collective-permute-start
  20.8 1.3 %collective-permute-start.2 = (bf16[16,4096]{1,0:T(8,128)(2,1)S(1)}, bf16[16,4096]{1,0:T(8,128)(2,1)S(1)}, u32[]{:S(2)}, u32[]{:S(2)}) collective-permute-start(bf16[16,4096]{1,0:T(8,128)(2,1)S(1)} %get-tuple-element.42), channel_id=1, source_target_pairs={{0,3},{1,2},{2,1},{3,0},{4,7},{5,6},{6,5},{7,4},{8,11},{9,10},{10,... | collective-permute-start | bytes 393224 | tf_op jit(solution)/shard_map/ppermute | solution.py:507
  22.1 4.8 %collective-permute-done.1.refs_3_ = bf16[16,4096]{1,0:T(8,128)(2,1)S(1)} collective-permute-done((bf16[16,4096]{1,0:T(8,128)(2,1)S(1)}, bf16[16,4096]{1,0:T(8,128)(2,1)S(1)}, u32[]{:S(2)}, u32[]{:S(2)}) %collective-permute-start.1) | collective-permute-done | bytes 131104 | tf_op jit(solution)/shard_map/ppermute | solution.py:507
  26.9 5.3 %collective-permute-done.2.refs_4_ = bf16[16,4096]{1,0:T(8,128)(2,1)S(1)} collective-permute-done((bf16[16,4096]{1,0:T(8,128)(2,1)S(1)}, bf16[16,4096]{1,0:T(8,128)(2,1)S(1)}, u32[]{:S(2)}, u32[]{:S(2)}) %collective-permute-start.2) | collective-permute-done | bytes 131104 | tf_op jit(solution)/shard_map/ppermute | solution.py:507
  32.2 1.4 %all-to-all-done = bf16[64,8,384]{2,1,0:T(8,128)(2,1)S(1)} async-done(((bf16[64,8,384]{2,1,0:T(8,128)(2,1)}), bf16[64,8,384]{2,1,0:T(8,128)(2,1)S(1)}, u32[]{:S(2)}, u32[]{:S(2)}) %all-to-all-start) | async-done | bytes 393248 | tf_op jit(solution)/shard_map/all_to_all | solution.py:527
  33.6 3.2 %shard_map.130 = (bf16[512,384]{1,0:T(8,128)(2,1)}, f32[8,512]{1,0:T(8,128)S(1)}) custom-call(bf16[512,384]{1,0:T(8,128)(2,1)S(1)} %bitcast.19), custom_call_target="tpu_custom_call" | custom-call | flops 1000000000 | bytes 1000000 | tf_op jit(solution)/shard_map/pallas_call | solution.py:564
  36.9 10.2 %all-to-all-start.1 = ((bf16[64,8,384]{2,1,0:T(8,128)(2,1)}), bf16[64,8,384]{2,1,0:T(8,128)(2,1)S(1)}, u32[]{:S(2)}, u32[]{:S(2)}) async-start(bf16[64,8,384]{2,1,0:T(8,128)(2,1)} %bitcast.11), calls=%async_computation.1 | async-start | bytes 786432 | tf_op jit(solution)/shard_map/all_to_all | solution.py:527
  47.0 0.8 collective-permute-start.6
  47.9 1.7 %collective-permute-start.8 = (bf16[16,5632]{1,0:T(8,128)(2,1)S(1)}, bf16[16,5632]{1,0:T(8,128)(2,1)S(1)}, u32[]{:S(2)}, u32[]{:S(2)}) collective-permute-start(bf16[16,5632]{1,0:T(8,128)(2,1)S(1)} %get-tuple-element.55), channel_id=1, source_target_pairs={{0,3},{1,2},{2,1},{3,0},{4,7},{5,6},{6,5},{7,4},{8,11},{9,10},{10,... | collective-permute-start | bytes 540680 | tf_op jit(solution)/shard_map/ppermute | solution.py:507
  49.5 12.2 %all-to-all-done.1 = bf16[64,8,384]{2,1,0:T(8,128)(2,1)S(1)} async-done(((bf16[64,8,384]{2,1,0:T(8,128)(2,1)}), bf16[64,8,384]{2,1,0:T(8,128)(2,1)S(1)}, u32[]{:S(2)}, u32[]{:S(2)}) %all-to-all-start.1) | async-done | bytes 393248 | tf_op jit(solution)/shard_map/all_to_all | solution.py:527
  62.3 2.9 %collective-permute-start.3 = (bf16[128,384]{1,0:T(8,128)(2,1)S(1)}, bf16[128,384]{1,0:T(8,128)(2,1)S(1)}, u32[]{:S(2)}, u32[]{:S(2)}) collective-permute-start(bf16[128,384]{1,0:T(8,128)(2,1)S(1)} %get-tuple-element.46), channel_id=1, source_target_pairs={{0,1},{1,0},{2,3},{3,2},{4,5},{5,4},{6,7},{7,6},{8,9},{9,8},{10,11... | collective-permute-start | bytes 294920 | tf_op jit(solution)/shard_map/ppermute | solution.py:507
  65.2 1.7 %collective-permute-start.5 = (bf16[128,384]{1,0:T(8,128)(2,1)S(1)}, bf16[128,384]{1,0:T(8,128)(2,1)S(1)}, u32[]{:S(2)}, u32[]{:S(2)}) collective-permute-start(bf16[128,384]{1,0:T(8,128)(2,1)S(1)} %get-tuple-element.48), channel_id=1, source_target_pairs={{0,3},{1,2},{2,1},{3,0},{4,7},{5,6},{6,5},{7,4},{8,11},{9,10},{10,... | collective-permute-start | bytes 294920 | tf_op jit(solution)/shard_map/ppermute | solution.py:507
  66.9 2.9 %shard_map.132 = (bf16[2,1024,1024]{2,1,0:T(8,128)(2,1)S(1)}, bf16[256,1024]{1,0:T(8,128)(2,1)S(1)}, bf16[64,256]{1,0:T(8,128)(2,1)S(1)}, bf16[256,64]{1,0:T(8,1...) custom-call(s32[1]{0:T(128)} %bitcast.me_ref, ...), custom_call_target="tpu_custom_call" | custom-call | flops 1000000000 | bytes 4000000 | tf_op jit(solution)/shard_map/pallas_call | solution.py:575
  69.9 1.9 %collective-permute-done.5.refs_3_ = bf16[128,384]{1,0:T(8,128)(2,1)S(1)} collective-permute-done((bf16[128,384]{1,0:T(8,128)(2,1)S(1)}, bf16[128,384]{1,0:T(8,128)(2,1)S(1)}, u32[]{:S(2)}, u32[]{:S(2)}) %collective-permute-start.5) | collective-permute-done | bytes 98336 | tf_op jit(solution)/shard_map/ppermute | solution.py:507
  71.8 5.9 %shard_map.133 = (bf16[64,1024]{1,0:T(8,128)(2,1)S(1)}, bf16[64,1024]{1,0:T(8,128)(2,1)S(1)}, bf16[64,1024]{1,0:T(8,128)(2,1)S(1)}, bf16[64,1024]{1,0:T(8,128)(2,1)S(1)}) custom-call(s32[1]{0:T(128)} %bitcast.me_ref, bf16[128,384]{1,0:T(8,128)(2,1)S(1)} %get-tuple-element.45.refs_0_, bf16[128,384]{1,0:T(8,128)(2,1)S(1)} %collective-permute-done.3.refs_1_, ...), custom_call_target="tpu_custom_call" | custom-call | flops 4000000000 | bytes 4000000 | tf_op jit(solution)/shard_map/pallas_call | solution.py:609
  77.8 1.8 %collective-permute-start.11 = (bf16[64,1024]{1,0:T(8,128)(2,1)S(1)}, bf16[64,1024]{1,0:T(8,128)(2,1)S(1)}, u32[]{:S(2)}, u32[]{:S(2)}) collective-permute-start(bf16[64,1024]{1,0:T(8,128)(2,1)S(1)} %get-tuple-element.68), channel_id=1, source_target_pairs={{0,3},{1,2},{2,1},{3,0},{4,7},{5,6},{6,5},{7,4},{8,11},{9,10},{10,... | collective-permute-start | bytes 393224 | tf_op jit(solution)/shard_map/ppermute | solution.py:507
  79.7 3.0 %collective-permute-done.10.refs_2_ = bf16[64,1024]{1,0:T(8,128)(2,1)S(1)} collective-permute-done((bf16[64,1024]{1,0:T(8,128)(2,1)S(1)}, bf16[64,1024]{1,0:T(8,128)(2,1)S(1)}, u32[]{:S(2)}, u32[]{:S(2)}) %collective-permute-start.10) | collective-permute-done | bytes 131104 | tf_op jit(solution)/shard_map/ppermute | solution.py:507
  82.6 3.2 %collective-permute-done.11.refs_3_ = bf16[64,1024]{1,0:T(8,128)(2,1)S(1)} collective-permute-done((bf16[64,1024]{1,0:T(8,128)(2,1)S(1)}, bf16[64,1024]{1,0:T(8,128)(2,1)S(1)}, u32[]{:S(2)}, u32[]{:S(2)}) %collective-permute-start.11) | collective-permute-done | bytes 131104 | tf_op jit(solution)/shard_map/ppermute | solution.py:507
  86.3 21.0 %all_to_all.20 = bf16[64,8,384]{2,1,0:T(8,128)(2,1)S(1)} all-to-all(bf16[64,8,384]{2,1,0:T(8,128)(2,1)S(1)} %bitcast.21), channel_id=1, replica_groups=mesh['tile'=64,'chan'=4] {'tile'}, dimensions={0} | all-to-all | bytes 786432 | tf_op jit(solution)/shard_map/all_to_all | solution.py:527
  107.3 0.8 shard_map.135
  108.1 20.1 %all_to_all.21 = bf16[64,8,384]{2,1,0:T(8,128)(2,1)S(1)} all-to-all(bf16[64,8,384]{2,1,0:T(8,128)(2,1)S(1)} %bitcast.24), channel_id=1, replica_groups=mesh['tile'=64,'chan'=4] {'tile'}, dimensions={0} | all-to-all | bytes 786432 | tf_op jit(solution)/shard_map/all_to_all | solution.py:527
  128.2 1.4 %shard_map.136 = (bf16[32,4096]{1,0:T(8,128)(2,1)}, f32[16,576]{1,0:T(8,128)}, f32[64,64]{1,0:T(8,128)}, f32[1,16]{1,0:T(1,128)}) custom-call(bf16[512,384]{1,0:T(8,128)(2,1)S(1)} %bitcast.22), custom_call_target="tpu_custom_call" | custom-call | flops 400000000 | bytes 1000000 | tf_op jit(solution)/shard_map/pallas_call | solution.py:639
  (16 shorter events, 1.7 us)
Async XLA Ops:
  4.0 62.9 %copy-start = (bf16[8,16,4096]{2,1,0:T(8,128)(2,1)S(1)}, bf16[8,16,4096]{2,1,0:T(8,128)(2,1)}, u32[]{:S(2)}) copy-start(bf16[8,16,4096]{2,1,0:T(8,128)(2,1)} %param.10) | copy-start | bytes 3145732
  4.0 29.6 %all-to-all-start = ((bf16[64,8,384]{2,1,0:T(8,128)(2,1)}), bf16[64,8,384]{2,1,0:T(8,128)(2,1)S(1)}, u32[]{:S(2)}, u32[]{:S(2)}) async-start(bf16[64,8,384]{2,1,0:T(8,128)(2,1)} %bitcast.9), calls=%async_computation | async-start | bytes 786432 | tf_op jit(solution)/shard_map/all_to_all | solution.py:527
  19.3 2.8 %collective-permute-start = (bf16[16,4096]{1,0:T(8,128)(2,1)S(1)}, bf16[16,4096]{1,0:T(8,128)(2,1)S(1)}, u32[]{:S(2)}, u32[]{:S(2)}) collective-permute-start(bf16[16,4096]{1,0:T(8,128)(2,1)S(1)} %get-tuple-element.40), channel_id=1, source_target_pairs={{0,1},{1,0},{2,3},{3,2},{4,5},{5,4},{6,7},{7,6},{8,9},{9,8},{10,11... | collective-permute-start | bytes 393224 | tf_op jit(solution)/shard_map/ppermute | solution.py:507
  20.3 6.5 %collective-permute-start.1 = (bf16[16,4096]{1,0:T(8,128)(2,1)S(1)}, bf16[16,4096]{1,0:T(8,128)(2,1)S(1)}, u32[]{:S(2)}, u32[]{:S(2)}) collective-permute-start(bf16[16,4096]{1,0:T(8,128)(2,1)S(1)} %get-tuple-element.41), channel_id=1, source_target_pairs={{0,2},{1,3},{2,0},{3,1},{4,6},{5,7},{6,4},{7,5},{8,10},{9,11},{10,... | collective-permute-start | bytes 393224 | tf_op jit(solution)/shard_map/ppermute | solution.py:507
  20.8 11.5 %collective-permute-start.2 = (bf16[16,4096]{1,0:T(8,128)(2,1)S(1)}, bf16[16,4096]{1,0:T(8,128)(2,1)S(1)}, u32[]{:S(2)}, u32[]{:S(2)}) collective-permute-start(bf16[16,4096]{1,0:T(8,128)(2,1)S(1)} %get-tuple-element.42), channel_id=1, source_target_pairs={{0,3},{1,2},{2,1},{3,0},{4,7},{5,6},{6,5},{7,4},{8,11},{9,10},{10,... | collective-permute-start | bytes 393224 | tf_op jit(solution)/shard_map/ppermute | solution.py:507
  36.9 24.8 %all-to-all-start.1 = ((bf16[64,8,384]{2,1,0:T(8,128)(2,1)}), bf16[64,8,384]{2,1,0:T(8,128)(2,1)S(1)}, u32[]{:S(2)}, u32[]{:S(2)}) async-start(bf16[64,8,384]{2,1,0:T(8,128)(2,1)} %bitcast.11), calls=%async_computation.1 | async-start | bytes 786432 | tf_op jit(solution)/shard_map/all_to_all | solution.py:527
  47.0 18.2 %collective-permute-start.6 = (bf16[16,5632]{1,0:T(8,128)(2,1)S(1)}, bf16[16,5632]{1,0:T(8,128)(2,1)S(1)}, u32[]{:S(2)}, u32[]{:S(2)}) collective-permute-start(bf16[16,5632]{1,0:T(8,128)(2,1)S(1)} %get-tuple-element.53), channel_id=1, source_target_pairs={{0,1},{1,0},{2,3},{3,2},{4,5},{5,4},{6,7},{7,6},{8,9},{9,8},{10,11... | collective-permute-start | bytes 540680 | tf_op jit(solution)/shard_map/ppermute | solution.py:507
  47.8 19.1 %collective-permute-start.7 = (bf16[16,5632]{1,0:T(8,128)(2,1)S(1)}, bf16[16,5632]{1,0:T(8,128)(2,1)S(1)}, u32[]{:S(2)}, u32[]{:S(2)}) collective-permute-start(bf16[16,5632]{1,0:T(8,128)(2,1)S(1)} %get-tuple-element.54), channel_id=1, source_target_pairs={{0,2},{1,3},{2,0},{3,1},{4,6},{5,7},{6,4},{7,5},{8,10},{9,11},{10,... | collective-permute-start | bytes 540680 | tf_op jit(solution)/shard_map/ppermute | solution.py:507
  47.9 19.0 %collective-permute-start.8 = (bf16[16,5632]{1,0:T(8,128)(2,1)S(1)}, bf16[16,5632]{1,0:T(8,128)(2,1)S(1)}, u32[]{:S(2)}, u32[]{:S(2)}) collective-permute-start(bf16[16,5632]{1,0:T(8,128)(2,1)S(1)} %get-tuple-element.55), channel_id=1, source_target_pairs={{0,3},{1,2},{2,1},{3,0},{4,7},{5,6},{6,5},{7,4},{8,11},{9,10},{10,... | collective-permute-start | bytes 540680 | tf_op jit(solution)/shard_map/ppermute | solution.py:507
  62.3 7.6 %collective-permute-start.3 = (bf16[128,384]{1,0:T(8,128)(2,1)S(1)}, bf16[128,384]{1,0:T(8,128)(2,1)S(1)}, u32[]{:S(2)}, u32[]{:S(2)}) collective-permute-start(bf16[128,384]{1,0:T(8,128)(2,1)S(1)} %get-tuple-element.46), channel_id=1, source_target_pairs={{0,1},{1,0},{2,3},{3,2},{4,5},{5,4},{6,7},{7,6},{8,9},{9,8},{10,11... | collective-permute-start | bytes 294920 | tf_op jit(solution)/shard_map/ppermute | solution.py:507
  65.2 4.7 %collective-permute-start.4 = (bf16[128,384]{1,0:T(8,128)(2,1)S(1)}, bf16[128,384]{1,0:T(8,128)(2,1)S(1)}, u32[]{:S(2)}, u32[]{:S(2)}) collective-permute-start(bf16[128,384]{1,0:T(8,128)(2,1)S(1)} %get-tuple-element.47), channel_id=1, source_target_pairs={{0,2},{1,3},{2,0},{3,1},{4,6},{5,7},{6,4},{7,5},{8,10},{9,11},{10,... | collective-permute-start | bytes 294920 | tf_op jit(solution)/shard_map/ppermute | solution.py:507
  65.2 6.6 %collective-permute-start.5 = (bf16[128,384]{1,0:T(8,128)(2,1)S(1)}, bf16[128,384]{1,0:T(8,128)(2,1)S(1)}, u32[]{:S(2)}, u32[]{:S(2)}) collective-permute-start(bf16[128,384]{1,0:T(8,128)(2,1)S(1)} %get-tuple-element.48), channel_id=1, source_target_pairs={{0,3},{1,2},{2,1},{3,0},{4,7},{5,6},{6,5},{7,4},{8,11},{9,10},{10,... | collective-permute-start | bytes 294920 | tf_op jit(solution)/shard_map/ppermute | solution.py:507
  77.7 4.9 %collective-permute-start.10 = (bf16[64,1024]{1,0:T(8,128)(2,1)S(1)}, bf16[64,1024]{1,0:T(8,128)(2,1)S(1)}, u32[]{:S(2)}, u32[]{:S(2)}) collective-permute-start(bf16[64,1024]{1,0:T(8,128)(2,1)S(1)} %get-tuple-element.67), channel_id=1, source_target_pairs={{0,2},{1,3},{2,0},{3,1},{4,6},{5,7},{6,4},{7,5},{8,10},{9,11},{10,... | collective-permute-start | bytes 393224 | tf_op jit(solution)/shard_map/ppermute | solution.py:507
  77.8 8.0 %collective-permute-start.11 = (bf16[64,1024]{1,0:T(8,128)(2,1)S(1)}, bf16[64,1024]{1,0:T(8,128)(2,1)S(1)}, u32[]{:S(2)}, u32[]{:S(2)}) collective-permute-start(bf16[64,1024]{1,0:T(8,128)(2,1)S(1)} %get-tuple-element.68), channel_id=1, source_target_pairs={{0,3},{1,2},{2,1},{3,0},{4,7},{5,6},{6,5},{7,4},{8,11},{9,10},{10,... | collective-permute-start | bytes 393224 | tf_op jit(solution)/shard_map/ppermute | solution.py:507
  79.7 6.2 %collective-permute-start.9 = (bf16[64,1024]{1,0:T(8,128)(2,1)S(1)}, bf16[64,1024]{1,0:T(8,128)(2,1)S(1)}, u32[]{:S(2)}, u32[]{:S(2)}) collective-permute-start(bf16[64,1024]{1,0:T(8,128)(2,1)S(1)} %get-tuple-element.66), channel_id=1, source_target_pairs={{0,1},{1,0},{2,3},{3,2},{4,5},{5,4},{6,7},{7,6},{8,9},{9,8},{10,11... | collective-permute-start | bytes 393224 | tf_op jit(solution)/shard_map/ppermute | solution.py:507

commit v8 on v7

--- a/solution.py
+++ b/solution.py
@@ -482,23 +482,16 @@
 
     row = down_col(256)
     got = mm(ones_where(col == ((row & 63) << 3) + (row >> 6)), msg_ref[:, 256:384])
-    near = down_col(1024)
-    to = jnp.where((near & 255) < 144, (near >> 8) * 144 + (near & 255), -1)
-    place = ones_where(lane_row(576) == to)
-    lane = lane_row(128)
-    shift = ones_where(down_col(128) == jnp.where(lane < 64, lane + 16, -1))
-    conv = jnp.zeros((16, 576), F32)
-    down = jnp.zeros((64, 128), F32)
-    for h in range(2):
-        low, high = got[h * 128 : h * 128 + 64, :], got[h * 128 + 64 : h * 128 + 128, :]
-        wide = jnp.concatenate(
-            [x[s * 16 : s * 16 + 16, :] for s in range(4) for x in (low, high)], axis=1
-        )
-        conv = conv + mm(wide.astype(BF), place)
-        down = down + mm(high.astype(BF), shift)
-    conv_ref[...] = conv
-    down_ref[...] = down[:, 0:64]
-    bias = got[64:80, 80:81] + got[192:208, 80:81]
+    value = jnp.concatenate([got[0:64] + got[128:192], got[64:128] + got[192:256]], axis=1)
+    head = jnp.where(lane_row(256) < 144, value, 0.0)
+    pad = jnp.zeros((16, 384), F32)
+    conv = jnp.zeros((16, 640), F32)
+    for q in range(4):
+        part = jnp.concatenate([head[q * 16 : q * 16 + 16, :], pad], axis=1)
+        conv = conv + (pltpu.roll(part, q * 144, axis=1) if q else part)
+    conv_ref[...] = conv[:, 0:576]
+    down_ref[...] = pltpu.roll(value, 112, axis=1)[:, 0:64]
+    bias = value[0:16, 208:209]
     bias_ref[...] = jnp.sum(jnp.where(lane_row(16) == down_col(16), bias, 0.0), axis=0, keepdims=True)
 
 

time: 132 us -> 132 us (level)
  no operation moved by 1% of the time
where the time goes in v8:
time: 132 us; the launch traced here: 129 us
  blocking collectives  41.1 us (31%)
  starting transfers between devices  37.3 us (28%)
  waiting for transfers between devices  31.8 us (24%)
  Pallas kernels  18.5 us (14%)
    all_to_all x2, blocking collectives, to_nodes(): lax.all_to_all(x.reshape(64, 8, 384), 'tile', 0, 0, tiled=True).reshape(MSG)  41.1 us
    all_to_all x2, starting transfers between devices, to_nodes(): lax.all_to_all(x.reshape(64, 8, 384), 'tile', 0, 0, tiled=True).reshape(MSG)  25.4 us
    ppermute x12, waiting for transfers between devices, to_peers(): lax.ppermute(parts[d], 'chan', [(i, i ^ d) for i in range(4)])  18.2 us
    all_to_all x2, waiting for transfers between devices, to_nodes(): lax.all_to_all(x.reshape(64, 8, 384), 'tile', 0, 0, tiled=True).reshape(MSG)  13.6 us
    ppermute x12, starting transfers between devices, to_peers(): lax.ppermute(parts[d], 'chan', [(i, i ^ d) for i in range(4)])  11.9 us
    pallas_call x1, Pallas kernels, on_device(): pl.pallas_call(level_body, out_shape=(jax.ShapeDtypeStruct((64, 1024), BF...  5.87 us
    pallas_call x1, Pallas kernels, on_device(): call(send_body, (msg, jax.ShapeDtypeStruct((64, 384), BF)) + (first,) * 3...  3.41 us
    pallas_call x1, Pallas kernels, on_device(): call(pick_body, (msg, jax.ShapeDtypeStruct((8, 512), F32)), (1,), [vmem],...  3.23 us
  transfers between devices with their start and end apart: 14, of which 7 were waited for; matrix products, arithmetic and copies ran while one was open for 0% of the time, Pallas kernels for 3%

profile of v8, /device:TPU:1, one launch (start us, length us, event | category | flops | bytes accessed | tf_op | source)
XLA Modules:
  0.0 129.4 jit_solution(2992587717098040694)
XLA Ops:
  0.6 3.4 %shard_map.129 = (bf16[512,384]{1,0:T(8,128)(2,1)}, bf16[64,384]{1,0:T(8,128)(2,1)S(1)}, bf16[16,4096]{1,0:T(8,128)(2,1)S(1)}, bf16[16,4096]{1,0:T(8,128)(2,1)S(...) custom-call(s32[1]{0:T(128)} %bitcast.me_ref, ...), custom_call_target="tpu_custom_call" | custom-call | flops 1000000000 | bytes 2000000 | tf_op jit(solution)/shard_map/pallas_call | solution.py:526
  4.0 15.2 %all-to-all-start = ((bf16[64,8,384]{2,1,0:T(8,128)(2,1)}), bf16[64,8,384]{2,1,0:T(8,128)(2,1)S(1)}, u32[]{:S(2)}, u32[]{:S(2)}) async-start(bf16[64,8,384]{2,1,0:T(8,128)(2,1)} %bitcast.9), calls=%async_computation | async-start | bytes 786432 | tf_op jit(solution)/shard_map/all_to_all | solution.py:520
  19.3 1.0 collective-permute-start
  20.8 1.3 %collective-permute-start.2 = (bf16[16,4096]{1,0:T(8,128)(2,1)S(1)}, bf16[16,4096]{1,0:T(8,128)(2,1)S(1)}, u32[]{:S(2)}, u32[]{:S(2)}) collective-permute-start(bf16[16,4096]{1,0:T(8,128)(2,1)S(1)} %get-tuple-element.42), channel_id=1, source_target_pairs={{0,3},{1,2},{2,1},{3,0},{4,7},{5,6},{6,5},{7,4},{8,11},{9,10},{10,... | collective-permute-start | bytes 393224 | tf_op jit(solution)/shard_map/ppermute | solution.py:500
  22.1 4.8 %collective-permute-done.1.refs_3_ = bf16[16,4096]{1,0:T(8,128)(2,1)S(1)} collective-permute-done((bf16[16,4096]{1,0:T(8,128)(2,1)S(1)}, bf16[16,4096]{1,0:T(8,128)(2,1)S(1)}, u32[]{:S(2)}, u32[]{:S(2)}) %collective-permute-start.1) | collective-permute-done | bytes 131104 | tf_op jit(solution)/shard_map/ppermute | solution.py:500
  26.9 5.3 %collective-permute-done.2.refs_4_ = bf16[16,4096]{1,0:T(8,128)(2,1)S(1)} collective-permute-done((bf16[16,4096]{1,0:T(8,128)(2,1)S(1)}, bf16[16,4096]{1,0:T(8,128)(2,1)S(1)}, u32[]{:S(2)}, u32[]{:S(2)}) %collective-permute-start.2) | collective-permute-done | bytes 131104 | tf_op jit(solution)/shard_map/ppermute | solution.py:500
  32.2 1.4 %all-to-all-done = bf16[64,8,384]{2,1,0:T(8,128)(2,1)S(1)} async-done(((bf16[64,8,384]{2,1,0:T(8,128)(2,1)}), bf16[64,8,384]{2,1,0:T(8,128)(2,1)S(1)}, u32[]{:S(2)}, u32[]{:S(2)}) %all-to-all-start) | async-done | bytes 393248 | tf_op jit(solution)/shard_map/all_to_all | solution.py:520
  33.6 3.2 %shard_map.130 = (bf16[512,384]{1,0:T(8,128)(2,1)}, f32[8,512]{1,0:T(8,128)S(1)}) custom-call(bf16[512,384]{1,0:T(8,128)(2,1)S(1)} %bitcast.19), custom_call_target="tpu_custom_call" | custom-call | flops 1000000000 | bytes 1000000 | tf_op jit(solution)/shard_map/pallas_call | solution.py:557
  36.9 10.2 %all-to-all-start.1 = ((bf16[64,8,384]{2,1,0:T(8,128)(2,1)}), bf16[64,8,384]{2,1,0:T(8,128)(2,1)S(1)}, u32[]{:S(2)}, u32[]{:S(2)}) async-start(bf16[64,8,384]{2,1,0:T(8,128)(2,1)} %bitcast.11), calls=%async_computation.1 | async-start | bytes 786432 | tf_op jit(solution)/shard_map/all_to_all | solution.py:520
  47.0 0.8 collective-permute-start.6
  47.9 1.7 %collective-permute-start.8 = (bf16[16,5632]{1,0:T(8,128)(2,1)S(1)}, bf16[16,5632]{1,0:T(8,128)(2,1)S(1)}, u32[]{:S(2)}, u32[]{:S(2)}) collective-permute-start(bf16[16,5632]{1,0:T(8,128)(2,1)S(1)} %get-tuple-element.55), channel_id=1, source_target_pairs={{0,3},{1,2},{2,1},{3,0},{4,7},{5,6},{6,5},{7,4},{8,11},{9,10},{10,... | collective-permute-start | bytes 540680 | tf_op jit(solution)/shard_map/ppermute | solution.py:500
  49.5 12.2 %all-to-all-done.1 = bf16[64,8,384]{2,1,0:T(8,128)(2,1)S(1)} async-done(((bf16[64,8,384]{2,1,0:T(8,128)(2,1)}), bf16[64,8,384]{2,1,0:T(8,128)(2,1)S(1)}, u32[]{:S(2)}, u32[]{:S(2)}) %all-to-all-start.1) | async-done | bytes 393248 | tf_op jit(solution)/shard_map/all_to_all | solution.py:520
  62.3 2.9 %collective-permute-start.3 = (bf16[128,384]{1,0:T(8,128)(2,1)S(1)}, bf16[128,384]{1,0:T(8,128)(2,1)S(1)}, u32[]{:S(2)}, u32[]{:S(2)}) collective-permute-start(bf16[128,384]{1,0:T(8,128)(2,1)S(1)} %get-tuple-element.46), channel_id=1, source_target_pairs={{0,1},{1,0},{2,3},{3,2},{4,5},{5,4},{6,7},{7,6},{8,9},{9,8},{10,11... | collective-permute-start | bytes 294920 | tf_op jit(solution)/shard_map/ppermute | solution.py:500
  65.2 1.7 %collective-permute-start.5 = (bf16[128,384]{1,0:T(8,128)(2,1)S(1)}, bf16[128,384]{1,0:T(8,128)(2,1)S(1)}, u32[]{:S(2)}, u32[]{:S(2)}) collective-permute-start(bf16[128,384]{1,0:T(8,128)(2,1)S(1)} %get-tuple-element.48), channel_id=1, source_target_pairs={{0,3},{1,2},{2,1},{3,0},{4,7},{5,6},{6,5},{7,4},{8,11},{9,10},{10,... | collective-permute-start | bytes 294920 | tf_op jit(solution)/shard_map/ppermute | solution.py:500
  66.9 2.9 %shard_map.132 = (bf16[2,1024,1024]{2,1,0:T(8,128)(2,1)S(1)}, bf16[256,1024]{1,0:T(8,128)(2,1)S(1)}, bf16[64,256]{1,0:T(8,128)(2,1)S(1)}, bf16[256,64]{1,0:T(8,1...) custom-call(s32[1]{0:T(128)} %bitcast.me_ref, ...), custom_call_target="tpu_custom_call" | custom-call | flops 1000000000 | bytes 4000000 | tf_op jit(solution)/shard_map/pallas_call | solution.py:568
  69.9 1.9 %collective-permute-done.5.refs_3_ = bf16[128,384]{1,0:T(8,128)(2,1)S(1)} collective-permute-done((bf16[128,384]{1,0:T(8,128)(2,1)S(1)}, bf16[128,384]{1,0:T(8,128)(2,1)S(1)}, u32[]{:S(2)}, u32[]{:S(2)}) %collective-permute-start.5) | collective-permute-done | bytes 98336 | tf_op jit(solution)/shard_map/ppermute | solution.py:500
  71.8 5.9 %shard_map.133 = (bf16[64,1024]{1,0:T(8,128)(2,1)S(1)}, bf16[64,1024]{1,0:T(8,128)(2,1)S(1)}, bf16[64,1024]{1,0:T(8,128)(2,1)S(1)}, bf16[64,1024]{1,0:T(8,128)(2,1)S(1)}) custom-call(s32[1]{0:T(128)} %bitcast.me_ref, bf16[128,384]{1,0:T(8,128)(2,1)S(1)} %get-tuple-element.45.refs_0_, bf16[128,384]{1,0:T(8,128)(2,1)S(1)} %collective-permute-done.3.refs_1_, ...), custom_call_target="tpu_custom_call" | custom-call | flops 4000000000 | bytes 4000000 | tf_op jit(solution)/shard_map/pallas_call | solution.py:602
  77.8 1.8 %collective-permute-start.11 = (bf16[64,1024]{1,0:T(8,128)(2,1)S(1)}, bf16[64,1024]{1,0:T(8,128)(2,1)S(1)}, u32[]{:S(2)}, u32[]{:S(2)}) collective-permute-start(bf16[64,1024]{1,0:T(8,128)(2,1)S(1)} %get-tuple-element.68), channel_id=1, source_target_pairs={{0,3},{1,2},{2,1},{3,0},{4,7},{5,6},{6,5},{7,4},{8,11},{9,10},{10,... | collective-permute-start | bytes 393224 | tf_op jit(solution)/shard_map/ppermute | solution.py:500
  79.7 3.0 %collective-permute-done.10.refs_2_ = bf16[64,1024]{1,0:T(8,128)(2,1)S(1)} collective-permute-done((bf16[64,1024]{1,0:T(8,128)(2,1)S(1)}, bf16[64,1024]{1,0:T(8,128)(2,1)S(1)}, u32[]{:S(2)}, u32[]{:S(2)}) %collective-permute-start.10) | collective-permute-done | bytes 131104 | tf_op jit(solution)/shard_map/ppermute | solution.py:500
  82.6 3.2 %collective-permute-done.11.refs_3_ = bf16[64,1024]{1,0:T(8,128)(2,1)S(1)} collective-permute-done((bf16[64,1024]{1,0:T(8,128)(2,1)S(1)}, bf16[64,1024]{1,0:T(8,128)(2,1)S(1)}, u32[]{:S(2)}, u32[]{:S(2)}) %collective-permute-start.11) | collective-permute-done | bytes 131104 | tf_op jit(solution)/shard_map/ppermute | solution.py:500
  86.3 21.0 %all_to_all.20 = bf16[64,8,384]{2,1,0:T(8,128)(2,1)S(1)} all-to-all(bf16[64,8,384]{2,1,0:T(8,128)(2,1)S(1)} %bitcast.21), channel_id=1, replica_groups=mesh['tile'=64,'chan'=4] {'tile'}, dimensions={0} | all-to-all | bytes 786432 | tf_op jit(solution)/shard_map/all_to_all | solution.py:520
  107.3 0.8 shard_map.135
  108.1 20.1 %all_to_all.21 = bf16[64,8,384]{2,1,0:T(8,128)(2,1)S(1)} all-to-all(bf16[64,8,384]{2,1,0:T(8,128)(2,1)S(1)} %bitcast.24), channel_id=1, replica_groups=mesh['tile'=64,'chan'=4] {'tile'}, dimensions={0} | all-to-all | bytes 786432 | tf_op jit(solution)/shard_map/all_to_all | solution.py:520
  128.2 1.2 shard_map.136
  (16 shorter events, 1.7 us)
Async XLA Ops:
  4.0 62.9 %copy-start = (bf16[8,16,4096]{2,1,0:T(8,128)(2,1)S(1)}, bf16[8,16,4096]{2,1,0:T(8,128)(2,1)}, u32[]{:S(2)}) copy-start(bf16[8,16,4096]{2,1,0:T(8,128)(2,1)} %param.10) | copy-start | bytes 3145732
  4.0 29.6 %all-to-all-start = ((bf16[64,8,384]{2,1,0:T(8,128)(2,1)}), bf16[64,8,384]{2,1,0:T(8,128)(2,1)S(1)}, u32[]{:S(2)}, u32[]{:S(2)}) async-start(bf16[64,8,384]{2,1,0:T(8,128)(2,1)} %bitcast.9), calls=%async_computation | async-start | bytes 786432 | tf_op jit(solution)/shard_map/all_to_all | solution.py:520
  19.3 2.8 %collective-permute-start = (bf16[16,4096]{1,0:T(8,128)(2,1)S(1)}, bf16[16,4096]{1,0:T(8,128)(2,1)S(1)}, u32[]{:S(2)}, u32[]{:S(2)}) collective-permute-start(bf16[16,4096]{1,0:T(8,128)(2,1)S(1)} %get-tuple-element.40), channel_id=1, source_target_pairs={{0,1},{1,0},{2,3},{3,2},{4,5},{5,4},{6,7},{7,6},{8,9},{9,8},{10,11... | collective-permute-start | bytes 393224 | tf_op jit(solution)/shard_map/ppermute | solution.py:500
  20.3 6.5 %collective-permute-start.1 = (bf16[16,4096]{1,0:T(8,128)(2,1)S(1)}, bf16[16,4096]{1,0:T(8,128)(2,1)S(1)}, u32[]{:S(2)}, u32[]{:S(2)}) collective-permute-start(bf16[16,4096]{1,0:T(8,128)(2,1)S(1)} %get-tuple-element.41), channel_id=1, source_target_pairs={{0,2},{1,3},{2,0},{3,1},{4,6},{5,7},{6,4},{7,5},{8,10},{9,11},{10,... | collective-permute-start | bytes 393224 | tf_op jit(solution)/shard_map/ppermute | solution.py:500
  20.8 11.5 %collective-permute-start.2 = (bf16[16,4096]{1,0:T(8,128)(2,1)S(1)}, bf16[16,4096]{1,0:T(8,128)(2,1)S(1)}, u32[]{:S(2)}, u32[]{:S(2)}) collective-permute-start(bf16[16,4096]{1,0:T(8,128)(2,1)S(1)} %get-tuple-element.42), channel_id=1, source_target_pairs={{0,3},{1,2},{2,1},{3,0},{4,7},{5,6},{6,5},{7,4},{8,11},{9,10},{10,... | collective-permute-start | bytes 393224 | tf_op jit(solution)/shard_map/ppermute | solution.py:500
  36.9 24.8 %all-to-all-start.1 = ((bf16[64,8,384]{2,1,0:T(8,128)(2,1)}), bf16[64,8,384]{2,1,0:T(8,128)(2,1)S(1)}, u32[]{:S(2)}, u32[]{:S(2)}) async-start(bf16[64,8,384]{2,1,0:T(8,128)(2,1)} %bitcast.11), calls=%async_computation.1 | async-start | bytes 786432 | tf_op jit(solution)/shard_map/all_to_all | solution.py:520
  47.0 18.2 %collective-permute-start.6 = (bf16[16,5632]{1,0:T(8,128)(2,1)S(1)}, bf16[16,5632]{1,0:T(8,128)(2,1)S(1)}, u32[]{:S(2)}, u32[]{:S(2)}) collective-permute-start(bf16[16,5632]{1,0:T(8,128)(2,1)S(1)} %get-tuple-element.53), channel_id=1, source_target_pairs={{0,1},{1,0},{2,3},{3,2},{4,5},{5,4},{6,7},{7,6},{8,9},{9,8},{10,11... | collective-permute-start | bytes 540680 | tf_op jit(solution)/shard_map/ppermute | solution.py:500
  47.8 19.1 %collective-permute-start.7 = (bf16[16,5632]{1,0:T(8,128)(2,1)S(1)}, bf16[16,5632]{1,0:T(8,128)(2,1)S(1)}, u32[]{:S(2)}, u32[]{:S(2)}) collective-permute-start(bf16[16,5632]{1,0:T(8,128)(2,1)S(1)} %get-tuple-element.54), channel_id=1, source_target_pairs={{0,2},{1,3},{2,0},{3,1},{4,6},{5,7},{6,4},{7,5},{8,10},{9,11},{10,... | collective-permute-start | bytes 540680 | tf_op jit(solution)/shard_map/ppermute | solution.py:500
  47.9 19.0 %collective-permute-start.8 = (bf16[16,5632]{1,0:T(8,128)(2,1)S(1)}, bf16[16,5632]{1,0:T(8,128)(2,1)S(1)}, u32[]{:S(2)}, u32[]{:S(2)}) collective-permute-start(bf16[16,5632]{1,0:T(8,128)(2,1)S(1)} %get-tuple-element.55), channel_id=1, source_target_pairs={{0,3},{1,2},{2,1},{3,0},{4,7},{5,6},{6,5},{7,4},{8,11},{9,10},{10,... | collective-permute-start | bytes 540680 | tf_op jit(solution)/shard_map/ppermute | solution.py:500
  62.3 7.6 %collective-permute-start.3 = (bf16[128,384]{1,0:T(8,128)(2,1)S(1)}, bf16[128,384]{1,0:T(8,128)(2,1)S(1)}, u32[]{:S(2)}, u32[]{:S(2)}) collective-permute-start(bf16[128,384]{1,0:T(8,128)(2,1)S(1)} %get-tuple-element.46), channel_id=1, source_target_pairs={{0,1},{1,0},{2,3},{3,2},{4,5},{5,4},{6,7},{7,6},{8,9},{9,8},{10,11... | collective-permute-start | bytes 294920 | tf_op jit(solution)/shard_map/ppermute | solution.py:500
  65.2 4.7 %collective-permute-start.4 = (bf16[128,384]{1,0:T(8,128)(2,1)S(1)}, bf16[128,384]{1,0:T(8,128)(2,1)S(1)}, u32[]{:S(2)}, u32[]{:S(2)}) collective-permute-start(bf16[128,384]{1,0:T(8,128)(2,1)S(1)} %get-tuple-element.47), channel_id=1, source_target_pairs={{0,2},{1,3},{2,0},{3,1},{4,6},{5,7},{6,4},{7,5},{8,10},{9,11},{10,... | collective-permute-start | bytes 294920 | tf_op jit(solution)/shard_map/ppermute | solution.py:500
  65.2 6.6 %collective-permute-start.5 = (bf16[128,384]{1,0:T(8,128)(2,1)S(1)}, bf16[128,384]{1,0:T(8,128)(2,1)S(1)}, u32[]{:S(2)}, u32[]{:S(2)}) collective-permute-start(bf16[128,384]{1,0:T(8,128)(2,1)S(1)} %get-tuple-element.48), channel_id=1, source_target_pairs={{0,3},{1,2},{2,1},{3,0},{4,7},{5,6},{6,5},{7,4},{8,11},{9,10},{10,... | collective-permute-start | bytes 294920 | tf_op jit(solution)/shard_map/ppermute | solution.py:500
  77.7 4.9 %collective-permute-start.10 = (bf16[64,1024]{1,0:T(8,128)(2,1)S(1)}, bf16[64,1024]{1,0:T(8,128)(2,1)S(1)}, u32[]{:S(2)}, u32[]{:S(2)}) collective-permute-start(bf16[64,1024]{1,0:T(8,128)(2,1)S(1)} %get-tuple-element.67), channel_id=1, source_target_pairs={{0,2},{1,3},{2,0},{3,1},{4,6},{5,7},{6,4},{7,5},{8,10},{9,11},{10,... | collective-permute-start | bytes 393224 | tf_op jit(solution)/shard_map/ppermute | solution.py:500
  77.8 8.0 %collective-permute-start.11 = (bf16[64,1024]{1,0:T(8,128)(2,1)S(1)}, bf16[64,1024]{1,0:T(8,128)(2,1)S(1)}, u32[]{:S(2)}, u32[]{:S(2)}) collective-permute-start(bf16[64,1024]{1,0:T(8,128)(2,1)S(1)} %get-tuple-element.68), channel_id=1, source_target_pairs={{0,3},{1,2},{2,1},{3,0},{4,7},{5,6},{6,5},{7,4},{8,11},{9,10},{10,... | collective-permute-start | bytes 393224 | tf_op jit(solution)/shard_map/ppermute | solution.py:500
  79.7 6.2 %collective-permute-start.9 = (bf16[64,1024]{1,0:T(8,128)(2,1)S(1)}, bf16[64,1024]{1,0:T(8,128)(2,1)S(1)}, u32[]{:S(2)}, u32[]{:S(2)}) collective-permute-start(bf16[64,1024]{1,0:T(8,128)(2,1)S(1)} %get-tuple-element.66), channel_id=1, source_target_pairs={{0,1},{1,0},{2,3},{3,2},{4,5},{5,4},{6,7},{7,6},{8,9},{9,8},{10,11... | collective-permute-start | bytes 393224 | tf_op jit(solution)/shard_map/ppermute | solution.py:500

commit v9 on v8

--- a/solution.py
+++ b/solution.py
@@ -80,7 +80,7 @@
 
 def send_body(
     me_ref,
-    feat_ref,
+    all_ref,
     cot_ref,
     el_ref,
     et_ref,
@@ -92,17 +92,19 @@
     down_ref,
     out_ref,
     raw_ref,
-    *peer_refs,
+    *more_refs,
 ):
-    pack_weights(conv_ref, bias_ref, down_ref, raw_ref)
+    peer_refs, (feat_ref, sems) = more_refs[0:6], more_refs[6:]
+    copies = [pltpu.make_async_copy(all_ref, feat_ref, sems.at[0])]
     for d in range(1, 4):
         peer = me_ref[0] ^ d
-        first_ref, second_ref = peer_refs[d - 1], peer_refs[d + 2]
-        first_ref[...] = feat_ref[pl.ds(pl.multiple_of(peer * 32, 16), 16), :]
-        second_ref[:, 0:4096] = feat_ref[pl.ds(pl.multiple_of(peer * 32 + 16, 16), 16), :]
-        for q in range(4):
-            second_ref[:, 4096 + q * 384 : 4480 + q * 384] = raw_ref[q * 16 : q * 16 + 16, :]
-
+        first = all_ref.at[pl.ds(pl.multiple_of(peer * 32, 16), 16), :]
+        second = all_ref.at[pl.ds(pl.multiple_of(peer * 32 + 16, 16), 16), :]
+        copies.append(pltpu.make_async_copy(first, peer_refs[d - 1], sems.at[d]))
+        copies.append(pltpu.make_async_copy(second, peer_refs[d + 2].at[:, 0:4096], sems.at[d + 3]))
+    for copy in copies:
+        copy.start()
+    pack_weights(conv_ref, bias_ref, down_ref, raw_ref)
     cot = cot_ref[...]
     stack = jnp.concatenate([cot[:, q * 256 : q * 256 + 256] for q in range(16)], axis=0)
     row = down_col(512)
@@ -110,6 +112,7 @@
     source = (qr << 8) | (g << 6) | (hf << 5) | (a << 4) | k
     out_ref[:, 0:256] = mm(ones_where(lane_row(512) == source), stack).astype(BF)
 
+    copies[0].wait()
     first = feat_ref[:, 0:128]
     last = feat_ref[:, 3968:4096]
     p = down_col(64)
@@ -161,6 +164,11 @@
     source = jnp.where(r == 4, 256 + (node & 15), jnp.where(r == 5, 272, jnp.where(r == 6, 273 + (node >> 4), -1)))
     source = jnp.where(r < 4, r * 64 + node, source)
     out_ref[:, 256:384] = mm(ones_where(lane_row(384) == source), stack).astype(BF)
+    for copy in copies[1:]:
+        copy.wait()
+    for d in range(1, 4):
+        for q in range(4):
+            peer_refs[d + 2][:, 4096 + q * 384 : 4480 + q * 384] = raw_ref[q * 16 : q * 16 + 16, :]
 
 
 def pick_body(msg_ref, out_ref, slot_ref):
@@ -527,10 +535,11 @@
         send_body,
         (msg, jax.ShapeDtypeStruct((64, 384), BF)) + (first,) * 3 + (second,) * 3,
         (1,),
-        [scalar, whole((128, 4096)), whole((32, 4096))]
+        [scalar, pl.BlockSpec(memory_space=pl.ANY), whole((32, 4096))]
         + [whole((4, 8))] * 4
         + [whole((1, 8)), whole((16, 576)), whole((1, 16)), whole((64, 64))],
         (vmem,) * 8,
+        (pltpu.VMEM((128, 4096), BF), pltpu.SemaphoreType.DMA((7,))),
         flops=10**9,
         moved=2 * 10**6,
     )(

time: 132 us -> 132 us (level)
  no operation moved by 1% of the time
where the time goes in v9:
time: 132 us; the launch traced here: 130 us
  blocking collectives  41.1 us (31%)
  starting transfers between devices  37.3 us (28%)
  waiting for transfers between devices  31.9 us (24%)
  Pallas kernels  19.3 us (15%)
    all_to_all x2, blocking collectives, to_nodes(): lax.all_to_all(x.reshape(64, 8, 384), 'tile', 0, 0, tiled=True).reshape(MSG)  41.1 us
    all_to_all x2, starting transfers between devices, to_nodes(): lax.all_to_all(x.reshape(64, 8, 384), 'tile', 0, 0, tiled=True).reshape(MSG)  25.4 us
    ppermute x12, waiting for transfers between devices, to_peers(): lax.ppermute(parts[d], 'chan', [(i, i ^ d) for i in range(4)])  18.3 us
    all_to_all x2, waiting for transfers between devices, to_nodes(): lax.all_to_all(x.reshape(64, 8, 384), 'tile', 0, 0, tiled=True).reshape(MSG)  13.6 us
    ppermute x12, starting transfers between devices, to_peers(): lax.ppermute(parts[d], 'chan', [(i, i ^ d) for i in range(4)])  11.9 us
    pallas_call x1, Pallas kernels, on_device(): pl.pallas_call(level_body, out_shape=(jax.ShapeDtypeStruct((64, 1024), BF...  5.87 us
    pallas_call x1, Pallas kernels, on_device(): call(send_body, (msg, jax.ShapeDtypeStruct((64, 384), BF)) + (first,) * 3...  4.21 us
    pallas_call x1, Pallas kernels, on_device(): call(pick_body, (msg, jax.ShapeDtypeStruct((8, 512), F32)), (1,), [vmem],...  3.24 us
  transfers between devices with their start and end apart: 14, of which 7 were waited for; matrix products, arithmetic and copies ran while one was open for 0% of the time, Pallas kernels for 3%

profile of v9, /device:TPU:1, one launch (start us, length us, event | category | flops | bytes accessed | tf_op | source)
XLA Modules:
  0.0 130.3 jit_solution(17171160928383003949)
XLA Ops:
  0.6 4.2 %shard_map.129 = (bf16[512,384]{1,0:T(8,128)(2,1)}, bf16[64,384]{1,0:T(8,128)(2,1)S(1)}, bf16[16,4096]{1,0:T(8,128)(2,1)S(1)}, bf16[16,4096]{1,0:T(8,128)(2,1)S(...) custom-call(s32[1]{0:T(128)} %bitcast.me_ref, ...), custom_call_target="tpu_custom_call" | custom-call | flops 1000000000 | bytes 2000000 | tf_op jit(solution)/shard_map/pallas_call | solution.py:534
  4.9 15.3 %all-to-all-start = ((bf16[64,8,384]{2,1,0:T(8,128)(2,1)}), bf16[64,8,384]{2,1,0:T(8,128)(2,1)S(1)}, u32[]{:S(2)}, u32[]{:S(2)}) async-start(bf16[64,8,384]{2,1,0:T(8,128)(2,1)} %bitcast.9), calls=%async_computation | async-start | bytes 786432 | tf_op jit(solution)/shard_map/all_to_all | solution.py:528
  20.1 1.0 collective-permute-start
  21.6 1.3 %collective-permute-start.2 = (bf16[16,4096]{1,0:T(8,128)(2,1)S(1)}, bf16[16,4096]{1,0:T(8,128)(2,1)S(1)}, u32[]{:S(2)}, u32[]{:S(2)}) collective-permute-start(bf16[16,4096]{1,0:T(8,128)(2,1)S(1)} %get-tuple-element.42), channel_id=1, source_target_pairs={{0,3},{1,2},{2,1},{3,0},{4,7},{5,6},{6,5},{7,4},{8,11},{9,10},{10,... | collective-permute-start | bytes 393224 | tf_op jit(solution)/shard_map/ppermute | solution.py:508
  22.9 4.8 %collective-permute-done.1.refs_3_ = bf16[16,4096]{1,0:T(8,128)(2,1)S(1)} collective-permute-done((bf16[16,4096]{1,0:T(8,128)(2,1)S(1)}, bf16[16,4096]{1,0:T(8,128)(2,1)S(1)}, u32[]{:S(2)}, u32[]{:S(2)}) %collective-permute-start.1) | collective-permute-done | bytes 131104 | tf_op jit(solution)/shard_map/ppermute | solution.py:508
  27.7 5.3 %collective-permute-done.2.refs_4_ = bf16[16,4096]{1,0:T(8,128)(2,1)S(1)} collective-permute-done((bf16[16,4096]{1,0:T(8,128)(2,1)S(1)}, bf16[16,4096]{1,0:T(8,128)(2,1)S(1)}, u32[]{:S(2)}, u32[]{:S(2)}) %collective-permute-start.2) | collective-permute-done | bytes 131104 | tf_op jit(solution)/shard_map/ppermute | solution.py:508
  33.1 1.4 %all-to-all-done = bf16[64,8,384]{2,1,0:T(8,128)(2,1)S(1)} async-done(((bf16[64,8,384]{2,1,0:T(8,128)(2,1)}), bf16[64,8,384]{2,1,0:T(8,128)(2,1)S(1)}, u32[]{:S(2)}, u32[]{:S(2)}) %all-to-all-start) | async-done | bytes 393248 | tf_op jit(solution)/shard_map/all_to_all | solution.py:528
  34.5 3.2 %shard_map.130 = (bf16[512,384]{1,0:T(8,128)(2,1)}, f32[8,512]{1,0:T(8,128)S(1)}) custom-call(bf16[512,384]{1,0:T(8,128)(2,1)S(1)} %bitcast.19), custom_call_target="tpu_custom_call" | custom-call | flops 1000000000 | bytes 1000000 | tf_op jit(solution)/shard_map/pallas_call | solution.py:566
  37.7 10.1 %all-to-all-start.1 = ((bf16[64,8,384]{2,1,0:T(8,128)(2,1)}), bf16[64,8,384]{2,1,0:T(8,128)(2,1)S(1)}, u32[]{:S(2)}, u32[]{:S(2)}) async-start(bf16[64,8,384]{2,1,0:T(8,128)(2,1)} %bitcast.11), calls=%async_computation.1 | async-start | bytes 786432 | tf_op jit(solution)/shard_map/all_to_all | solution.py:528
  47.9 0.8 collective-permute-start.6
  48.7 1.7 %collective-permute-start.8 = (bf16[16,5632]{1,0:T(8,128)(2,1)S(1)}, bf16[16,5632]{1,0:T(8,128)(2,1)S(1)}, u32[]{:S(2)}, u32[]{:S(2)}) collective-permute-start(bf16[16,5632]{1,0:T(8,128)(2,1)S(1)} %get-tuple-element.55), channel_id=1, source_target_pairs={{0,3},{1,2},{2,1},{3,0},{4,7},{5,6},{6,5},{7,4},{8,11},{9,10},{10,... | collective-permute-start | bytes 540680 | tf_op jit(solution)/shard_map/ppermute | solution.py:508
  50.4 12.2 %all-to-all-done.1 = bf16[64,8,384]{2,1,0:T(8,128)(2,1)S(1)} async-done(((bf16[64,8,384]{2,1,0:T(8,128)(2,1)}), bf16[64,8,384]{2,1,0:T(8,128)(2,1)S(1)}, u32[]{:S(2)}, u32[]{:S(2)}) %all-to-all-start.1) | async-done | bytes 393248 | tf_op jit(solution)/shard_map/all_to_all | solution.py:528
  63.1 2.9 %collective-permute-start.3 = (bf16[128,384]{1,0:T(8,128)(2,1)S(1)}, bf16[128,384]{1,0:T(8,128)(2,1)S(1)}, u32[]{:S(2)}, u32[]{:S(2)}) collective-permute-start(bf16[128,384]{1,0:T(8,128)(2,1)S(1)} %get-tuple-element.46), channel_id=1, source_target_pairs={{0,1},{1,0},{2,3},{3,2},{4,5},{5,4},{6,7},{7,6},{8,9},{9,8},{10,11... | collective-permute-start | bytes 294920 | tf_op jit(solution)/shard_map/ppermute | solution.py:508
  66.1 1.7 %collective-permute-start.5 = (bf16[128,384]{1,0:T(8,128)(2,1)S(1)}, bf16[128,384]{1,0:T(8,128)(2,1)S(1)}, u32[]{:S(2)}, u32[]{:S(2)}) collective-permute-start(bf16[128,384]{1,0:T(8,128)(2,1)S(1)} %get-tuple-element.48), channel_id=1, source_target_pairs={{0,3},{1,2},{2,1},{3,0},{4,7},{5,6},{6,5},{7,4},{8,11},{9,10},{10,... | collective-permute-start | bytes 294920 | tf_op jit(solution)/shard_map/ppermute | solution.py:508
  67.7 2.9 %shard_map.132 = (bf16[2,1024,1024]{2,1,0:T(8,128)(2,1)S(1)}, bf16[256,1024]{1,0:T(8,128)(2,1)S(1)}, bf16[64,256]{1,0:T(8,128)(2,1)S(1)}, bf16[256,64]{1,0:T(8,1...) custom-call(s32[1]{0:T(128)} %bitcast.me_ref, ...), custom_call_target="tpu_custom_call" | custom-call | flops 1000000000 | bytes 4000000 | tf_op jit(solution)/shard_map/pallas_call | solution.py:577
  70.7 1.9 %collective-permute-done.5.refs_3_ = bf16[128,384]{1,0:T(8,128)(2,1)S(1)} collective-permute-done((bf16[128,384]{1,0:T(8,128)(2,1)S(1)}, bf16[128,384]{1,0:T(8,128)(2,1)S(1)}, u32[]{:S(2)}, u32[]{:S(2)}) %collective-permute-start.5) | collective-permute-done | bytes 98336 | tf_op jit(solution)/shard_map/ppermute | solution.py:508
  72.6 5.9 %shard_map.133 = (bf16[64,1024]{1,0:T(8,128)(2,1)S(1)}, bf16[64,1024]{1,0:T(8,128)(2,1)S(1)}, bf16[64,1024]{1,0:T(8,128)(2,1)S(1)}, bf16[64,1024]{1,0:T(8,128)(2,1)S(1)}) custom-call(s32[1]{0:T(128)} %bitcast.me_ref, bf16[128,384]{1,0:T(8,128)(2,1)S(1)} %get-tuple-element.45.refs_0_, bf16[128,384]{1,0:T(8,128)(2,1)S(1)} %collective-permute-done.3.refs_1_, ...), custom_call_target="tpu_custom_call" | custom-call | flops 4000000000 | bytes 4000000 | tf_op jit(solution)/shard_map/pallas_call | solution.py:611
  78.7 1.8 %collective-permute-start.11 = (bf16[64,1024]{1,0:T(8,128)(2,1)S(1)}, bf16[64,1024]{1,0:T(8,128)(2,1)S(1)}, u32[]{:S(2)}, u32[]{:S(2)}) collective-permute-start(bf16[64,1024]{1,0:T(8,128)(2,1)S(1)} %get-tuple-element.68), channel_id=1, source_target_pairs={{0,3},{1,2},{2,1},{3,0},{4,7},{5,6},{6,5},{7,4},{8,11},{9,10},{10,... | collective-permute-start | bytes 393224 | tf_op jit(solution)/shard_map/ppermute | solution.py:508
  80.5 3.0 %collective-permute-done.10.refs_2_ = bf16[64,1024]{1,0:T(8,128)(2,1)S(1)} collective-permute-done((bf16[64,1024]{1,0:T(8,128)(2,1)S(1)}, bf16[64,1024]{1,0:T(8,128)(2,1)S(1)}, u32[]{:S(2)}, u32[]{:S(2)}) %collective-permute-start.10) | collective-permute-done | bytes 131104 | tf_op jit(solution)/shard_map/ppermute | solution.py:508
  83.5 3.2 %collective-permute-done.11.refs_3_ = bf16[64,1024]{1,0:T(8,128)(2,1)S(1)} collective-permute-done((bf16[64,1024]{1,0:T(8,128)(2,1)S(1)}, bf16[64,1024]{1,0:T(8,128)(2,1)S(1)}, u32[]{:S(2)}, u32[]{:S(2)}) %collective-permute-start.11) | collective-permute-done | bytes 131104 | tf_op jit(solution)/shard_map/ppermute | solution.py:508
  87.1 21.0 %all_to_all.20 = bf16[64,8,384]{2,1,0:T(8,128)(2,1)S(1)} all-to-all(bf16[64,8,384]{2,1,0:T(8,128)(2,1)S(1)} %bitcast.21), channel_id=1, replica_groups=mesh['tile'=64,'chan'=4] {'tile'}, dimensions={0} | all-to-all | bytes 786432 | tf_op jit(solution)/shard_map/all_to_all | solution.py:528
  108.2 0.8 shard_map.135
  108.9 20.1 %all_to_all.21 = bf16[64,8,384]{2,1,0:T(8,128)(2,1)S(1)} all-to-all(bf16[64,8,384]{2,1,0:T(8,128)(2,1)S(1)} %bitcast.24), channel_id=1, replica_groups=mesh['tile'=64,'chan'=4] {'tile'}, dimensions={0} | all-to-all | bytes 786432 | tf_op jit(solution)/shard_map/all_to_all | solution.py:528
  129.1 1.2 shard_map.136
  (16 shorter events, 1.7 us)
Async XLA Ops:
  4.9 62.9 %copy-start = (bf16[8,16,4096]{2,1,0:T(8,128)(2,1)S(1)}, bf16[8,16,4096]{2,1,0:T(8,128)(2,1)}, u32[]{:S(2)}) copy-start(bf16[8,16,4096]{2,1,0:T(8,128)(2,1)} %param.10) | copy-start | bytes 3145732
  4.9 29.6 %all-to-all-start = ((bf16[64,8,384]{2,1,0:T(8,128)(2,1)}), bf16[64,8,384]{2,1,0:T(8,128)(2,1)S(1)}, u32[]{:S(2)}, u32[]{:S(2)}) async-start(bf16[64,8,384]{2,1,0:T(8,128)(2,1)} %bitcast.9), calls=%async_computation | async-start | bytes 786432 | tf_op jit(solution)/shard_map/all_to_all | solution.py:528
  20.1 2.8 %collective-permute-start = (bf16[16,4096]{1,0:T(8,128)(2,1)S(1)}, bf16[16,4096]{1,0:T(8,128)(2,1)S(1)}, u32[]{:S(2)}, u32[]{:S(2)}) collective-permute-start(bf16[16,4096]{1,0:T(8,128)(2,1)S(1)} %get-tuple-element.40), channel_id=1, source_target_pairs={{0,1},{1,0},{2,3},{3,2},{4,5},{5,4},{6,7},{7,6},{8,9},{9,8},{10,11... | collective-permute-start | bytes 393224 | tf_op jit(solution)/shard_map/ppermute | solution.py:508
  21.2 6.6 %collective-permute-start.1 = (bf16[16,4096]{1,0:T(8,128)(2,1)S(1)}, bf16[16,4096]{1,0:T(8,128)(2,1)S(1)}, u32[]{:S(2)}, u32[]{:S(2)}) collective-permute-start(bf16[16,4096]{1,0:T(8,128)(2,1)S(1)} %get-tuple-element.41), channel_id=1, source_target_pairs={{0,2},{1,3},{2,0},{3,1},{4,6},{5,7},{6,4},{7,5},{8,10},{9,11},{10,... | collective-permute-start | bytes 393224 | tf_op jit(solution)/shard_map/ppermute | solution.py:508
  21.6 11.5 %collective-permute-start.2 = (bf16[16,4096]{1,0:T(8,128)(2,1)S(1)}, bf16[16,4096]{1,0:T(8,128)(2,1)S(1)}, u32[]{:S(2)}, u32[]{:S(2)}) collective-permute-start(bf16[16,4096]{1,0:T(8,128)(2,1)S(1)} %get-tuple-element.42), channel_id=1, source_target_pairs={{0,3},{1,2},{2,1},{3,0},{4,7},{5,6},{6,5},{7,4},{8,11},{9,10},{10,... | collective-permute-start | bytes 393224 | tf_op jit(solution)/shard_map/ppermute | solution.py:508
  37.7 24.8 %all-to-all-start.1 = ((bf16[64,8,384]{2,1,0:T(8,128)(2,1)}), bf16[64,8,384]{2,1,0:T(8,128)(2,1)S(1)}, u32[]{:S(2)}, u32[]{:S(2)}) async-start(bf16[64,8,384]{2,1,0:T(8,128)(2,1)} %bitcast.11), calls=%async_computation.1 | async-start | bytes 786432 | tf_op jit(solution)/shard_map/all_to_all | solution.py:528
  47.9 18.2 %collective-permute-start.6 = (bf16[16,5632]{1,0:T(8,128)(2,1)S(1)}, bf16[16,5632]{1,0:T(8,128)(2,1)S(1)}, u32[]{:S(2)}, u32[]{:S(2)}) collective-permute-start(bf16[16,5632]{1,0:T(8,128)(2,1)S(1)} %get-tuple-element.53), channel_id=1, source_target_pairs={{0,1},{1,0},{2,3},{3,2},{4,5},{5,4},{6,7},{7,6},{8,9},{9,8},{10,11... | collective-permute-start | bytes 540680 | tf_op jit(solution)/shard_map/ppermute | solution.py:508
  48.6 19.1 %collective-permute-start.7 = (bf16[16,5632]{1,0:T(8,128)(2,1)S(1)}, bf16[16,5632]{1,0:T(8,128)(2,1)S(1)}, u32[]{:S(2)}, u32[]{:S(2)}) collective-permute-start(bf16[16,5632]{1,0:T(8,128)(2,1)S(1)} %get-tuple-element.54), channel_id=1, source_target_pairs={{0,2},{1,3},{2,0},{3,1},{4,6},{5,7},{6,4},{7,5},{8,10},{9,11},{10,... | collective-permute-start | bytes 540680 | tf_op jit(solution)/shard_map/ppermute | solution.py:508
  48.7 19.0 %collective-permute-start.8 = (bf16[16,5632]{1,0:T(8,128)(2,1)S(1)}, bf16[16,5632]{1,0:T(8,128)(2,1)S(1)}, u32[]{:S(2)}, u32[]{:S(2)}) collective-permute-start(bf16[16,5632]{1,0:T(8,128)(2,1)S(1)} %get-tuple-element.55), channel_id=1, source_target_pairs={{0,3},{1,2},{2,1},{3,0},{4,7},{5,6},{6,5},{7,4},{8,11},{9,10},{10,... | collective-permute-start | bytes 540680 | tf_op jit(solution)/shard_map/ppermute | solution.py:508
  63.1 7.6 %collective-permute-start.3 = (bf16[128,384]{1,0:T(8,128)(2,1)S(1)}, bf16[128,384]{1,0:T(8,128)(2,1)S(1)}, u32[]{:S(2)}, u32[]{:S(2)}) collective-permute-start(bf16[128,384]{1,0:T(8,128)(2,1)S(1)} %get-tuple-element.46), channel_id=1, source_target_pairs={{0,1},{1,0},{2,3},{3,2},{4,5},{5,4},{6,7},{7,6},{8,9},{9,8},{10,11... | collective-permute-start | bytes 294920 | tf_op jit(solution)/shard_map/ppermute | solution.py:508
  66.0 4.7 %collective-permute-start.4 = (bf16[128,384]{1,0:T(8,128)(2,1)S(1)}, bf16[128,384]{1,0:T(8,128)(2,1)S(1)}, u32[]{:S(2)}, u32[]{:S(2)}) collective-permute-start(bf16[128,384]{1,0:T(8,128)(2,1)S(1)} %get-tuple-element.47), channel_id=1, source_target_pairs={{0,2},{1,3},{2,0},{3,1},{4,6},{5,7},{6,4},{7,5},{8,10},{9,11},{10,... | collective-permute-start | bytes 294920 | tf_op jit(solution)/shard_map/ppermute | solution.py:508
  66.1 6.6 %collective-permute-start.5 = (bf16[128,384]{1,0:T(8,128)(2,1)S(1)}, bf16[128,384]{1,0:T(8,128)(2,1)S(1)}, u32[]{:S(2)}, u32[]{:S(2)}) collective-permute-start(bf16[128,384]{1,0:T(8,128)(2,1)S(1)} %get-tuple-element.48), channel_id=1, source_target_pairs={{0,3},{1,2},{2,1},{3,0},{4,7},{5,6},{6,5},{7,4},{8,11},{9,10},{10,... | collective-permute-start | bytes 294920 | tf_op jit(solution)/shard_map/ppermute | solution.py:508
  78.5 4.9 %collective-permute-start.10 = (bf16[64,1024]{1,0:T(8,128)(2,1)S(1)}, bf16[64,1024]{1,0:T(8,128)(2,1)S(1)}, u32[]{:S(2)}, u32[]{:S(2)}) collective-permute-start(bf16[64,1024]{1,0:T(8,128)(2,1)S(1)} %get-tuple-element.67), channel_id=1, source_target_pairs={{0,2},{1,3},{2,0},{3,1},{4,6},{5,7},{6,4},{7,5},{8,10},{9,11},{10,... | collective-permute-start | bytes 393224 | tf_op jit(solution)/shard_map/ppermute | solution.py:508
  78.7 8.0 %collective-permute-start.11 = (bf16[64,1024]{1,0:T(8,128)(2,1)S(1)}, bf16[64,1024]{1,0:T(8,128)(2,1)S(1)}, u32[]{:S(2)}, u32[]{:S(2)}) collective-permute-start(bf16[64,1024]{1,0:T(8,128)(2,1)S(1)} %get-tuple-element.68), channel_id=1, source_target_pairs={{0,3},{1,2},{2,1},{3,0},{4,7},{5,6},{6,5},{7,4},{8,11},{9,10},{10,... | collective-permute-start | bytes 393224 | tf_op jit(solution)/shard_map/ppermute | solution.py:508
  80.5 6.2 %collective-permute-start.9 = (bf16[64,1024]{1,0:T(8,128)(2,1)S(1)}, bf16[64,1024]{1,0:T(8,128)(2,1)S(1)}, u32[]{:S(2)}, u32[]{:S(2)}) collective-permute-start(bf16[64,1024]{1,0:T(8,128)(2,1)S(1)} %get-tuple-element.66), channel_id=1, source_target_pairs={{0,1},{1,0},{2,3},{3,2},{4,5},{5,4},{6,7},{7,6},{8,9},{9,8},{10,11... | collective-permute-start | bytes 393224 | tf_op jit(solution)/shard_map/ppermute | solution.py:508

commit v10 on v8

--- a/solution.py
+++ b/solution.py
@@ -80,7 +80,7 @@
 
 def send_body(
     me_ref,
-    feat_ref,
+    all_ref,
     cot_ref,
     el_ref,
     et_ref,
@@ -92,9 +92,20 @@
     down_ref,
     out_ref,
     raw_ref,
-    *peer_refs,
+    *more_refs,
 ):
+    peer_refs, (feat_ref, sems) = more_refs[0:6], more_refs[6:]
+    copy = pltpu.make_async_copy(all_ref, feat_ref, sems.at[0])
+    copy.start()
     pack_weights(conv_ref, bias_ref, down_ref, raw_ref)
+    cot = cot_ref[...]
+    stack = jnp.concatenate([cot[:, q * 256 : q * 256 + 256] for q in range(16)], axis=0)
+    row = down_col(512)
+    k, g, a, qr, hf = row >> 5, (row >> 3) & 3, (row >> 2) & 1, (row >> 1) & 1, row & 1
+    source = (qr << 8) | (g << 6) | (hf << 5) | (a << 4) | k
+    out_ref[:, 0:256] = mm(ones_where(lane_row(512) == source), stack).astype(BF)
+
+    copy.wait()
     for d in range(1, 4):
         peer = me_ref[0] ^ d
         first_ref, second_ref = peer_refs[d - 1], peer_refs[d + 2]
@@ -102,14 +113,6 @@
         second_ref[:, 0:4096] = feat_ref[pl.ds(pl.multiple_of(peer * 32 + 16, 16), 16), :]
         for q in range(4):
             second_ref[:, 4096 + q * 384 : 4480 + q * 384] = raw_ref[q * 16 : q * 16 + 16, :]
-
-    cot = cot_ref[...]
-    stack = jnp.concatenate([cot[:, q * 256 : q * 256 + 256] for q in range(16)], axis=0)
-    row = down_col(512)
-    k, g, a, qr, hf = row >> 5, (row >> 3) & 3, (row >> 2) & 1, (row >> 1) & 1, row & 1
-    source = (qr << 8) | (g << 6) | (hf << 5) | (a << 4) | k
-    out_ref[:, 0:256] = mm(ones_where(lane_row(512) == source), stack).astype(BF)
-
     first = feat_ref[:, 0:128]
     last = feat_ref[:, 3968:4096]
     p = down_col(64)
@@ -527,10 +530,11 @@
         send_body,
         (msg, jax.ShapeDtypeStruct((64, 384), BF)) + (first,) * 3 + (second,) * 3,
         (1,),
-        [scalar, whole((128, 4096)), whole((32, 4096))]
+        [scalar, pl.BlockSpec(memory_space=pl.ANY), whole((32, 4096))]
         + [whole((4, 8))] * 4
         + [whole((1, 8)), whole((16, 576)), whole((1, 16)), whole((64, 64))],
         (vmem,) * 8,
+        (pltpu.VMEM((128, 4096), BF), pltpu.SemaphoreType.DMA((1,))),
         flops=10**9,
         moved=2 * 10**6,
     )(

time: 132 us -> 132 us (level)
  no operation moved by 1% of the time
where the time goes in v10:
time: 132 us; the launch traced here: 130 us
  blocking collectives  41.1 us (31%)
  starting transfers between devices  37.3 us (28%)
  waiting for transfers between devices  31.9 us (24%)
  Pallas kernels  19.2 us (15%)
    all_to_all x2, blocking collectives, to_nodes(): lax.all_to_all(x.reshape(64, 8, 384), 'tile', 0, 0, tiled=True).reshape(MSG)  41.1 us
    all_to_all x2, starting transfers between devices, to_nodes(): lax.all_to_all(x.reshape(64, 8, 384), 'tile', 0, 0, tiled=True).reshape(MSG)  25.4 us
    ppermute x12, waiting for transfers between devices, to_peers(): lax.ppermute(parts[d], 'chan', [(i, i ^ d) for i in range(4)])  18.3 us
    all_to_all x2, waiting for transfers between devices, to_nodes(): lax.all_to_all(x.reshape(64, 8, 384), 'tile', 0, 0, tiled=True).reshape(MSG)  13.6 us
    ppermute x12, starting transfers between devices, to_peers(): lax.ppermute(parts[d], 'chan', [(i, i ^ d) for i in range(4)])  11.9 us
    pallas_call x1, Pallas kernels, on_device(): pl.pallas_call(level_body, out_shape=(jax.ShapeDtypeStruct((64, 1024), BF...  5.88 us
    pallas_call x1, Pallas kernels, on_device(): call(send_body, (msg, jax.ShapeDtypeStruct((64, 384), BF)) + (first,) * 3...  4.2 us
    pallas_call x1, Pallas kernels, on_device(): call(pick_body, (msg, jax.ShapeDtypeStruct((8, 512), F32)), (1,), [vmem],...  3.23 us
  transfers between devices with their start and end apart: 14, of which 7 were waited for; matrix products, arithmetic and copies ran while one was open for 0% of the time, Pallas kernels for 3%

profile of v10, /device:TPU:1, one launch (start us, length us, event | category | flops | bytes accessed | tf_op | source)
XLA Modules:
  0.0 130.2 jit_solution(15532567617568408158)
XLA Ops:
  0.6 4.2 %shard_map.129 = (bf16[512,384]{1,0:T(8,128)(2,1)}, bf16[64,384]{1,0:T(8,128)(2,1)S(1)}, bf16[16,4096]{1,0:T(8,128)(2,1)S(1)}, bf16[16,4096]{1,0:T(8,128)(2,1)S(...) custom-call(s32[1]{0:T(128)} %bitcast.me_ref, ...), custom_call_target="tpu_custom_call" | custom-call | flops 1000000000 | bytes 2000000 | tf_op jit(solution)/shard_map/pallas_call | solution.py:529
  4.9 15.3 %all-to-all-start = ((bf16[64,8,384]{2,1,0:T(8,128)(2,1)}), bf16[64,8,384]{2,1,0:T(8,128)(2,1)S(1)}, u32[]{:S(2)}, u32[]{:S(2)}) async-start(bf16[64,8,384]{2,1,0:T(8,128)(2,1)} %bitcast.9), calls=%async_computation | async-start | bytes 786432 | tf_op jit(solution)/shard_map/all_to_all | solution.py:523
  20.1 1.0 collective-permute-start
  21.6 1.3 %collective-permute-start.2 = (bf16[16,4096]{1,0:T(8,128)(2,1)S(1)}, bf16[16,4096]{1,0:T(8,128)(2,1)S(1)}, u32[]{:S(2)}, u32[]{:S(2)}) collective-permute-start(bf16[16,4096]{1,0:T(8,128)(2,1)S(1)} %get-tuple-element.42), channel_id=1, source_target_pairs={{0,3},{1,2},{2,1},{3,0},{4,7},{5,6},{6,5},{7,4},{8,11},{9,10},{10,... | collective-permute-start | bytes 393224 | tf_op jit(solution)/shard_map/ppermute | solution.py:503
  22.9 4.8 %collective-permute-done.1.refs_3_ = bf16[16,4096]{1,0:T(8,128)(2,1)S(1)} collective-permute-done((bf16[16,4096]{1,0:T(8,128)(2,1)S(1)}, bf16[16,4096]{1,0:T(8,128)(2,1)S(1)}, u32[]{:S(2)}, u32[]{:S(2)}) %collective-permute-start.1) | collective-permute-done | bytes 131104 | tf_op jit(solution)/shard_map/ppermute | solution.py:503
  27.7 5.3 %collective-permute-done.2.refs_4_ = bf16[16,4096]{1,0:T(8,128)(2,1)S(1)} collective-permute-done((bf16[16,4096]{1,0:T(8,128)(2,1)S(1)}, bf16[16,4096]{1,0:T(8,128)(2,1)S(1)}, u32[]{:S(2)}, u32[]{:S(2)}) %collective-permute-start.2) | collective-permute-done | bytes 131104 | tf_op jit(solution)/shard_map/ppermute | solution.py:503
  33.1 1.4 %all-to-all-done = bf16[64,8,384]{2,1,0:T(8,128)(2,1)S(1)} async-done(((bf16[64,8,384]{2,1,0:T(8,128)(2,1)}), bf16[64,8,384]{2,1,0:T(8,128)(2,1)S(1)}, u32[]{:S(2)}, u32[]{:S(2)}) %all-to-all-start) | async-done | bytes 393248 | tf_op jit(solution)/shard_map/all_to_all | solution.py:523
  34.5 3.2 %shard_map.130 = (bf16[512,384]{1,0:T(8,128)(2,1)}, f32[8,512]{1,0:T(8,128)S(1)}) custom-call(bf16[512,384]{1,0:T(8,128)(2,1)S(1)} %bitcast.19), custom_call_target="tpu_custom_call" | custom-call | flops 1000000000 | bytes 1000000 | tf_op jit(solution)/shard_map/pallas_call | solution.py:561
  37.7 10.2 %all-to-all-start.1 = ((bf16[64,8,384]{2,1,0:T(8,128)(2,1)}), bf16[64,8,384]{2,1,0:T(8,128)(2,1)S(1)}, u32[]{:S(2)}, u32[]{:S(2)}) async-start(bf16[64,8,384]{2,1,0:T(8,128)(2,1)} %bitcast.11), calls=%async_computation.1 | async-start | bytes 786432 | tf_op jit(solution)/shard_map/all_to_all | solution.py:523
  47.9 0.8 collective-permute-start.6
  48.7 1.7 %collective-permute-start.8 = (bf16[16,5632]{1,0:T(8,128)(2,1)S(1)}, bf16[16,5632]{1,0:T(8,128)(2,1)S(1)}, u32[]{:S(2)}, u32[]{:S(2)}) collective-permute-start(bf16[16,5632]{1,0:T(8,128)(2,1)S(1)} %get-tuple-element.55), channel_id=1, source_target_pairs={{0,3},{1,2},{2,1},{3,0},{4,7},{5,6},{6,5},{7,4},{8,11},{9,10},{10,... | collective-permute-start | bytes 540680 | tf_op jit(solution)/shard_map/ppermute | solution.py:503
  50.4 12.2 %all-to-all-done.1 = bf16[64,8,384]{2,1,0:T(8,128)(2,1)S(1)} async-done(((bf16[64,8,384]{2,1,0:T(8,128)(2,1)}), bf16[64,8,384]{2,1,0:T(8,128)(2,1)S(1)}, u32[]{:S(2)}, u32[]{:S(2)}) %all-to-all-start.1) | async-done | bytes 393248 | tf_op jit(solution)/shard_map/all_to_all | solution.py:523
  63.1 2.9 %collective-permute-start.3 = (bf16[128,384]{1,0:T(8,128)(2,1)S(1)}, bf16[128,384]{1,0:T(8,128)(2,1)S(1)}, u32[]{:S(2)}, u32[]{:S(2)}) collective-permute-start(bf16[128,384]{1,0:T(8,128)(2,1)S(1)} %get-tuple-element.46), channel_id=1, source_target_pairs={{0,1},{1,0},{2,3},{3,2},{4,5},{5,4},{6,7},{7,6},{8,9},{9,8},{10,11... | collective-permute-start | bytes 294920 | tf_op jit(solution)/shard_map/ppermute | solution.py:503
  66.1 1.7 %collective-permute-start.5 = (bf16[128,384]{1,0:T(8,128)(2,1)S(1)}, bf16[128,384]{1,0:T(8,128)(2,1)S(1)}, u32[]{:S(2)}, u32[]{:S(2)}) collective-permute-start(bf16[128,384]{1,0:T(8,128)(2,1)S(1)} %get-tuple-element.48), channel_id=1, source_target_pairs={{0,3},{1,2},{2,1},{3,0},{4,7},{5,6},{6,5},{7,4},{8,11},{9,10},{10,... | collective-permute-start | bytes 294920 | tf_op jit(solution)/shard_map/ppermute | solution.py:503
  67.7 2.9 %shard_map.132 = (bf16[2,1024,1024]{2,1,0:T(8,128)(2,1)S(1)}, bf16[256,1024]{1,0:T(8,128)(2,1)S(1)}, bf16[64,256]{1,0:T(8,128)(2,1)S(1)}, bf16[256,64]{1,0:T(8,1...) custom-call(s32[1]{0:T(128)} %bitcast.me_ref, ...), custom_call_target="tpu_custom_call" | custom-call | flops 1000000000 | bytes 4000000 | tf_op jit(solution)/shard_map/pallas_call | solution.py:572
  70.7 1.9 %collective-permute-done.5.refs_3_ = bf16[128,384]{1,0:T(8,128)(2,1)S(1)} collective-permute-done((bf16[128,384]{1,0:T(8,128)(2,1)S(1)}, bf16[128,384]{1,0:T(8,128)(2,1)S(1)}, u32[]{:S(2)}, u32[]{:S(2)}) %collective-permute-start.5) | collective-permute-done | bytes 98336 | tf_op jit(solution)/shard_map/ppermute | solution.py:503
  72.6 5.9 %shard_map.133 = (bf16[64,1024]{1,0:T(8,128)(2,1)S(1)}, bf16[64,1024]{1,0:T(8,128)(2,1)S(1)}, bf16[64,1024]{1,0:T(8,128)(2,1)S(1)}, bf16[64,1024]{1,0:T(8,128)(2,1)S(1)}) custom-call(s32[1]{0:T(128)} %bitcast.me_ref, bf16[128,384]{1,0:T(8,128)(2,1)S(1)} %get-tuple-element.45.refs_0_, bf16[128,384]{1,0:T(8,128)(2,1)S(1)} %collective-permute-done.3.refs_1_, ...), custom_call_target="tpu_custom_call" | custom-call | flops 4000000000 | bytes 4000000 | tf_op jit(solution)/shard_map/pallas_call | solution.py:606
  78.6 1.8 %collective-permute-start.11 = (bf16[64,1024]{1,0:T(8,128)(2,1)S(1)}, bf16[64,1024]{1,0:T(8,128)(2,1)S(1)}, u32[]{:S(2)}, u32[]{:S(2)}) collective-permute-start(bf16[64,1024]{1,0:T(8,128)(2,1)S(1)} %get-tuple-element.68), channel_id=1, source_target_pairs={{0,3},{1,2},{2,1},{3,0},{4,7},{5,6},{6,5},{7,4},{8,11},{9,10},{10,... | collective-permute-start | bytes 393224 | tf_op jit(solution)/shard_map/ppermute | solution.py:503
  80.5 3.0 %collective-permute-done.10.refs_2_ = bf16[64,1024]{1,0:T(8,128)(2,1)S(1)} collective-permute-done((bf16[64,1024]{1,0:T(8,128)(2,1)S(1)}, bf16[64,1024]{1,0:T(8,128)(2,1)S(1)}, u32[]{:S(2)}, u32[]{:S(2)}) %collective-permute-start.10) | collective-permute-done | bytes 131104 | tf_op jit(solution)/shard_map/ppermute | solution.py:503
  83.4 3.2 %collective-permute-done.11.refs_3_ = bf16[64,1024]{1,0:T(8,128)(2,1)S(1)} collective-permute-done((bf16[64,1024]{1,0:T(8,128)(2,1)S(1)}, bf16[64,1024]{1,0:T(8,128)(2,1)S(1)}, u32[]{:S(2)}, u32[]{:S(2)}) %collective-permute-start.11) | collective-permute-done | bytes 131104 | tf_op jit(solution)/shard_map/ppermute | solution.py:503
  87.1 21.0 %all_to_all.20 = bf16[64,8,384]{2,1,0:T(8,128)(2,1)S(1)} all-to-all(bf16[64,8,384]{2,1,0:T(8,128)(2,1)S(1)} %bitcast.21), channel_id=1, replica_groups=mesh['tile'=64,'chan'=4] {'tile'}, dimensions={0} | all-to-all | bytes 786432 | tf_op jit(solution)/shard_map/all_to_all | solution.py:523
  108.1 0.8 shard_map.135
  108.9 20.1 %all_to_all.21 = bf16[64,8,384]{2,1,0:T(8,128)(2,1)S(1)} all-to-all(bf16[64,8,384]{2,1,0:T(8,128)(2,1)S(1)} %bitcast.24), channel_id=1, replica_groups=mesh['tile'=64,'chan'=4] {'tile'}, dimensions={0} | all-to-all | bytes 786432 | tf_op jit(solution)/shard_map/all_to_all | solution.py:523
  129.0 1.2 shard_map.136
  (16 shorter events, 1.7 us)
Async XLA Ops:
  4.8 62.9 %copy-start = (bf16[8,16,4096]{2,1,0:T(8,128)(2,1)S(1)}, bf16[8,16,4096]{2,1,0:T(8,128)(2,1)}, u32[]{:S(2)}) copy-start(bf16[8,16,4096]{2,1,0:T(8,128)(2,1)} %param.10) | copy-start | bytes 3145732
  4.9 29.6 %all-to-all-start = ((bf16[64,8,384]{2,1,0:T(8,128)(2,1)}), bf16[64,8,384]{2,1,0:T(8,128)(2,1)S(1)}, u32[]{:S(2)}, u32[]{:S(2)}) async-start(bf16[64,8,384]{2,1,0:T(8,128)(2,1)} %bitcast.9), calls=%async_computation | async-start | bytes 786432 | tf_op jit(solution)/shard_map/all_to_all | solution.py:523
  20.1 2.8 %collective-permute-start = (bf16[16,4096]{1,0:T(8,128)(2,1)S(1)}, bf16[16,4096]{1,0:T(8,128)(2,1)S(1)}, u32[]{:S(2)}, u32[]{:S(2)}) collective-permute-start(bf16[16,4096]{1,0:T(8,128)(2,1)S(1)} %get-tuple-element.40), channel_id=1, source_target_pairs={{0,1},{1,0},{2,3},{3,2},{4,5},{5,4},{6,7},{7,6},{8,9},{9,8},{10,11... | collective-permute-start | bytes 393224 | tf_op jit(solution)/shard_map/ppermute | solution.py:503
  21.2 6.5 %collective-permute-start.1 = (bf16[16,4096]{1,0:T(8,128)(2,1)S(1)}, bf16[16,4096]{1,0:T(8,128)(2,1)S(1)}, u32[]{:S(2)}, u32[]{:S(2)}) collective-permute-start(bf16[16,4096]{1,0:T(8,128)(2,1)S(1)} %get-tuple-element.41), channel_id=1, source_target_pairs={{0,2},{1,3},{2,0},{3,1},{4,6},{5,7},{6,4},{7,5},{8,10},{9,11},{10,... | collective-permute-start | bytes 393224 | tf_op jit(solution)/shard_map/ppermute | solution.py:503
  21.6 11.5 %collective-permute-start.2 = (bf16[16,4096]{1,0:T(8,128)(2,1)S(1)}, bf16[16,4096]{1,0:T(8,128)(2,1)S(1)}, u32[]{:S(2)}, u32[]{:S(2)}) collective-permute-start(bf16[16,4096]{1,0:T(8,128)(2,1)S(1)} %get-tuple-element.42), channel_id=1, source_target_pairs={{0,3},{1,2},{2,1},{3,0},{4,7},{5,6},{6,5},{7,4},{8,11},{9,10},{10,... | collective-permute-start | bytes 393224 | tf_op jit(solution)/shard_map/ppermute | solution.py:503
  37.7 24.8 %all-to-all-start.1 = ((bf16[64,8,384]{2,1,0:T(8,128)(2,1)}), bf16[64,8,384]{2,1,0:T(8,128)(2,1)S(1)}, u32[]{:S(2)}, u32[]{:S(2)}) async-start(bf16[64,8,384]{2,1,0:T(8,128)(2,1)} %bitcast.11), calls=%async_computation.1 | async-start | bytes 786432 | tf_op jit(solution)/shard_map/all_to_all | solution.py:523
  47.9 18.2 %collective-permute-start.6 = (bf16[16,5632]{1,0:T(8,128)(2,1)S(1)}, bf16[16,5632]{1,0:T(8,128)(2,1)S(1)}, u32[]{:S(2)}, u32[]{:S(2)}) collective-permute-start(bf16[16,5632]{1,0:T(8,128)(2,1)S(1)} %get-tuple-element.53), channel_id=1, source_target_pairs={{0,1},{1,0},{2,3},{3,2},{4,5},{5,4},{6,7},{7,6},{8,9},{9,8},{10,11... | collective-permute-start | bytes 540680 | tf_op jit(solution)/shard_map/ppermute | solution.py:503
  48.6 19.1 %collective-permute-start.7 = (bf16[16,5632]{1,0:T(8,128)(2,1)S(1)}, bf16[16,5632]{1,0:T(8,128)(2,1)S(1)}, u32[]{:S(2)}, u32[]{:S(2)}) collective-permute-start(bf16[16,5632]{1,0:T(8,128)(2,1)S(1)} %get-tuple-element.54), channel_id=1, source_target_pairs={{0,2},{1,3},{2,0},{3,1},{4,6},{5,7},{6,4},{7,5},{8,10},{9,11},{10,... | collective-permute-start | bytes 540680 | tf_op jit(solution)/shard_map/ppermute | solution.py:503
  48.7 19.0 %collective-permute-start.8 = (bf16[16,5632]{1,0:T(8,128)(2,1)S(1)}, bf16[16,5632]{1,0:T(8,128)(2,1)S(1)}, u32[]{:S(2)}, u32[]{:S(2)}) collective-permute-start(bf16[16,5632]{1,0:T(8,128)(2,1)S(1)} %get-tuple-element.55), channel_id=1, source_target_pairs={{0,3},{1,2},{2,1},{3,0},{4,7},{5,6},{6,5},{7,4},{8,11},{9,10},{10,... | collective-permute-start | bytes 540680 | tf_op jit(solution)/shard_map/ppermute | solution.py:503
  63.1 7.6 %collective-permute-start.3 = (bf16[128,384]{1,0:T(8,128)(2,1)S(1)}, bf16[128,384]{1,0:T(8,128)(2,1)S(1)}, u32[]{:S(2)}, u32[]{:S(2)}) collective-permute-start(bf16[128,384]{1,0:T(8,128)(2,1)S(1)} %get-tuple-element.46), channel_id=1, source_target_pairs={{0,1},{1,0},{2,3},{3,2},{4,5},{5,4},{6,7},{7,6},{8,9},{9,8},{10,11... | collective-permute-start | bytes 294920 | tf_op jit(solution)/shard_map/ppermute | solution.py:503
  66.0 4.7 %collective-permute-start.4 = (bf16[128,384]{1,0:T(8,128)(2,1)S(1)}, bf16[128,384]{1,0:T(8,128)(2,1)S(1)}, u32[]{:S(2)}, u32[]{:S(2)}) collective-permute-start(bf16[128,384]{1,0:T(8,128)(2,1)S(1)} %get-tuple-element.47), channel_id=1, source_target_pairs={{0,2},{1,3},{2,0},{3,1},{4,6},{5,7},{6,4},{7,5},{8,10},{9,11},{10,... | collective-permute-start | bytes 294920 | tf_op jit(solution)/shard_map/ppermute | solution.py:503
  66.1 6.6 %collective-permute-start.5 = (bf16[128,384]{1,0:T(8,128)(2,1)S(1)}, bf16[128,384]{1,0:T(8,128)(2,1)S(1)}, u32[]{:S(2)}, u32[]{:S(2)}) collective-permute-start(bf16[128,384]{1,0:T(8,128)(2,1)S(1)} %get-tuple-element.48), channel_id=1, source_target_pairs={{0,3},{1,2},{2,1},{3,0},{4,7},{5,6},{6,5},{7,4},{8,11},{9,10},{10,... | collective-permute-start | bytes 294920 | tf_op jit(solution)/shard_map/ppermute | solution.py:503
  78.5 4.9 %collective-permute-start.10 = (bf16[64,1024]{1,0:T(8,128)(2,1)S(1)}, bf16[64,1024]{1,0:T(8,128)(2,1)S(1)}, u32[]{:S(2)}, u32[]{:S(2)}) collective-permute-start(bf16[64,1024]{1,0:T(8,128)(2,1)S(1)} %get-tuple-element.67), channel_id=1, source_target_pairs={{0,2},{1,3},{2,0},{3,1},{4,6},{5,7},{6,4},{7,5},{8,10},{9,11},{10,... | collective-permute-start | bytes 393224 | tf_op jit(solution)/shard_map/ppermute | solution.py:503
  78.6 8.0 %collective-permute-start.11 = (bf16[64,1024]{1,0:T(8,128)(2,1)S(1)}, bf16[64,1024]{1,0:T(8,128)(2,1)S(1)}, u32[]{:S(2)}, u32[]{:S(2)}) collective-permute-start(bf16[64,1024]{1,0:T(8,128)(2,1)S(1)} %get-tuple-element.68), channel_id=1, source_target_pairs={{0,3},{1,2},{2,1},{3,0},{4,7},{5,6},{6,5},{7,4},{8,11},{9,10},{10,... | collective-permute-start | bytes 393224 | tf_op jit(solution)/shard_map/ppermute | solution.py:503
  80.5 6.2 %collective-permute-start.9 = (bf16[64,1024]{1,0:T(8,128)(2,1)S(1)}, bf16[64,1024]{1,0:T(8,128)(2,1)S(1)}, u32[]{:S(2)}, u32[]{:S(2)}) collective-permute-start(bf16[64,1024]{1,0:T(8,128)(2,1)S(1)} %get-tuple-element.66), channel_id=1, source_target_pairs={{0,1},{1,0},{2,3},{3,2},{4,5},{5,4},{6,7},{7,6},{8,9},{9,8},{10,11... | collective-permute-start | bytes 393224 | tf_op jit(solution)/shard_map/ppermute | solution.py:503
